TPU v7x, 128 devices: a whole 4x4x4 slice. The times are simulated.
128 devices in a mesh: dp: 4 (over x), region: 32 (over y, z, core).
Axes of the slice: x: 4, y: 4, z: 4, core: 2. Of those that a mesh axis runs over, the one named last changes fastest.
Arguments:
- feats: bfloat16 [4, 32768, 256], P('dp', 'region'), may hold values from -6 to 6
- grad_out: bfloat16 [4, 32768, 256], P('dp', 'region'), may hold values from -6 to 6
- weight: bfloat16 [27, 256, 256], replicated, may hold values from -0.078125 to 0.078125
- loc_in: int32 [4, 32, 26, 256], P('dp', 'region'), may hold values from 0 to 1024, as said below
- loc_out: int32 [4, 32, 26, 256], P('dp', 'region'), may hold values from 0 to 1024, as said below
- bnd_out: int32 [4, 32, 2, 9, 128], P('dp', 'region'), may hold values from 0 to 1024, as said below
- bnd_in: int32 [4, 32, 2, 9, 128], P('dp', 'region'), may hold values from 0 to 1024, as said below
Outputs:
- grad_input: bfloat16 [4, 32768, 256], P('dp', 'region')
- grad_weight: float32 [27, 256, 256], replicated
Inputs may be any that keep to these rules, and one draw needn't show every extreme that they name: `loc_in`: 1024 marks an empty slot; within one offset list of a block the live slots name distinct rows; a slot is empty in loc_in exactly where it is empty in loc_out. `loc_out`: 1024 marks an empty slot; within one offset list of a block the live slots name distinct rows. bnd_out[n, r, 1] is slot-aligned with bnd_in[n, r+1, 0], and bnd_out[n, r, 0] with bnd_in[n, r-1, 1] (n the scan, r the block): slot (f, b) of both names one pair, and it is empty (1024) in both together. Side 0 of the first block and side 1 of the last block are empty. Within one face list the live rows are distinct. `bnd_in`: aligned with bnd_out as stated there; within one face list the live rows are distinct.
All inputs are finite; a program needn't handle non-finite values.
Results may differ from a plain program's by a relative error of at most 0.0028.
Values may be sent and summed in bfloat16 or wider, within the bound.
A program may use at most 128 MiB of HBM per device.

v0:
```python
import math

import jax
import jax.numpy as jnp
from jax import lax
from jax.sharding import PartitionSpec as P


def passed_along(array, axis, by):
    peers = lax.axis_size(axis)
    pairs = [(i, i + by) for i in range(peers) if 0 <= i + by < peers]
    return lax.ppermute(array, axis, pairs)


def contract_rows(left, right):
    return lax.dot_general(
        left, right, (((0,), (0,)), ((), ())), preferred_element_type=jnp.float32
    )


def through_kernel(grads, kernel):
    return lax.dot_general(
        grads, kernel, (((1,), (1,)), ((), ())), preferred_element_type=jnp.float32
    )


def one_hot_rows(lists, rows_here):
    numbers = lax.broadcasted_iota(jnp.int32, lists.shape + (rows_here,), lists.ndim)
    return (lists[..., None] == numbers).astype(jnp.bfloat16)


def pick_rows(table, source):
    return jnp.einsum("...v,vc->...c", table, source, preferred_element_type=jnp.float32).astype(
        jnp.bfloat16
    )


def place_rows(table, rows):
    return jnp.einsum("fbv,fbc->vc", table, rows, preferred_element_type=jnp.float32)


def face_products(features, grads, kernels):
    weight_grad = jnp.einsum("fbc,fbd->fcd", features, grads, preferred_element_type=jnp.float32)
    out_rows = jnp.einsum(
        "fbd,fcd->fbc", grads, kernels, preferred_element_type=jnp.float32
    ).astype(jnp.bfloat16)
    return (weight_grad, out_rows)


def per_device(feats, grad_out, weight, loc_in, loc_out, bnd_out, bnd_in):
    rows_here = feats.shape[1]
    pairs = loc_in.shape[3]
    own_feat = feats[0]
    own_grad = grad_out[0]
    center = contract_rows(own_feat, own_grad)
    accumulated = through_kernel(own_grad, weight[13])
    table_in = one_hot_rows(loc_in[0, 0], rows_here)
    table_out = one_hot_rows(loc_out[0, 0], rows_here)
    gathered_x = pick_rows(table_in, own_feat)
    gathered_g = pick_rows(table_out, own_grad)
    placed = jnp.einsum(
        "kpv,kpc->vkc", table_in, gathered_g, preferred_element_type=jnp.float32
    ).astype(jnp.bfloat16)
    side_kernels = jnp.concatenate([weight[0:13], weight[14:27]], 0)
    accumulated = accumulated + jnp.einsum(
        "vkd,kcd->vc", placed, side_kernels, preferred_element_type=jnp.float32
    )
    offset_grads = jnp.einsum(
        "kpc,kpd->kcd", gathered_x, gathered_g, preferred_element_type=jnp.float32
    )
    low_kernels = weight[0:9]
    high_kernels = weight[18:27]
    face_out_table = one_hot_rows(bnd_out[0, 0], rows_here)
    face_in_table = one_hot_rows(bnd_in[0, 0], rows_here)
    own_grads = pick_rows(face_out_table, own_grad)
    asked = pick_rows(face_in_table, own_feat)
    fetched = [None, None]
    for face_side in range(2):
        fetched[1 - face_side] = passed_along(asked[face_side], "region", 2 * face_side - 1)
    low_grad, low_rows = face_products(fetched[0], own_grads[0], low_kernels)
    high_grad, high_rows = face_products(fetched[1], own_grads[1], high_kernels)
    outgoing = [low_rows, high_rows]
    for face_side in range(2):
        arrived = passed_along(outgoing[face_side], "region", 2 * face_side - 1)
        accumulated = accumulated + place_rows(face_in_table[1 - face_side], arrived)
    stacked = jnp.concatenate(
        [
            offset_grads[0:9] + low_grad,
            offset_grads[9:13],
            center[None],
            offset_grads[13:17],
            offset_grads[17:26] + high_grad,
        ],
        0,
    )
    loss_scale = 1.0 / math.sqrt(pairs * lax.axis_size("dp") * lax.axis_size("region"))
    summed = lax.psum(stacked, ("dp", "region"))
    grad_weight = summed * loss_scale
    grad_input = accumulated.astype(jnp.bfloat16)[None]
    return (grad_input, grad_weight)


def solution(mesh):
    placed = (
        P("dp", "region", None),
        P("dp", "region", None),
        P(),
        P("dp", "region", None, None),
        P("dp", "region", None, None),
        P("dp", "region", None, None, None),
        P("dp", "region", None, None, None),
    )
    return jax.shard_map(
        per_device,
        mesh=mesh,
        in_specs=placed,
        out_specs=(P("dp", "region", None), P()),
        check_vma=False,
    )
```

profile of v0, /device:TPU:1, one launch (start us, length us, event | category | flops | bytes accessed | tf_op | source)
XLA Modules:
  0.0 240.7 jit_solution(6951616289086005550)
XLA Ops:
  7.2 0.0 copy-start
  7.2 0.0 all-reduce.2.cloned.1.call-start
  7.2 0.8 copy.10
  8.0 0.3 copy-done
  8.2 0.0 copy-start.2
  8.2 2.0 fusion.21
  10.2 0.0 copy-done.2
  10.2 0.0 copy-start.6
  10.3 0.0 copy-start.7
  10.3 1.4 convolution_convert_fusion.2
  11.6 3.3 %collective-permute-start = (bf16[9,128,256]{2,1,0:T(8,128)(2,1)}, bf16[9,128,256]{2,1,0:T(8,128)(2,1)}, u32[]{:S(2)}, u32[]{:S(2)}) collective-permute-start(bf16[9,128,256]{2,1,0:T(8,128)(2,1)} %convolution_convert_fusion.2), channel_id=1, source_target_pairs={{1,0},{2,1},{3,2},{4,3},{5,4},{6,5},{7,6},{8,7},{9,8},{10,9},{11,1... | collective-permute-start | bytes 1769480 | tf_op jit(solution)/shard_map/ppermute | solution.py:12
  14.9 1.4 convolution_convert_fusion.1
  16.3 3.6 %collective-permute-start.1 = (bf16[9,128,256]{2,1,0:T(8,128)(2,1)}, bf16[9,128,256]{2,1,0:T(8,128)(2,1)}, u32[]{:S(2)}, u32[]{:S(2)}) collective-permute-start(bf16[9,128,256]{2,1,0:T(8,128)(2,1)} %convolution_convert_fusion.1), channel_id=1, source_target_pairs={{0,1},{1,2},{2,3},{3,4},{4,5},{5,6},{6,7},{7,8},{8,9},{9,10},{10,1... | collective-permute-start | bytes 1769480 | tf_op jit(solution)/shard_map/ppermute | solution.py:12
  19.8 0.0 copy-done.6
  19.9 0.0 copy-done.7
  19.9 0.0 copy-start.4
  19.9 0.0 copy-start.5
  19.9 2.6 %convolution_convert_fusion = bf16[2,9,128,256]{3,2,1,0:T(8,128)(2,1)S(1)} fusion(bf16[1,1024,256]{2,1,0:T(8,128)(2,1)S(1)} %copy-done.7, s32[2,9,128]{2,1,0:T(8,128)S(1)} %copy.9), kind=kOutput, calls=%fused_computation.30 | convolution fusion | flops 1210908672 | bytes 1713152 | tf_op jit(solution)/shard_map/...v,vc->...c/dot_general | solution.py:33
  22.5 1.1 slice_bitcast_fusion.16
  23.6 1.9 collective-permute-start.3
  25.5 3.8 %collective-permute-start.2 = (bf16[9,128,256]{2,1,0:T(8,128)(2,1)}, bf16[9,128,256]{2,1,0:T(8,128)(2,1)}, u32[]{:S(2)}, u32[]{:S(2)}) collective-permute-start(bf16[9,128,256]{2,1,0:T(8,128)(2,1)} %get-tuple-element.5), channel_id=1, source_target_pairs={{0,1},{1,2},{2,3},{3,4},{4,5},{5,6},{6,7},{7,8},{8,9},{9,10},{10,1... | collective-permute-start | bytes 1769480 | tf_op jit(solution)/shard_map/ppermute | solution.py:12
  29.4 0.0 copy-done.4
  29.4 0.0 copy-done.5
  29.4 6.6 %fusion.18 = bf16[26,256,256]{2,1,0:T(8,128)(2,1)} fusion(s32[26,256]{1,0:T(8,128)S(1)} %bitcast.105, bf16[1,1024,256]{2,1,0:T(8,128)(2,1)S(1)} %copy-done), kind=kOutput, calls=%fused_computation.25 | convolution fusion | flops 3498180608 | bytes 3958784 | tf_op jit(solution)/shard_map/...v,vc->...c/dot_general | solution.py:33
  36.1 10.2 %fusion.16 = f32[26,256,256]{2,1,0:T(8,128)} fusion(bf16[26,256,256]{2,1,0:T(8,128)(2,1)} %fusion.18, s32[26,256]{1,0:T(8,128)S(1)} %bitcast.103, bf16[1,1024,256]{2,1,0:T(8,128)(2,1)S(1)} %copy-done.7), kind=kOutput, calls=%fused_computation.23 | convolution fusion | flops 4370595840 | bytes 10774528 | tf_op jit(solution)/shard_map/kpc,kpd->kcd/dot_general | solution.py:68
  46.2 2.3 fusion.48
  48.5 3.6 %fusion.53 = (bf16[13,256,256]{2,1,0:T(8,128)(2,1)S(1)}, bf16[13,256,256]{2,1,0:T(8,128)(2,1)}) fusion(bf16[27,256,256]{2,1,0:T(8,128)(2,1)} %param.9), kind=kLoop, calls=%fused_computation.65 | loop fusion | bytes 6815744 | tf_op jit(solution)/shard_map/slice | solution.py:64
  52.1 0.0 collective-permute-done.2
  52.1 1.0 copy-done.1
  53.1 3.0 %fusion.20 = f32[27,256,256]{2,1,0:T(8,128)} fusion(f32[26,256,256]{2,1,0:T(8,128)S(1)} %copy-done.1, bf16[9,128,256]{2,1,0:T(8,128)(2,1)} %collective-permute-done.2, bf16[2,9,128,256]{3,2,1,0:T(8,128)(2,1)S(1)} %fusion.21), kind=kOutput, calls=%fused_computation.29 | convolution fusion | flops 151584768 | bytes 5898240 | tf_op jit(solution)/shard_map/fbc,fbd->fcd/dot_general | solution.py:43
  56.1 1.0 slice_dynamic-update-slice_fusion.1
  57.1 0.0 copy-done.8
  57.1 1.0 fusion.40
  58.2 1.0 slice_dynamic-update-slice_fusion
  59.2 0.0 collective-permute-done.3
  59.2 3.0 %fusion.19 = f32[27,256,256]{2,1,0:T(8,128)} fusion(f32[27,256,256]{2,1,0:T(8,128)} %slice_dynamic-update-slice_fusion, f32[26,256,256]{2,1,0:T(8,128)S(1)} %copy-done.1, bf16[9,128,256]{2,1,0:T(8,128)(2,1)} %collective-permute-done.3, bf16[2,9,128,256]{3,2,1,0:T(8,128)(2,1)S(1)} %fusion.21), kind=kOutput, calls=%fused_computation.27 | convolution fusion | flops 151584768 | bytes 5898240 | tf_op jit(solution)/shard_map/fbc,fbd->fcd/dot_general | solution.py:43
  62.2 0.0 all-reduce.2.cloned.1.call-update
  62.2 1.2 copy-done.3
  63.4 11.9 %fusion.29 = f32[1024,256]{1,0:T(8,128)} fusion(f32[1024,256]{1,0:T(8,128)S(1)} %copy-done.3, bf16[13,256,256]{2,1,0:T(8,128)(2,1)} %get-tuple-element.3, bf16[13,256,256]{2,1,0:T(8,128)(2,1)S(1)} %get-tuple-element.2, bf16[26,256,256]{2,1,0:T(8,128)(2,1)} %fusion.18, s32[26,256]{1,0:T(8,128)S(1)} %bitcast.104), kind=kOutput, calls=%fused_computation.35 | convolution fusion | flops 6994919424 | bytes 8939520 | tf_op jit(solution)/shard_map/vkd,kcd->vc/dot_general | solution.py:65
  75.3 1.4 iota_compare_fusion.10
  76.7 0.0 copy-start.9
  76.7 0.0 collective-permute-done.1
  76.7 2.3 fusion.23
  79.0 0.0 collective-permute-done
  79.0 0.0 copy-done.9
  79.1 3.1 %fusion.37 = bf16[1,1024,256]{2,1,0:T(8,128)(2,1)} fusion(f32[1024,256]{1,0:T(8,128)S(1)} %fusion.23, f32[1024,256]{1,0:T(8,128)S(1)} %copy-done.9, bf16[9,128,256]{2,1,0:T(8,128)(2,1)} %collective-permute-done, pred[2,9,128,1024]{2,3,1,0:T(32,128)(4,1)S(1)} %iota_compare_fusion.10), kind=kOutput, calls=%fused_computation.41 | convolution fusion | flops 604766208 | bytes 4390912 | tf_op jit(solution)/shard_map/fbv,fbc->vc/dot_general | solution.py:39
  82.2 144.7 %all-reduce.2.cloned.1.call-done = f32[27,256,256]{2,1,0:T(8,128)} async-done(((f32[27,256,256]{2,1,0:T(8,128)}), f32[27,256,256]{2,1,0:T(8,128)}) %all-reduce.2.cloned.1.call-update) | async-done | bytes 7077904 | tf_op jit(solution)/shard_map/psum | solution.py:97
  226.9 6.9 %broadcast_multiply_fusion = f32[27,256,256]{2,1,0:T(8,128)} fusion(f32[27,256,256]{2,1,0:T(8,128)} %all-reduce.2.cloned.1.call-done), kind=kLoop, calls=%fused_computation.19 | loop fusion | flops 1769472 | bytes 14155776 | tf_op jit(solution)/shard_map/mul | solution.py:98
  (6 shorter events, 0.0 us)
Async XLA Ops:
  7.2 1.1 copy-start
  7.2 219.7 %all-reduce.2.cloned.1.call-start = ((), (), s32[]{:S(2)}) async-start(), calls=%async_computation | async-start | bytes 14155776 | tf_op jit(solution)/shard_map/psum | solution.py:97
  8.2 2.0 copy-start.2
  10.2 9.6 %copy-start.6 = (s32[1,1,2,9,128]{4,2,3,1,0:T(2,128)S(1)}, s32[1,1,2,9,128]{4,2,3,1,0:T(2,128)}, u32[]{:S(2)}) copy-start(s32[1,1,2,9,128]{4,2,3,1,0:T(2,128)} %param.13) | copy-start | bytes 27652
  10.3 9.6 %copy-start.7 = (bf16[1,1024,256]{2,1,0:T(8,128)(2,1)S(1)}, bf16[1,1024,256]{2,1,0:T(8,128)(2,1)}, u32[]{:S(2)}) copy-start(bf16[1,1024,256]{2,1,0:T(8,128)(2,1)} %param.7) | copy-start | bytes 1572868
  11.6 67.4 %collective-permute-start = (bf16[9,128,256]{2,1,0:T(8,128)(2,1)}, bf16[9,128,256]{2,1,0:T(8,128)(2,1)}, u32[]{:S(2)}, u32[]{:S(2)}) collective-permute-start(bf16[9,128,256]{2,1,0:T(8,128)(2,1)} %convolution_convert_fusion.2), channel_id=1, source_target_pairs={{1,0},{2,1},{3,2},{4,3},{5,4},{6,5},{7,6},{8,7},{9,8},{10,9},{11,1... | collective-permute-start | bytes 1769480 | tf_op jit(solution)/shard_map/ppermute | solution.py:12
  16.3 60.4 %collective-permute-start.1 = (bf16[9,128,256]{2,1,0:T(8,128)(2,1)}, bf16[9,128,256]{2,1,0:T(8,128)(2,1)}, u32[]{:S(2)}, u32[]{:S(2)}) collective-permute-start(bf16[9,128,256]{2,1,0:T(8,128)(2,1)} %convolution_convert_fusion.1), channel_id=1, source_target_pairs={{0,1},{1,2},{2,3},{3,4},{4,5},{5,6},{6,7},{7,8},{8,9},{9,10},{10,1... | collective-permute-start | bytes 1769480 | tf_op jit(solution)/shard_map/ppermute | solution.py:12
  19.9 9.5 %copy-start.4 = (s32[1,1,26,256]{3,1,2,0:T(1,128)S(1)}, s32[1,1,26,256]{3,1,2,0:T(1,128)}, u32[]{:S(2)}) copy-start(s32[1,1,26,256]{3,1,2,0:T(1,128)} %param.10) | copy-start | bytes 79876
  19.9 9.5 %copy-start.5 = (s32[1,1,26,256]{3,1,2,0:T(1,128)S(1)}, s32[1,1,26,256]{3,1,2,0:T(1,128)}, u32[]{:S(2)}) copy-start(s32[1,1,26,256]{3,1,2,0:T(1,128)} %param.11) | copy-start | bytes 79876
  23.6 35.6 %collective-permute-start.3 = (bf16[9,128,256]{2,1,0:T(8,128)(2,1)}, bf16[9,128,256]{2,1,0:T(8,128)(2,1)}, u32[]{:S(2)}, u32[]{:S(2)}) collective-permute-start(bf16[9,128,256]{2,1,0:T(8,128)(2,1)} %get-tuple-element.4), channel_id=1, source_target_pairs={{1,0},{2,1},{3,2},{4,3},{5,4},{6,5},{7,6},{8,7},{9,8},{10,9},{11,1... | collective-permute-start | bytes 1769480 | tf_op jit(solution)/shard_map/ppermute | solution.py:12
  25.5 26.5 %collective-permute-start.2 = (bf16[9,128,256]{2,1,0:T(8,128)(2,1)}, bf16[9,128,256]{2,1,0:T(8,128)(2,1)}, u32[]{:S(2)}, u32[]{:S(2)}) collective-permute-start(bf16[9,128,256]{2,1,0:T(8,128)(2,1)} %get-tuple-element.5), channel_id=1, source_target_pairs={{0,1},{1,2},{2,3},{3,4},{4,5},{5,6},{6,7},{7,8},{8,9},{9,10},{10,1... | collective-permute-start | bytes 1769480 | tf_op jit(solution)/shard_map/ppermute | solution.py:12
  48.5 4.6 %copy-start.1 = (f32[26,256,256]{2,1,0:T(8,128)S(1)}, f32[26,256,256]{2,1,0:T(8,128)}, u32[]{:S(2)}) copy-start(f32[26,256,256]{2,1,0:T(8,128)} %fusion.16) | copy-start | bytes 20447236
  52.1 5.0 %copy-start.8 = (bf16[1,1024,256]{2,1,0:T(8,128)(2,1)S(1)}, bf16[1,1024,256]{2,1,0:T(8,128)(2,1)}, u32[]{:S(2)}) copy-start(bf16[1,1024,256]{2,1,0:T(8,128)(2,1)} %param.7) | copy-start | bytes 1572868
  62.2 1.2 copy-start.3
  76.7 2.4 copy-start.9
Sparse Core Ops, SparseCore 0:
  62.3 164.5 all-reduce.1
where the time goes:
time: 241 us
  waiting for transfers between devices  145 us (60%)
  matrix products  50.8 us (21%)
  between operations  14.2 us (6%)
  starting transfers between devices  12.6 us (5%)
  local copies, waits for them, and re-layouts  9.99 us (4%)
  other arithmetic  8.33 us (3%)
    psum x1, waiting for transfers between devices, per_device(): summed = lax.psum(stacked, ('dp', 'region'))  145 us
    ppermute x4, starting transfers between devices, passed_along(): return lax.ppermute(array, axis, pairs)  12.6 us
    dot_general x1, matrix products, per_device(): jnp.einsum('vkd,kcd->vc', placed, side_kernels, preferred_element_type=jn...  11.9 us
    dot_general x3, matrix products, pick_rows(): jnp.einsum('...v,vc->...c', table, source, preferred_element_type=jnp.flo...  11.3 us
    dot_general x1, matrix products, per_device(): jnp.einsum('kpc,kpd->kcd', gathered_x, gathered_g, preferred_element_type...  10.2 us
    mul x1, other arithmetic, per_device(): grad_weight = summed * loss_scale  6.92 us
    dot_general x2, matrix products, face_products(): jnp.einsum('fbc,fbd->fcd', features, grads, preferred_element_type=jnp.fl...  5.98 us
    dot_general x2, matrix products, place_rows(): jnp.einsum('fbv,fbc->vc', table, rows, preferred_element_type=jnp.float32)  5.45 us
  transfers between devices with their start and end apart: 5, of which 1 were waited for; matrix products, arithmetic and copies ran while one was open for 23% of the time, Pallas kernels for 0%

commit v1 on v0

--- a/solution.py
+++ b/solution.py
@@ -1,9 +1,190 @@
+import functools
 import math
 
 import jax
 import jax.numpy as jnp
 from jax import lax
 from jax.sharding import PartitionSpec as P
+
+from jax.experimental import pallas as pl
+from jax.experimental.pallas import tpu as pltpu
+
+MESH_IDS = pl.DeviceIdType.MESH
+COLOR_ORDERS = (("z", "y", "x"), ("y", "x", "z"), ("x", "z", "y"))
+CHUNK_ROWS = 24
+COLOR_ROWS = 128 * CHUNK_ROWS
+PAD_OFFSETS = 36
+
+
+def coords_here():
+    r = lax.axis_index("region")
+    return {"x": lax.axis_index("dp"), "y": r // 8, "z": (r // 2) % 4, "core": r % 2}
+
+
+def peer_of(at, dim, shift):
+    x, y, z, c = at["x"], at["y"], at["z"], at["core"]
+    if dim == "x":
+        x = (x + shift) % 4
+    elif dim == "y":
+        y = (y + shift) % 4
+    elif dim == "z":
+        z = (z + shift) % 4
+    else:
+        c = 1 - c
+    return (x, (y * 4 + z) * 2 + c)
+
+
+def add_rows(dst, first, others, rows, slab):
+    def body(i, carry):
+        at = pl.ds(pl.multiple_of(i * slab, slab), slab)
+        total = first(at)
+        for other in others:
+            total = total + other(at)
+        dst(at, total)
+        return carry
+
+    lax.fori_loop(0, rows // slab, body, 0)
+
+
+def allreduce_kernel(scale, x_ref, out_ref, rcore, part, r1, p1, r2, p2, r3, red, gathered,
+                     core_send, core_recv, rs_send, rs_recv, ag_send, ag_recv, agc_send, agc_recv, out_sem):
+    at = coords_here()
+    half = COLOR_ROWS // 2
+    barrier = pltpu.get_barrier_semaphore()
+    peers = [peer_of(at, "core", 1)] + [peer_of(at, d, s) for d in ("z", "y", "x") for s in (1, 2, 3)]
+    for p in peers:
+        pl.semaphore_signal(barrier, inc=1, device_id=p, device_id_type=MESH_IDS)
+    pl.semaphore_wait(barrier, len(peers))
+
+    c = at["core"]
+    copies = []
+    for k in range(3):
+        cp = pltpu.make_async_remote_copy(
+            src_ref=x_ref.at[pl.ds(pl.multiple_of(k * COLOR_ROWS + (1 - c) * half, 8), half)],
+            dst_ref=rcore.at[k], send_sem=core_send.at[k], recv_sem=core_recv.at[k],
+            device_id=peer_of(at, "core", 1), device_id_type=MESH_IDS)
+        cp.start()
+        copies.append(cp)
+    for k in range(3):
+        copies[k].wait()
+        base = k * COLOR_ROWS + c * half
+        add_rows(lambda a, v, k=k: part.__setitem__((k, a), v),
+                 lambda a, base=base: x_ref[pl.ds(pl.multiple_of(base, 8) + a.start, a.size)],
+                 [lambda a, k=k: rcore[k, a]], half, 128)
+
+    sources = (part, p1, p2)
+    recvs = (r1, r2, r3)
+    blocks = (COLOR_ROWS // 8, COLOR_ROWS // 32, COLOR_ROWS // 128)
+    ranks = [[at[d] for d in order] for order in COLOR_ORDERS]
+    for stage in range(3):
+        blk = blocks[stage]
+        src, rbuf = sources[stage], recvs[stage]
+        staged = []
+        for k, order in enumerate(COLOR_ORDERS):
+            dim = order[stage]
+            me = ranks[k][stage]
+            row = []
+            for s in (1, 2, 3):
+                cp = pltpu.make_async_remote_copy(
+                    src_ref=src.at[k, pl.ds(pl.multiple_of(((me + s) % 4) * blk, 8), blk)],
+                    dst_ref=rbuf.at[k, s - 1], send_sem=rs_send.at[stage, k, s - 1],
+                    recv_sem=rs_recv.at[stage, k, s - 1],
+                    device_id=peer_of(at, dim, s), device_id_type=MESH_IDS)
+                cp.start()
+                row.append(cp)
+            staged.append(row)
+        for k in range(3):
+            for cp in staged[k]:
+                cp.wait()
+            me = ranks[k][stage]
+            own = pl.multiple_of(me * blk, 8)
+            others = [lambda a, k=k, j=j: rbuf[k, j, a] for j in range(3)]
+            first = lambda a, k=k, own=own, src=src: src[k, pl.ds(own + a.start, a.size)]
+            if stage == 0:
+                add_rows(lambda a, v, k=k: p1.__setitem__((k, a), v), first, others, blk, 128)
+            elif stage == 1:
+                add_rows(lambda a, v, k=k: p2.__setitem__((k, a), v), first, others, blk, blk)
+            else:
+                total = first(pl.ds(0, blk)) + others[0](pl.ds(0, blk)) + others[1](pl.ds(0, blk)) + others[2](pl.ds(0, blk))
+                a, b, e = ranks[k]
+                pos = pl.multiple_of(k * COLOR_ROWS + (c * 64 + a * 16 + b * 4 + e) * CHUNK_ROWS, 8)
+                gathered[pl.ds(pos, blk), :] = total * scale
+
+    sizes = (COLOR_ROWS // 128, COLOR_ROWS // 32, COLOR_ROWS // 8)
+    for step, stage in enumerate((2, 1, 0)):
+        blk = sizes[step]
+        staged = []
+        for k, order in enumerate(COLOR_ORDERS):
+            dim = order[stage]
+            a, b, e = ranks[k]
+            lead = (c * 64 + a * 16 + b * 4 + e, c * 64 + a * 16 + b * 4, c * 64 + a * 16)[step]
+            pos = pl.multiple_of(k * COLOR_ROWS + lead * CHUNK_ROWS, 8)
+            row = []
+            for s in (1, 2, 3):
+                cp = pltpu.make_async_remote_copy(
+                    src_ref=gathered.at[pl.ds(pos, blk)], dst_ref=gathered.at[pl.ds(pos, blk)],
+                    send_sem=ag_send.at[stage, k, s - 1], recv_sem=ag_recv.at[stage, k, s - 1],
+                    device_id=peer_of(at, dim, s), device_id_type=MESH_IDS)
+                cp.start()
+                row.append(cp)
+            staged.append(row)
+        for row in staged:
+            for cp in row:
+                cp.wait()
+    last = []
+    for k in range(3):
+        pos = pl.multiple_of(k * COLOR_ROWS + c * half, 8)
+        cp = pltpu.make_async_remote_copy(
+            src_ref=gathered.at[pl.ds(pos, half)], dst_ref=gathered.at[pl.ds(pos, half)],
+            send_sem=agc_send.at[k], recv_sem=agc_recv.at[k],
+            device_id=peer_of(at, "core", 1), device_id_type=MESH_IDS)
+        cp.start()
+        last.append(cp)
+    for cp in last:
+        cp.wait()
+    done = pltpu.make_async_copy(gathered, out_ref, out_sem)
+    done.start()
+    done.wait()
+
+
+def summed_everywhere(stacked, scale):
+    rows = PAD_OFFSETS * 256
+    width = stacked.shape[2]
+    data = jnp.concatenate(
+        [stacked, jnp.zeros((PAD_OFFSETS - stacked.shape[0],) + stacked.shape[1:], stacked.dtype)], 0
+    ).reshape(rows, width)
+    f32 = jnp.float32
+    blocks = (COLOR_ROWS // 8, COLOR_ROWS // 32, COLOR_ROWS // 128)
+    total = pl.pallas_call(
+        functools.partial(allreduce_kernel, scale),
+        out_shape=jax.ShapeDtypeStruct((rows, width), f32),
+        in_specs=[pl.BlockSpec(memory_space=pltpu.VMEM)],
+        out_specs=pl.BlockSpec(memory_space=pl.ANY),
+        scratch_shapes=[
+            pltpu.VMEM((3, COLOR_ROWS // 2, width), f32),
+            pltpu.VMEM((3, COLOR_ROWS // 2, width), f32),
+            pltpu.VMEM((3, 3, blocks[0], width), f32),
+            pltpu.VMEM((3, blocks[0], width), f32),
+            pltpu.VMEM((3, 3, blocks[1], width), f32),
+            pltpu.VMEM((3, blocks[1], width), f32),
+            pltpu.VMEM((3, 3, blocks[2], width), f32),
+            pltpu.VMEM((3, blocks[2], width), f32),
+            pltpu.VMEM((rows, width), f32),
+            pltpu.SemaphoreType.DMA((3,)),
+            pltpu.SemaphoreType.DMA((3,)),
+            pltpu.SemaphoreType.DMA((3, 3, 3)),
+            pltpu.SemaphoreType.DMA((3, 3, 3)),
+            pltpu.SemaphoreType.DMA((3, 3, 3)),
+            pltpu.SemaphoreType.DMA((3, 3, 3)),
+            pltpu.SemaphoreType.DMA((3,)),
+            pltpu.SemaphoreType.DMA((3,)),
+            pltpu.SemaphoreType.DMA(()),
+        ],
+        compiler_params=pltpu.CompilerParams(
+            collective_id=0, has_side_effects=True, vmem_limit_bytes=64 * 1024 * 1024
+        ),
+    )(data)
+    return total[: stacked.shape[0] * stacked.shape[1]].reshape(stacked.shape)
 
 
 def passed_along(array, axis, by):
@@ -94,8 +275,7 @@
         0,
     )
     loss_scale = 1.0 / math.sqrt(pairs * lax.axis_size("dp") * lax.axis_size("region"))
-    summed = lax.psum(stacked, ("dp", "region"))
-    grad_weight = summed * loss_scale
+    grad_weight = summed_everywhere(stacked, loss_scale)
     grad_input = accumulated.astype(jnp.bfloat16)[None]
     return (grad_input, grad_weight)
 

time: 241 us -> 175 us (0.73)
  waiting for transfers between devices: 145 us -> 0.01 us
  Pallas kernels: 0 us -> 93 us
  between operations: 14.2 us -> 0.83 us
  other arithmetic: 8.33 us -> 2.83 us
  local copies, waits for them, and re-layouts: 9.99 us -> 13 us
    psum x1 -> x0, waiting for transfers between devices: 145 us -> none  [per_device(): summed = lax.psum(stacked, ('dp', 'region'))]
    pallas_call x0 -> x1, Pallas kernels: none -> 93 us  [summed_everywhere(): pl.pallas_call(functools.partial(allreduce_kernel, scale), out_shape=jax....]
    mul x1 -> x0, other arithmetic: 6.92 us -> none  [per_device(): grad_weight = summed * loss_scale]
    slice x0 -> x1, local copies, waits for them, and re-layouts: none -> 6.58 us  [summed_everywhere(): return total[:stacked.shape[0] * stacked.shape[1]].reshape(stacked.shape)]
    slice x1, local copies, waits for them, and re-layouts: 3.57 us -> 0.22 us  [per_device(): side_kernels = jnp.concatenate([weight[0:13], weight[14:27]], 0)]
  transfers between devices with their start and end apart: 5 -> 4, of which waited for: 1 -> 0; matrix products, arithmetic and copies ran while one was open for 23% -> 34% of each run, Pallas kernels for 0% -> 53%
where the time goes in v1:
time: 175 us
  Pallas kernels  93 us (53%)
  matrix products  52.3 us (30%)
  local copies, waits for them, and re-layouts  13 us (7%)
  starting transfers between devices  12.6 us (7%)
  other arithmetic  2.83 us (2%)
    pallas_call x1, Pallas kernels, summed_everywhere(): pl.pallas_call(functools.partial(allreduce_kernel, scale), out_shape=jax....  93 us
    ppermute x4, starting transfers between devices, passed_along(): return lax.ppermute(array, axis, pairs)  12.6 us
    dot_general x3, matrix products, pick_rows(): jnp.einsum('...v,vc->...c', table, source, preferred_element_type=jnp.flo...  12.4 us
    dot_general x1, matrix products, per_device(): jnp.einsum('vkd,kcd->vc', placed, side_kernels, preferred_element_type=jn...  12.1 us
    dot_general x1, matrix products, per_device(): jnp.einsum('kpc,kpd->kcd', gathered_x, gathered_g, preferred_element_type...  10.4 us
    dot_general x2, matrix products, face_products(): jnp.einsum('fbc,fbd->fcd', features, grads, preferred_element_type=jnp.fl...  6.93 us
    slice x1, local copies, waits for them, and re-layouts, summed_everywhere(): return total[:stacked.shape[0] * stacked.shape[1]].reshape(stacked.shape)  6.58 us
    dot_general x2, matrix products, place_rows(): jnp.einsum('fbv,fbc->vc', table, rows, preferred_element_type=jnp.float32)  5.44 us
  transfers between devices with their start and end apart: 4, of which 0 were waited for; matrix products, arithmetic and copies ran while one was open for 34% of the time, Pallas kernels for 53%

profile of v1, /device:TPU:1, one launch (start us, length us, event | category | flops | bytes accessed | tf_op | source)
XLA Modules:
  0.0 174.6 jit_solution(11012779079689931890)
XLA Ops:
  0.6 0.7 copy.10
  1.3 3.2 %fusion.21 = bf16[2,9,128,256]{3,2,1,0:T(8,128)(2,1)S(1)} fusion(s32[2,9,128]{2,1,0:T(8,128)S(1)} %copy.10, bf16[1,1024,256]{2,1,0:T(8,128)(2,1)} %param.8), kind=kOutput, calls=%fused_computation.30 | convolution fusion | flops 1210908672 | bytes 1713152 | tf_op jit(solution)/shard_map/...v,vc->...c/dot_general | solution.py:214
  4.5 0.0 copy-done.1
  4.5 0.0 copy-start.3
  4.6 0.0 copy-start.9
  4.6 0.0 copy-start.10
  4.6 1.4 convolution_convert_fusion.2
  5.9 3.3 %collective-permute-start = (bf16[9,128,256]{2,1,0:T(8,128)(2,1)}, bf16[9,128,256]{2,1,0:T(8,128)(2,1)}, u32[]{:S(2)}, u32[]{:S(2)}) collective-permute-start(bf16[9,128,256]{2,1,0:T(8,128)(2,1)} %convolution_convert_fusion.2), channel_id=1, source_target_pairs={{1,0},{2,1},{3,2},{4,3},{5,4},{6,5},{7,6},{8,7},{9,8},{10,9},{11,1... | collective-permute-start | bytes 1769480 | tf_op jit(solution)/shard_map/ppermute | solution.py:193
  9.2 0.0 copy-done.3
  9.3 1.4 convolution_convert_fusion.1
  10.6 3.6 %collective-permute-start.1 = (bf16[9,128,256]{2,1,0:T(8,128)(2,1)}, bf16[9,128,256]{2,1,0:T(8,128)(2,1)}, u32[]{:S(2)}, u32[]{:S(2)}) collective-permute-start(bf16[9,128,256]{2,1,0:T(8,128)(2,1)} %convolution_convert_fusion.1), channel_id=1, source_target_pairs={{0,1},{1,2},{2,3},{3,4},{4,5},{5,6},{6,7},{7,8},{8,9},{9,10},{10,1... | collective-permute-start | bytes 1769480 | tf_op jit(solution)/shard_map/ppermute | solution.py:193
  14.2 0.0 copy-done.9
  14.2 0.0 copy-done.10
  14.2 0.0 copy-start.5
  14.2 2.6 %convolution_convert_fusion = bf16[2,9,128,256]{3,2,1,0:T(8,128)(2,1)S(1)} fusion(bf16[1,1024,256]{2,1,0:T(8,128)(2,1)S(1)} %copy-done.10, s32[2,9,128]{2,1,0:T(8,128)S(1)} %copy.9), kind=kOutput, calls=%fused_computation.29 | convolution fusion | flops 1210908672 | bytes 1713152 | tf_op jit(solution)/shard_map/...v,vc->...c/dot_general | solution.py:214
  16.9 1.1 slice_bitcast_fusion.16
  18.0 1.9 %collective-permute-start.3 = (bf16[9,128,256]{2,1,0:T(8,128)(2,1)}, bf16[9,128,256]{2,1,0:T(8,128)(2,1)}, u32[]{:S(2)}, u32[]{:S(2)}) collective-permute-start(bf16[9,128,256]{2,1,0:T(8,128)(2,1)} %get-tuple-element.4), channel_id=1, source_target_pairs={{1,0},{2,1},{3,2},{4,3},{5,4},{6,5},{7,6},{8,7},{9,8},{10,9},{11,1... | collective-permute-start | bytes 1769480 | tf_op jit(solution)/shard_map/ppermute | solution.py:193
  19.9 3.8 %collective-permute-start.2 = (bf16[9,128,256]{2,1,0:T(8,128)(2,1)}, bf16[9,128,256]{2,1,0:T(8,128)(2,1)}, u32[]{:S(2)}, u32[]{:S(2)}) collective-permute-start(bf16[9,128,256]{2,1,0:T(8,128)(2,1)} %get-tuple-element.5), channel_id=1, source_target_pairs={{0,1},{1,2},{2,3},{3,4},{4,5},{5,6},{6,7},{7,8},{8,9},{9,10},{10,1... | collective-permute-start | bytes 1769480 | tf_op jit(solution)/shard_map/ppermute | solution.py:193
  23.7 0.0 copy-done.5
  23.8 1.3 fusion.48
  25.1 0.2 fusion.53
  25.3 0.5 copy-done.7
  25.8 0.0 copy-done.8
  25.8 6.5 %fusion.18 = bf16[26,256,256]{2,1,0:T(8,128)(2,1)} fusion(s32[26,256]{1,0:T(8,128)S(1)} %bitcast.108, bf16[1,1024,256]{2,1,0:T(8,128)(2,1)S(1)} %copy-done.5), kind=kOutput, calls=%fused_computation.24 | convolution fusion | flops 3498180608 | bytes 3958784 | tf_op jit(solution)/shard_map/...v,vc->...c/dot_general | solution.py:214
  32.4 12.1 %fusion.29 = f32[1024,256]{1,0:T(8,128)} fusion(f32[1024,256]{1,0:T(8,128)} %fusion.48, bf16[13,256,256]{2,1,0:T(8,128)(2,1)S(1)} %get-tuple-element.3, bf16[13,256,256]{2,1,0:T(8,128)(2,1)S(1)} %get-tuple-element.2, bf16[26,256,256]{2,1,0:T(8,128)(2,1)} %fusion.18, s32[26,256]{1,0:T(8,128)S(1)} %bitcast.106), kind=kOutput, calls=%fused_computation.34 | convolution fusion | flops 6994919424 | bytes 8939520 | tf_op jit(solution)/shard_map/vkd,kcd->vc/dot_general | solution.py:246
  44.5 10.4 %fusion.16 = f32[26,256,256]{2,1,0:T(8,128)} fusion(bf16[26,256,256]{2,1,0:T(8,128)(2,1)} %fusion.18, s32[26,256]{1,0:T(8,128)S(1)} %bitcast.107, bf16[1,1024,256]{2,1,0:T(8,128)(2,1)} %param.7), kind=kOutput, calls=%fused_computation.22 | convolution fusion | flops 4370595840 | bytes 10774528 | tf_op jit(solution)/shard_map/kpc,kpd->kcd/dot_general | solution.py:249
  54.9 2.8 %iota_compare_fusion.10 = pred[2,9,128,1024]{2,3,1,0:T(32,128)(4,1)} fusion(s32[2,9,128]{2,1,0:T(8,128)S(1)} %copy.9), kind=kLoop, calls=%fused_computation.12 | loop fusion | flops 2359296 | bytes 2368512 | tf_op jit(solution)/shard_map/eq | solution.py:210
  57.7 0.0 collective-permute-done.2
  57.7 0.0 copy-done.4
  57.7 3.9 %fusion.20 = f32[36,256,256]{2,1,0:T(8,128)} fusion(f32[26,256,256]{2,1,0:T(8,128)} %fusion.16, bf16[9,128,256]{2,1,0:T(8,128)(2,1)} %collective-permute-done.2, bf16[2,9,128,256]{3,2,1,0:T(8,128)(2,1)S(1)} %copy-done.4), kind=kOutput, calls=%fused_computation.28 | convolution fusion | flops 151584768 | bytes 5898240 | tf_op jit(solution)/shard_map/fbc,fbd->fcd/dot_general | solution.py:224
  61.6 0.0 copy-done
  61.6 1.1 slice_dynamic-update-slice_fusion.1
  62.7 0.0 copy-done.6
  62.7 0.0 copy-done.11
  62.7 1.0 fusion.40
  63.7 1.0 slice_dynamic-update-slice_fusion
  64.8 0.0 collective-permute-done.3
  64.8 3.0 %fusion.19 = f32[36,256,256]{2,1,0:T(8,128)} fusion(f32[36,256,256]{2,1,0:T(8,128)} %slice_dynamic-update-slice_fusion, f32[26,256,256]{2,1,0:T(8,128)S(1)} %copy-done, bf16[9,128,256]{2,1,0:T(8,128)(2,1)} %collective-permute-done.3, bf16[2,9,128,256]{3,2,1,0:T(8,128)(2,1)S(1)} %copy-done.4), kind=kOutput, calls=%fused_computation.26 | convolution fusion | flops 151584768 | bytes 5898240 | tf_op jit(solution)/shard_map/fbc,fbd->fcd/dot_general | solution.py:224
  67.8 1.7 broadcast_dynamic-update-slice_fusion
  69.5 93.0 %shard_map.86 = f32[9216,256]{1,0:T(8,128)} custom-call(f32[9216,256]{1,0:T(8,128)} %bitcast.23.x_ref), custom_call_target="tpu_custom_call" | custom-call | tf_op jit(solution)/shard_map/pallas_call | solution.py:158
  162.5 0.0 copy-start.2
  162.5 6.6 %slice.63 = f32[6912,256]{1,0:T(8,128)} slice(f32[9216,256]{1,0:T(8,128)} %shard_map.86), slice={[0:6912], [0:256]} | slice | bytes 14155776 | tf_op jit(solution)/shard_map/slice | solution.py:187
  169.1 0.0 collective-permute-done.1
  169.1 0.0 copy-done.2
  169.1 2.3 %fusion.23 = f32[1024,256]{1,0:T(8,128)S(1)} fusion(bf16[9,128,256]{2,1,0:T(8,128)(2,1)} %collective-permute-done.1, pred[2,9,128,1024]{2,3,1,0:T(32,128)(4,1)S(1)} %copy-done.2), kind=kOutput, calls=%fused_computation.32 | convolution fusion | flops 603979776 | bytes 2818048 | tf_op jit(solution)/shard_map/fbv,fbc->vc/dot_general | solution.py:220
  171.4 0.0 collective-permute-done
  171.4 0.0 copy-done.12
  171.4 3.1 %fusion.37 = bf16[1,1024,256]{2,1,0:T(8,128)(2,1)} fusion(f32[1024,256]{1,0:T(8,128)S(1)} %fusion.23, f32[1024,256]{1,0:T(8,128)S(1)} %copy-done.12, bf16[9,128,256]{2,1,0:T(8,128)(2,1)} %collective-permute-done, pred[2,9,128,1024]{2,3,1,0:T(32,128)(4,1)S(1)} %copy-done.2), kind=kOutput, calls=%fused_computation.40 | convolution fusion | flops 604766208 | bytes 4390912 | tf_op jit(solution)/shard_map/fbv,fbc->vc/dot_general | solution.py:220
  (11 shorter events, 0.0 us)
Async XLA Ops:
  1.3 3.2 %copy-start.1 = (bf16[27,256,256]{2,1,0:T(8,128)(2,1)S(1)}, bf16[27,256,256]{2,1,0:T(8,128)(2,1)}, u32[]{:S(2)}) copy-start(bf16[27,256,256]{2,1,0:T(8,128)(2,1)} %param.9) | copy-start | bytes 10616836
  4.5 4.7 %copy-start.3 = (bf16[2,9,128,256]{3,2,1,0:T(8,128)(2,1)}, bf16[2,9,128,256]{3,2,1,0:T(8,128)(2,1)S(1)}, u32[]{:S(2)}) copy-start(bf16[2,9,128,256]{3,2,1,0:T(8,128)(2,1)S(1)} %fusion.21) | copy-start | bytes 3538948
  4.6 9.6 %copy-start.9 = (s32[1,1,2,9,128]{4,2,3,1,0:T(2,128)S(1)}, s32[1,1,2,9,128]{4,2,3,1,0:T(2,128)}, u32[]{:S(2)}) copy-start(s32[1,1,2,9,128]{4,2,3,1,0:T(2,128)} %param.13) | copy-start | bytes 27652
  4.6 9.6 %copy-start.10 = (bf16[1,1024,256]{2,1,0:T(8,128)(2,1)S(1)}, bf16[1,1024,256]{2,1,0:T(8,128)(2,1)}, u32[]{:S(2)}) copy-start(bf16[1,1024,256]{2,1,0:T(8,128)(2,1)} %param.7) | copy-start | bytes 1572868
  5.9 165.5 %collective-permute-start = (bf16[9,128,256]{2,1,0:T(8,128)(2,1)}, bf16[9,128,256]{2,1,0:T(8,128)(2,1)}, u32[]{:S(2)}, u32[]{:S(2)}) collective-permute-start(bf16[9,128,256]{2,1,0:T(8,128)(2,1)} %convolution_convert_fusion.2), channel_id=1, source_target_pairs={{1,0},{2,1},{3,2},{4,3},{5,4},{6,5},{7,6},{8,7},{9,8},{10,9},{11,1... | collective-permute-start | bytes 1769480 | tf_op jit(solution)/shard_map/ppermute | solution.py:193
  10.6 158.5 %collective-permute-start.1 = (bf16[9,128,256]{2,1,0:T(8,128)(2,1)}, bf16[9,128,256]{2,1,0:T(8,128)(2,1)}, u32[]{:S(2)}, u32[]{:S(2)}) collective-permute-start(bf16[9,128,256]{2,1,0:T(8,128)(2,1)} %convolution_convert_fusion.1), channel_id=1, source_target_pairs={{0,1},{1,2},{2,3},{3,4},{4,5},{5,6},{6,7},{7,8},{8,9},{9,10},{10,1... | collective-permute-start | bytes 1769480 | tf_op jit(solution)/shard_map/ppermute | solution.py:193
  14.2 9.5 %copy-start.5 = (bf16[1,1024,256]{2,1,0:T(8,128)(2,1)S(1)}, bf16[1,1024,256]{2,1,0:T(8,128)(2,1)}, u32[]{:S(2)}) copy-start(bf16[1,1024,256]{2,1,0:T(8,128)(2,1)} %param.8) | copy-start | bytes 1572868
  18.0 46.8 %collective-permute-start.3 = (bf16[9,128,256]{2,1,0:T(8,128)(2,1)}, bf16[9,128,256]{2,1,0:T(8,128)(2,1)}, u32[]{:S(2)}, u32[]{:S(2)}) collective-permute-start(bf16[9,128,256]{2,1,0:T(8,128)(2,1)} %get-tuple-element.4), channel_id=1, source_target_pairs={{1,0},{2,1},{3,2},{4,3},{5,4},{6,5},{7,6},{8,7},{9,8},{10,9},{11,1... | collective-permute-start | bytes 1769480 | tf_op jit(solution)/shard_map/ppermute | solution.py:193
  19.9 37.8 %collective-permute-start.2 = (bf16[9,128,256]{2,1,0:T(8,128)(2,1)}, bf16[9,128,256]{2,1,0:T(8,128)(2,1)}, u32[]{:S(2)}, u32[]{:S(2)}) collective-permute-start(bf16[9,128,256]{2,1,0:T(8,128)(2,1)} %get-tuple-element.5), channel_id=1, source_target_pairs={{0,1},{1,2},{2,3},{3,4},{4,5},{5,6},{6,7},{7,8},{8,9},{9,10},{10,1... | collective-permute-start | bytes 1769480 | tf_op jit(solution)/shard_map/ppermute | solution.py:193
  25.1 0.7 copy-start.7
  25.1 0.8 copy-start.8
  44.5 13.2 %copy-start.4 = (bf16[2,9,128,256]{3,2,1,0:T(8,128)(2,1)S(1)}, bf16[2,9,128,256]{3,2,1,0:T(8,128)(2,1)}, u32[]{:S(2)}) copy-start(bf16[2,9,128,256]{3,2,1,0:T(8,128)(2,1)} %copy-done.3) | copy-start | bytes 3538948
  54.9 6.7 %copy-start = (f32[26,256,256]{2,1,0:T(8,128)S(1)}, f32[26,256,256]{2,1,0:T(8,128)}, u32[]{:S(2)}) copy-start(f32[26,256,256]{2,1,0:T(8,128)} %fusion.16) | copy-start | bytes 20447236
  57.7 5.0 %copy-start.6 = (bf16[1,1024,256]{2,1,0:T(8,128)(2,1)S(1)}, bf16[1,1024,256]{2,1,0:T(8,128)(2,1)}, u32[]{:S(2)}) copy-start(bf16[1,1024,256]{2,1,0:T(8,128)(2,1)} %param.8) | copy-start | bytes 1572868
  57.7 5.0 %copy-start.11 = (bf16[1,1024,256]{2,1,0:T(8,128)(2,1)S(1)}, bf16[1,1024,256]{2,1,0:T(8,128)(2,1)}, u32[]{:S(2)}) copy-start(bf16[1,1024,256]{2,1,0:T(8,128)(2,1)} %param.7) | copy-start | bytes 1572868
  162.5 6.6 %copy-start.2 = (pred[2,9,128,1024]{2,3,1,0:T(32,128)(4,1)S(1)}, pred[2,9,128,1024]{2,3,1,0:T(32,128)(4,1)}, u32[]{:S(2)}) copy-start(pred[2,9,128,1024]{2,3,1,0:T(32,128)(4,1)} %iota_compare_fusion.10) | copy-start | bytes 7077892
  169.1 2.3 %copy-start.12 = (f32[1024,256]{1,0:T(8,128)S(1)}, f32[1024,256]{1,0:T(8,128)}, u32[]{:S(2)}) copy-start(f32[1024,256]{1,0:T(8,128)} %fusion.29) | copy-start | bytes 3145732

commit v2 on v1

--- a/solution.py
+++ b/solution.py
@@ -46,7 +46,7 @@
     lax.fori_loop(0, rows // slab, body, 0)
 
 
-def allreduce_kernel(scale, x_ref, out_ref, rcore, part, r1, p1, r2, p2, r3, red, gathered,
+def allreduce_kernel(scale, x_ref, out_ref, rcore, part, r1, p1, r2, p2, r3, red,
                      core_send, core_recv, rs_send, rs_recv, ag_send, ag_recv, agc_send, agc_recv, out_sem):
     at = coords_here()
     half = COLOR_ROWS // 2
@@ -108,7 +108,10 @@
                 total = first(pl.ds(0, blk)) + others[0](pl.ds(0, blk)) + others[1](pl.ds(0, blk)) + others[2](pl.ds(0, blk))
                 a, b, e = ranks[k]
                 pos = pl.multiple_of(k * COLOR_ROWS + (c * 64 + a * 16 + b * 4 + e) * CHUNK_ROWS, 8)
-                gathered[pl.ds(pos, blk), :] = total * scale
+                red[k] = total * scale
+                put = pltpu.make_async_copy(red.at[k], out_ref.at[pl.ds(pos, blk)], out_sem.at[k])
+                put.start()
+                put.wait()
 
     sizes = (COLOR_ROWS // 128, COLOR_ROWS // 32, COLOR_ROWS // 8)
     for step, stage in enumerate((2, 1, 0)):
@@ -122,7 +125,7 @@
             row = []
             for s in (1, 2, 3):
                 cp = pltpu.make_async_remote_copy(
-                    src_ref=gathered.at[pl.ds(pos, blk)], dst_ref=gathered.at[pl.ds(pos, blk)],
+                    src_ref=out_ref.at[pl.ds(pos, blk)], dst_ref=out_ref.at[pl.ds(pos, blk)],
                     send_sem=ag_send.at[stage, k, s - 1], recv_sem=ag_recv.at[stage, k, s - 1],
                     device_id=peer_of(at, dim, s), device_id_type=MESH_IDS)
                 cp.start()
@@ -135,16 +138,13 @@
     for k in range(3):
         pos = pl.multiple_of(k * COLOR_ROWS + c * half, 8)
         cp = pltpu.make_async_remote_copy(
-            src_ref=gathered.at[pl.ds(pos, half)], dst_ref=gathered.at[pl.ds(pos, half)],
+            src_ref=out_ref.at[pl.ds(pos, half)], dst_ref=out_ref.at[pl.ds(pos, half)],
             send_sem=agc_send.at[k], recv_sem=agc_recv.at[k],
             device_id=peer_of(at, "core", 1), device_id_type=MESH_IDS)
         cp.start()
         last.append(cp)
     for cp in last:
         cp.wait()
-    done = pltpu.make_async_copy(gathered, out_ref, out_sem)
-    done.start()
-    done.wait()
 
 
 def summed_everywhere(stacked, scale):
@@ -169,16 +169,15 @@
             pltpu.VMEM((3, blocks[1], width), f32),
             pltpu.VMEM((3, 3, blocks[2], width), f32),
             pltpu.VMEM((3, blocks[2], width), f32),
-            pltpu.VMEM((rows, width), f32),
-            pltpu.SemaphoreType.DMA((3,)),
-            pltpu.SemaphoreType.DMA((3,)),
-            pltpu.SemaphoreType.DMA((3, 3, 3)),
-            pltpu.SemaphoreType.DMA((3, 3, 3)),
-            pltpu.SemaphoreType.DMA((3, 3, 3)),
-            pltpu.SemaphoreType.DMA((3, 3, 3)),
-            pltpu.SemaphoreType.DMA((3,)),
-            pltpu.SemaphoreType.DMA((3,)),
-            pltpu.SemaphoreType.DMA(()),
+            pltpu.SemaphoreType.DMA((3,)),
+            pltpu.SemaphoreType.DMA((3,)),
+            pltpu.SemaphoreType.DMA((3, 3, 3)),
+            pltpu.SemaphoreType.DMA((3, 3, 3)),
+            pltpu.SemaphoreType.DMA((3, 3, 3)),
+            pltpu.SemaphoreType.DMA((3, 3, 3)),
+            pltpu.SemaphoreType.DMA((3,)),
+            pltpu.SemaphoreType.DMA((3,)),
+            pltpu.SemaphoreType.DMA((3,)),
         ],
         compiler_params=pltpu.CompilerParams(
             collective_id=0, has_side_effects=True, vmem_limit_bytes=64 * 1024 * 1024

time: 175 us -> 172 us (0.983)
  Pallas kernels: 93 us -> 89.8 us
    pallas_call x1, Pallas kernels: 93 us -> 89.8 us  [summed_everywhere(): pl.pallas_call(functools.partial(allreduce_kernel, scale), out_shape=jax....]
  transfers between devices with their start and end apart: 4 -> 4, of which waited for: 0 -> 0; matrix products, arithmetic and copies ran while one was open for 34% -> 35% of each run, Pallas kernels for 53% -> 52%
where the time goes in v2:
time: 172 us; the launch traced here: 171 us
  Pallas kernels  89.8 us (52%)
  matrix products  52.3 us (30%)
  local copies, waits for them, and re-layouts  13 us (8%)
  starting transfers between devices  12.6 us (7%)
  other arithmetic  2.83 us (2%)
    pallas_call x1, Pallas kernels, summed_everywhere(): pl.pallas_call(functools.partial(allreduce_kernel, scale), out_shape=jax....  89.8 us
    ppermute x4, starting transfers between devices, passed_along(): return lax.ppermute(array, axis, pairs)  12.6 us
    dot_general x3, matrix products, pick_rows(): jnp.einsum('...v,vc->...c', table, source, preferred_element_type=jnp.flo...  12.4 us
    dot_general x1, matrix products, per_device(): jnp.einsum('vkd,kcd->vc', placed, side_kernels, preferred_element_type=jn...  12.1 us
    dot_general x1, matrix products, per_device(): jnp.einsum('kpc,kpd->kcd', gathered_x, gathered_g, preferred_element_type...  10.4 us
    dot_general x2, matrix products, face_products(): jnp.einsum('fbc,fbd->fcd', features, grads, preferred_element_type=jnp.fl...  6.93 us
    slice x1, local copies, waits for them, and re-layouts, summed_everywhere(): return total[:stacked.shape[0] * stacked.shape[1]].reshape(stacked.shape)  6.58 us
    dot_general x2, matrix products, place_rows(): jnp.einsum('fbv,fbc->vc', table, rows, preferred_element_type=jnp.float32)  5.43 us
  transfers between devices with their start and end apart: 4, of which 0 were waited for; matrix products, arithmetic and copies ran while one was open for 35% of the time, Pallas kernels for 52%

profile of v2, /device:TPU:1, one launch (start us, length us, event | category | flops | bytes accessed | tf_op | source)
XLA Modules:
  0.0 171.3 jit_solution(11044121289261102875)
XLA Ops:
  0.6 0.7 copy.10
  1.3 3.2 %fusion.21 = bf16[2,9,128,256]{3,2,1,0:T(8,128)(2,1)S(1)} fusion(s32[2,9,128]{2,1,0:T(8,128)S(1)} %copy.10, bf16[1,1024,256]{2,1,0:T(8,128)(2,1)} %param.8), kind=kOutput, calls=%fused_computation.30 | convolution fusion | flops 1210908672 | bytes 1713152 | tf_op jit(solution)/shard_map/...v,vc->...c/dot_general | solution.py:213
  4.5 0.0 copy-done.1
  4.5 0.0 copy-start.3
  4.6 0.0 copy-start.9
  4.6 0.0 copy-start.10
  4.6 1.4 convolution_convert_fusion.2
  5.9 3.3 %collective-permute-start = (bf16[9,128,256]{2,1,0:T(8,128)(2,1)}, bf16[9,128,256]{2,1,0:T(8,128)(2,1)}, u32[]{:S(2)}, u32[]{:S(2)}) collective-permute-start(bf16[9,128,256]{2,1,0:T(8,128)(2,1)} %convolution_convert_fusion.2), channel_id=1, source_target_pairs={{1,0},{2,1},{3,2},{4,3},{5,4},{6,5},{7,6},{8,7},{9,8},{10,9},{11,1... | collective-permute-start | bytes 1769480 | tf_op jit(solution)/shard_map/ppermute | solution.py:192
  9.2 0.0 copy-done.3
  9.3 1.4 convolution_convert_fusion.1
  10.6 3.6 %collective-permute-start.1 = (bf16[9,128,256]{2,1,0:T(8,128)(2,1)}, bf16[9,128,256]{2,1,0:T(8,128)(2,1)}, u32[]{:S(2)}, u32[]{:S(2)}) collective-permute-start(bf16[9,128,256]{2,1,0:T(8,128)(2,1)} %convolution_convert_fusion.1), channel_id=1, source_target_pairs={{0,1},{1,2},{2,3},{3,4},{4,5},{5,6},{6,7},{7,8},{8,9},{9,10},{10,1... | collective-permute-start | bytes 1769480 | tf_op jit(solution)/shard_map/ppermute | solution.py:192
  14.2 0.0 copy-done.9
  14.2 0.0 copy-done.10
  14.2 0.0 copy-start.5
  14.2 2.6 %convolution_convert_fusion = bf16[2,9,128,256]{3,2,1,0:T(8,128)(2,1)S(1)} fusion(bf16[1,1024,256]{2,1,0:T(8,128)(2,1)S(1)} %copy-done.10, s32[2,9,128]{2,1,0:T(8,128)S(1)} %copy.9), kind=kOutput, calls=%fused_computation.29 | convolution fusion | flops 1210908672 | bytes 1713152 | tf_op jit(solution)/shard_map/...v,vc->...c/dot_general | solution.py:213
  16.9 1.1 slice_bitcast_fusion.16
  18.0 1.9 %collective-permute-start.3 = (bf16[9,128,256]{2,1,0:T(8,128)(2,1)}, bf16[9,128,256]{2,1,0:T(8,128)(2,1)}, u32[]{:S(2)}, u32[]{:S(2)}) collective-permute-start(bf16[9,128,256]{2,1,0:T(8,128)(2,1)} %get-tuple-element.4), channel_id=1, source_target_pairs={{1,0},{2,1},{3,2},{4,3},{5,4},{6,5},{7,6},{8,7},{9,8},{10,9},{11,1... | collective-permute-start | bytes 1769480 | tf_op jit(solution)/shard_map/ppermute | solution.py:192
  19.9 3.8 %collective-permute-start.2 = (bf16[9,128,256]{2,1,0:T(8,128)(2,1)}, bf16[9,128,256]{2,1,0:T(8,128)(2,1)}, u32[]{:S(2)}, u32[]{:S(2)}) collective-permute-start(bf16[9,128,256]{2,1,0:T(8,128)(2,1)} %get-tuple-element.5), channel_id=1, source_target_pairs={{0,1},{1,2},{2,3},{3,4},{4,5},{5,6},{6,7},{7,8},{8,9},{9,10},{10,1... | collective-permute-start | bytes 1769480 | tf_op jit(solution)/shard_map/ppermute | solution.py:192
  23.7 0.0 copy-done.5
  23.8 1.3 fusion.48
  25.1 0.2 fusion.53
  25.3 0.5 copy-done.7
  25.8 0.0 copy-done.8
  25.8 6.5 %fusion.18 = bf16[26,256,256]{2,1,0:T(8,128)(2,1)} fusion(s32[26,256]{1,0:T(8,128)S(1)} %bitcast.108, bf16[1,1024,256]{2,1,0:T(8,128)(2,1)S(1)} %copy-done.5), kind=kOutput, calls=%fused_computation.24 | convolution fusion | flops 3498180608 | bytes 3958784 | tf_op jit(solution)/shard_map/...v,vc->...c/dot_general | solution.py:213
  32.4 12.1 %fusion.29 = f32[1024,256]{1,0:T(8,128)} fusion(f32[1024,256]{1,0:T(8,128)} %fusion.48, bf16[13,256,256]{2,1,0:T(8,128)(2,1)S(1)} %get-tuple-element.3, bf16[13,256,256]{2,1,0:T(8,128)(2,1)S(1)} %get-tuple-element.2, bf16[26,256,256]{2,1,0:T(8,128)(2,1)} %fusion.18, s32[26,256]{1,0:T(8,128)S(1)} %bitcast.106), kind=kOutput, calls=%fused_computation.34 | convolution fusion | flops 6994919424 | bytes 8939520 | tf_op jit(solution)/shard_map/vkd,kcd->vc/dot_general | solution.py:245
  44.5 10.4 %fusion.16 = f32[26,256,256]{2,1,0:T(8,128)} fusion(bf16[26,256,256]{2,1,0:T(8,128)(2,1)} %fusion.18, s32[26,256]{1,0:T(8,128)S(1)} %bitcast.107, bf16[1,1024,256]{2,1,0:T(8,128)(2,1)} %param.7), kind=kOutput, calls=%fused_computation.22 | convolution fusion | flops 4370595840 | bytes 10774528 | tf_op jit(solution)/shard_map/kpc,kpd->kcd/dot_general | solution.py:248
  54.9 2.8 %iota_compare_fusion.10 = pred[2,9,128,1024]{2,3,1,0:T(32,128)(4,1)} fusion(s32[2,9,128]{2,1,0:T(8,128)S(1)} %copy.9), kind=kLoop, calls=%fused_computation.12 | loop fusion | flops 2359296 | bytes 2368512 | tf_op jit(solution)/shard_map/eq | solution.py:209
  57.7 0.0 collective-permute-done.2
  57.7 0.0 copy-done.4
  57.7 3.9 %fusion.20 = f32[36,256,256]{2,1,0:T(8,128)} fusion(f32[26,256,256]{2,1,0:T(8,128)} %fusion.16, bf16[9,128,256]{2,1,0:T(8,128)(2,1)} %collective-permute-done.2, bf16[2,9,128,256]{3,2,1,0:T(8,128)(2,1)S(1)} %copy-done.4), kind=kOutput, calls=%fused_computation.28 | convolution fusion | flops 151584768 | bytes 5898240 | tf_op jit(solution)/shard_map/fbc,fbd->fcd/dot_general | solution.py:223
  61.6 0.0 copy-done
  61.6 1.1 slice_dynamic-update-slice_fusion.1
  62.7 0.0 copy-done.6
  62.7 0.0 copy-done.11
  62.7 1.0 fusion.40
  63.7 1.0 slice_dynamic-update-slice_fusion
  64.8 0.0 collective-permute-done.3
  64.8 3.0 %fusion.19 = f32[36,256,256]{2,1,0:T(8,128)} fusion(f32[36,256,256]{2,1,0:T(8,128)} %slice_dynamic-update-slice_fusion, f32[26,256,256]{2,1,0:T(8,128)S(1)} %copy-done, bf16[9,128,256]{2,1,0:T(8,128)(2,1)} %collective-permute-done.3, bf16[2,9,128,256]{3,2,1,0:T(8,128)(2,1)S(1)} %copy-done.4), kind=kOutput, calls=%fused_computation.26 | convolution fusion | flops 151584768 | bytes 5898240 | tf_op jit(solution)/shard_map/fbc,fbd->fcd/dot_general | solution.py:223
  67.8 1.7 broadcast_dynamic-update-slice_fusion
  69.5 89.8 %shard_map.86 = f32[9216,256]{1,0:T(8,128)} custom-call(f32[9216,256]{1,0:T(8,128)} %bitcast.23.x_ref), custom_call_target="tpu_custom_call" | custom-call | tf_op jit(solution)/shard_map/pallas_call | solution.py:158
  159.3 0.0 copy-start.2
  159.3 6.6 %slice.63 = f32[6912,256]{1,0:T(8,128)} slice(f32[9216,256]{1,0:T(8,128)} %shard_map.86), slice={[0:6912], [0:256]} | slice | bytes 14155776 | tf_op jit(solution)/shard_map/slice | solution.py:186
  165.8 0.0 collective-permute-done.1
  165.8 0.0 copy-done.2
  165.9 2.3 %fusion.23 = f32[1024,256]{1,0:T(8,128)S(1)} fusion(bf16[9,128,256]{2,1,0:T(8,128)(2,1)} %collective-permute-done.1, pred[2,9,128,1024]{2,3,1,0:T(32,128)(4,1)S(1)} %copy-done.2), kind=kOutput, calls=%fused_computation.32 | convolution fusion | flops 603979776 | bytes 2818048 | tf_op jit(solution)/shard_map/fbv,fbc->vc/dot_general | solution.py:219
  168.2 0.0 collective-permute-done
  168.2 0.0 copy-done.12
  168.2 3.1 %fusion.37 = bf16[1,1024,256]{2,1,0:T(8,128)(2,1)} fusion(f32[1024,256]{1,0:T(8,128)S(1)} %fusion.23, f32[1024,256]{1,0:T(8,128)S(1)} %copy-done.12, bf16[9,128,256]{2,1,0:T(8,128)(2,1)} %collective-permute-done, pred[2,9,128,1024]{2,3,1,0:T(32,128)(4,1)S(1)} %copy-done.2), kind=kOutput, calls=%fused_computation.40 | convolution fusion | flops 604766208 | bytes 4390912 | tf_op jit(solution)/shard_map/fbv,fbc->vc/dot_general | solution.py:219
  (11 shorter events, 0.0 us)
Async XLA Ops:
  1.3 3.2 %copy-start.1 = (bf16[27,256,256]{2,1,0:T(8,128)(2,1)S(1)}, bf16[27,256,256]{2,1,0:T(8,128)(2,1)}, u32[]{:S(2)}) copy-start(bf16[27,256,256]{2,1,0:T(8,128)(2,1)} %param.9) | copy-start | bytes 10616836
  4.5 4.7 %copy-start.3 = (bf16[2,9,128,256]{3,2,1,0:T(8,128)(2,1)}, bf16[2,9,128,256]{3,2,1,0:T(8,128)(2,1)S(1)}, u32[]{:S(2)}) copy-start(bf16[2,9,128,256]{3,2,1,0:T(8,128)(2,1)S(1)} %fusion.21) | copy-start | bytes 3538948
  4.6 9.6 %copy-start.9 = (s32[1,1,2,9,128]{4,2,3,1,0:T(2,128)S(1)}, s32[1,1,2,9,128]{4,2,3,1,0:T(2,128)}, u32[]{:S(2)}) copy-start(s32[1,1,2,9,128]{4,2,3,1,0:T(2,128)} %param.13) | copy-start | bytes 27652
  4.6 9.6 %copy-start.10 = (bf16[1,1024,256]{2,1,0:T(8,128)(2,1)S(1)}, bf16[1,1024,256]{2,1,0:T(8,128)(2,1)}, u32[]{:S(2)}) copy-start(bf16[1,1024,256]{2,1,0:T(8,128)(2,1)} %param.7) | copy-start | bytes 1572868
  5.9 162.2 %collective-permute-start = (bf16[9,128,256]{2,1,0:T(8,128)(2,1)}, bf16[9,128,256]{2,1,0:T(8,128)(2,1)}, u32[]{:S(2)}, u32[]{:S(2)}) collective-permute-start(bf16[9,128,256]{2,1,0:T(8,128)(2,1)} %convolution_convert_fusion.2), channel_id=1, source_target_pairs={{1,0},{2,1},{3,2},{4,3},{5,4},{6,5},{7,6},{8,7},{9,8},{10,9},{11,1... | collective-permute-start | bytes 1769480 | tf_op jit(solution)/shard_map/ppermute | solution.py:192
  10.6 155.2 %collective-permute-start.1 = (bf16[9,128,256]{2,1,0:T(8,128)(2,1)}, bf16[9,128,256]{2,1,0:T(8,128)(2,1)}, u32[]{:S(2)}, u32[]{:S(2)}) collective-permute-start(bf16[9,128,256]{2,1,0:T(8,128)(2,1)} %convolution_convert_fusion.1), channel_id=1, source_target_pairs={{0,1},{1,2},{2,3},{3,4},{4,5},{5,6},{6,7},{7,8},{8,9},{9,10},{10,1... | collective-permute-start | bytes 1769480 | tf_op jit(solution)/shard_map/ppermute | solution.py:192
  14.2 9.5 %copy-start.5 = (bf16[1,1024,256]{2,1,0:T(8,128)(2,1)S(1)}, bf16[1,1024,256]{2,1,0:T(8,128)(2,1)}, u32[]{:S(2)}) copy-start(bf16[1,1024,256]{2,1,0:T(8,128)(2,1)} %param.8) | copy-start | bytes 1572868
  18.0 46.8 %collective-permute-start.3 = (bf16[9,128,256]{2,1,0:T(8,128)(2,1)}, bf16[9,128,256]{2,1,0:T(8,128)(2,1)}, u32[]{:S(2)}, u32[]{:S(2)}) collective-permute-start(bf16[9,128,256]{2,1,0:T(8,128)(2,1)} %get-tuple-element.4), channel_id=1, source_target_pairs={{1,0},{2,1},{3,2},{4,3},{5,4},{6,5},{7,6},{8,7},{9,8},{10,9},{11,1... | collective-permute-start | bytes 1769480 | tf_op jit(solution)/shard_map/ppermute | solution.py:192
  19.9 37.8 %collective-permute-start.2 = (bf16[9,128,256]{2,1,0:T(8,128)(2,1)}, bf16[9,128,256]{2,1,0:T(8,128)(2,1)}, u32[]{:S(2)}, u32[]{:S(2)}) collective-permute-start(bf16[9,128,256]{2,1,0:T(8,128)(2,1)} %get-tuple-element.5), channel_id=1, source_target_pairs={{0,1},{1,2},{2,3},{3,4},{4,5},{5,6},{6,7},{7,8},{8,9},{9,10},{10,1... | collective-permute-start | bytes 1769480 | tf_op jit(solution)/shard_map/ppermute | solution.py:192
  25.1 0.7 copy-start.7
  25.1 0.8 copy-start.8
  44.5 13.2 %copy-start.4 = (bf16[2,9,128,256]{3,2,1,0:T(8,128)(2,1)S(1)}, bf16[2,9,128,256]{3,2,1,0:T(8,128)(2,1)}, u32[]{:S(2)}) copy-start(bf16[2,9,128,256]{3,2,1,0:T(8,128)(2,1)} %copy-done.3) | copy-start | bytes 3538948
  54.9 6.7 %copy-start = (f32[26,256,256]{2,1,0:T(8,128)S(1)}, f32[26,256,256]{2,1,0:T(8,128)}, u32[]{:S(2)}) copy-start(f32[26,256,256]{2,1,0:T(8,128)} %fusion.16) | copy-start | bytes 20447236
  57.7 5.0 %copy-start.6 = (bf16[1,1024,256]{2,1,0:T(8,128)(2,1)S(1)}, bf16[1,1024,256]{2,1,0:T(8,128)(2,1)}, u32[]{:S(2)}) copy-start(bf16[1,1024,256]{2,1,0:T(8,128)(2,1)} %param.8) | copy-start | bytes 1572868
  57.7 5.0 %copy-start.11 = (bf16[1,1024,256]{2,1,0:T(8,128)(2,1)S(1)}, bf16[1,1024,256]{2,1,0:T(8,128)(2,1)}, u32[]{:S(2)}) copy-start(bf16[1,1024,256]{2,1,0:T(8,128)(2,1)} %param.7) | copy-start | bytes 1572868
  159.3 6.6 %copy-start.2 = (pred[2,9,128,1024]{2,3,1,0:T(32,128)(4,1)S(1)}, pred[2,9,128,1024]{2,3,1,0:T(32,128)(4,1)}, u32[]{:S(2)}) copy-start(pred[2,9,128,1024]{2,3,1,0:T(32,128)(4,1)} %iota_compare_fusion.10) | copy-start | bytes 7077892
  165.8 2.3 %copy-start.12 = (f32[1024,256]{1,0:T(8,128)S(1)}, f32[1024,256]{1,0:T(8,128)}, u32[]{:S(2)}) copy-start(f32[1024,256]{1,0:T(8,128)} %fusion.29) | copy-start | bytes 3145732

commit v3 on v2

--- a/solution.py
+++ b/solution.py
@@ -254,15 +254,12 @@
     face_in_table = one_hot_rows(bnd_in[0, 0], rows_here)
     own_grads = pick_rows(face_out_table, own_grad)
     asked = pick_rows(face_in_table, own_feat)
-    fetched = [None, None]
-    for face_side in range(2):
-        fetched[1 - face_side] = passed_along(asked[face_side], "region", 2 * face_side - 1)
-    low_grad, low_rows = face_products(fetched[0], own_grads[0], low_kernels)
-    high_grad, high_rows = face_products(fetched[1], own_grads[1], high_kernels)
-    outgoing = [low_rows, high_rows]
-    for face_side in range(2):
-        arrived = passed_along(outgoing[face_side], "region", 2 * face_side - 1)
-        accumulated = accumulated + place_rows(face_in_table[1 - face_side], arrived)
+    from_below = passed_along(own_grads[1], "region", 1)
+    from_above = passed_along(own_grads[0], "region", -1)
+    high_grad, below_rows = face_products(asked[0], from_below, high_kernels)
+    low_grad, above_rows = face_products(asked[1], from_above, low_kernels)
+    accumulated = accumulated + place_rows(face_in_table[0], below_rows)
+    accumulated = accumulated + place_rows(face_in_table[1], above_rows)
     stacked = jnp.concatenate(
         [
             offset_grads[0:9] + low_grad,

time: 172 us -> 167 us (0.971)
  starting transfers between devices: 12.6 us -> 6.83 us
  Pallas kernels: 89.8 us -> 87.2 us
  matrix products: 52.3 us -> 54.6 us
  local copies, waits for them, and re-layouts: 13 us -> 14.9 us
    ppermute x4 -> x2, starting transfers between devices: 12.6 us -> 6.83 us  [passed_along(): return lax.ppermute(array, axis, pairs)]
    dot_general x2 -> x0, matrix products: 2.74 us -> none  [face_products(): jnp.einsum('fbd,fcd->fbc', grads, kernels, preferred_element_type=jnp.flo...]
    pallas_call x1, Pallas kernels: 89.8 us -> 87.2 us  [summed_everywhere(): pl.pallas_call(functools.partial(allreduce_kernel, scale), out_shape=jax....]
    dot_general x2, matrix products: 5.43 us -> 7.33 us  [place_rows(): jnp.einsum('fbv,fbc->vc', table, rows, preferred_element_type=jnp.float32)]
    slice x1, local copies, waits for them, and re-layouts: 0.22 us -> 2.08 us  [per_device(): side_kernels = jnp.concatenate([weight[0:13], weight[14:27]], 0)]
  transfers between devices with their start and end apart: 4 -> 2, of which waited for: 0 -> 0; matrix products, arithmetic and copies ran while one was open for 35% -> 21% of each run, Pallas kernels for 52% -> 0%
where the time goes in v3:
time: 167 us
  Pallas kernels  87.2 us (52%)
  matrix products  54.6 us (33%)
  local copies, waits for them, and re-layouts  14.9 us (9%)
  starting transfers between devices  6.83 us (4%)
  other arithmetic  2.81 us (2%)
    pallas_call x1, Pallas kernels, summed_everywhere(): pl.pallas_call(functools.partial(allreduce_kernel, scale), out_shape=jax....  87.2 us
    dot_general x3, matrix products, pick_rows(): jnp.einsum('...v,vc->...c', table, source, preferred_element_type=jnp.flo...  13.3 us
    dot_general x1, matrix products, per_device(): jnp.einsum('vkd,kcd->vc', placed, side_kernels, preferred_element_type=jn...  13.1 us
    dot_general x1, matrix products, per_device(): jnp.einsum('kpc,kpd->kcd', gathered_x, gathered_g, preferred_element_type...  10.3 us
    dot_general x2, matrix products, place_rows(): jnp.einsum('fbv,fbc->vc', table, rows, preferred_element_type=jnp.float32)  7.33 us
    dot_general x2, matrix products, face_products(): jnp.einsum('fbc,fbd->fcd', features, grads, preferred_element_type=jnp.fl...  6.93 us
    ppermute x2, starting transfers between devices, passed_along(): return lax.ppermute(array, axis, pairs)  6.83 us
    slice x1, local copies, waits for them, and re-layouts, summed_everywhere(): return total[:stacked.shape[0] * stacked.shape[1]].reshape(stacked.shape)  6.59 us
  transfers between devices with their start and end apart: 2, of which 0 were waited for; matrix products, arithmetic and copies ran while one was open for 21% of the time, Pallas kernels for 0%

profile of v3, /device:TPU:1, one launch (start us, length us, event | category | flops | bytes accessed | tf_op | source)
XLA Modules:
  0.0 167.1 jit_solution(13556315003864876489)
XLA Ops:
  0.6 0.7 copy.10
  1.3 0.0 copy-start.8
  1.3 0.0 copy-start.6
  1.3 0.0 copy-start.7
  1.3 0.0 copy-start.4
  1.3 3.1 %fusion.21 = bf16[2,9,128,256]{3,2,1,0:T(8,128)(2,1)S(1)} fusion(s32[2,9,128]{2,1,0:T(8,128)S(1)} %copy.10, bf16[1,1024,256]{2,1,0:T(8,128)(2,1)} %param.8), kind=kOutput, calls=%fused_computation.30 | convolution fusion | flops 1210908672 | bytes 1713152 | tf_op jit(solution)/shard_map/...v,vc->...c/dot_general | solution.py:213
  4.5 1.1 slice_bitcast_fusion.13
  5.6 4.9 %collective-permute-start = (bf16[9,128,256]{2,1,0:T(8,128)(2,1)}, bf16[9,128,256]{2,1,0:T(8,128)(2,1)}, u32[]{:S(2)}, u32[]{:S(2)}) collective-permute-start(bf16[9,128,256]{2,1,0:T(8,128)(2,1)} %get-tuple-element.4), channel_id=1, source_target_pairs={{0,1},{1,2},{2,3},{3,4},{4,5},{5,6},{6,7},{7,8},{8,9},{9,10},{10,1... | collective-permute-start | bytes 1769480 | tf_op jit(solution)/shard_map/ppermute | solution.py:192
  10.5 1.9 %collective-permute-start.1 = (bf16[9,128,256]{2,1,0:T(8,128)(2,1)}, bf16[9,128,256]{2,1,0:T(8,128)(2,1)}, u32[]{:S(2)}, u32[]{:S(2)}) collective-permute-start(bf16[9,128,256]{2,1,0:T(8,128)(2,1)} %get-tuple-element.5), channel_id=1, source_target_pairs={{1,0},{2,1},{3,2},{4,3},{5,4},{6,5},{7,6},{8,7},{9,8},{10,9},{11,1... | collective-permute-start | bytes 1769480 | tf_op jit(solution)/shard_map/ppermute | solution.py:192
  12.4 0.0 copy-done.8
  12.4 0.0 copy-done.6
  12.5 0.6 copy.23
  13.1 0.0 copy-done.7
  13.1 0.0 copy-done.4
  13.1 0.0 copy-start.1
  13.1 6.5 %fusion.18 = bf16[26,256,256]{2,1,0:T(8,128)(2,1)} fusion(s32[26,256]{1,0:T(8,128)S(1)} %bitcast.106, bf16[1,1024,256]{2,1,0:T(8,128)(2,1)S(1)} %copy-done.4), kind=kOutput, calls=%fused_computation.24 | convolution fusion | flops 3498180608 | bytes 3958784 | tf_op jit(solution)/shard_map/...v,vc->...c/dot_general | solution.py:213
  19.6 0.0 copy-done.1
  19.6 0.0 copy-start.9
  19.6 2.1 %fusion.71 = (bf16[13,256,256]{2,1,0:T(8,128)(2,1)}, bf16[13,256,256]{2,1,0:T(8,128)(2,1)}) fusion(bf16[27,256,256]{2,1,0:T(8,128)(2,1)S(1)} %copy-done.1), kind=kLoop, calls=%fused_computation.65 | loop fusion | bytes 6815744 | tf_op jit(solution)/shard_map/slice | solution.py:244
  21.7 0.0 copy-done.9
  21.7 3.7 %convolution_convert_fusion = bf16[2,9,128,256]{3,2,1,0:T(8,128)(2,1)} fusion(bf16[1,1024,256]{2,1,0:T(8,128)(2,1)S(1)} %copy-done.9, s32[2,9,128]{2,1,0:T(8,128)S(1)} %copy.9), kind=kOutput, calls=%fused_computation.29 | convolution fusion | flops 1210908672 | bytes 1713152 | tf_op jit(solution)/shard_map/...v,vc->...c/dot_general | solution.py:213
  25.4 10.3 %fusion.16 = f32[26,256,256]{2,1,0:T(8,128)} fusion(bf16[26,256,256]{2,1,0:T(8,128)(2,1)} %fusion.18, s32[26,256]{1,0:T(8,128)} %bitcast.104, bf16[1,1024,256]{2,1,0:T(8,128)(2,1)} %param.7), kind=kOutput, calls=%fused_computation.22 | convolution fusion | flops 4370595840 | bytes 10774528 | tf_op jit(solution)/shard_map/kpc,kpd->kcd/dot_general | solution.py:248
  35.7 0.0 copy-start.3
  35.7 2.4 %fusion.66 = f32[1024,256]{1,0:T(8,128)} fusion(bf16[1,1024,256]{2,1,0:T(8,128)(2,1)} %param.8, bf16[27,256,256]{2,1,0:T(8,128)(2,1)S(1)} %copy-done.1), kind=kOutput, calls=%fused_computation.58 | convolution fusion | flops 134217728 | bytes 1703936 | tf_op jit(solution)/shard_map/dot_general | solution.py:202
  38.2 0.0 copy-start
  38.2 2.8 %iota_compare_fusion.10 = pred[2,9,128,1024]{2,3,1,0:T(32,128)(4,1)} fusion(s32[2,9,128]{2,1,0:T(8,128)S(1)} %copy.9), kind=kLoop, calls=%fused_computation.12 | loop fusion | flops 2359296 | bytes 2368512 | tf_op jit(solution)/shard_map/eq | solution.py:209
  41.0 0.0 copy-start.5
  41.0 0.0 copy-start.10
  41.0 0.0 collective-permute-done.1
  41.0 0.0 copy-done.3
  41.0 3.9 %fusion.20 = f32[36,256,256]{2,1,0:T(8,128)} fusion(f32[26,256,256]{2,1,0:T(8,128)} %fusion.16, bf16[9,128,256]{2,1,0:T(8,128)(2,1)} %collective-permute-done.1, bf16[2,9,128,256]{3,2,1,0:T(8,128)(2,1)S(1)} %copy-done.3), kind=kOutput, calls=%fused_computation.28 | convolution fusion | flops 151584768 | bytes 5898240 | tf_op jit(solution)/shard_map/fbc,fbd->fcd/dot_general | solution.py:223
  44.9 0.0 copy-done
  44.9 1.0 slice_dynamic-update-slice_fusion.1
  45.9 0.0 copy-done.5
  45.9 0.0 copy-done.10
  45.9 1.0 fusion.58
  47.0 1.1 slice_dynamic-update-slice_fusion
  48.0 0.0 collective-permute-done
  48.0 3.0 %fusion.19 = f32[36,256,256]{2,1,0:T(8,128)} fusion(f32[36,256,256]{2,1,0:T(8,128)} %slice_dynamic-update-slice_fusion, f32[26,256,256]{2,1,0:T(8,128)S(1)} %copy-done, bf16[9,128,256]{2,1,0:T(8,128)(2,1)} %collective-permute-done, bf16[2,9,128,256]{3,2,1,0:T(8,128)(2,1)S(1)} %copy-done.3), kind=kOutput, calls=%fused_computation.26 | convolution fusion | flops 151584768 | bytes 5898240 | tf_op jit(solution)/shard_map/fbc,fbd->fcd/dot_general | solution.py:223
  51.1 1.7 %broadcast_dynamic-update-slice_fusion = f32[36,256,256]{2,1,0:T(8,128)} fusion(f32[36,256,256]{2,1,0:T(8,128)} %fusion.19), kind=kLoop, calls=%fused_computation.41 | loop fusion | bytes 2359296 | tf_op jit(solution)/shard_map/concatenate | solution.py:153
  52.8 87.2 %shard_map.86 = f32[9216,256]{1,0:T(8,128)} custom-call(f32[9216,256]{1,0:T(8,128)} %bitcast.23.x_ref), custom_call_target="tpu_custom_call" | custom-call | tf_op jit(solution)/shard_map/pallas_call | solution.py:158
  140.0 0.0 copy-start.2
  140.0 6.6 %slice.63 = f32[6912,256]{1,0:T(8,128)} slice(f32[9216,256]{1,0:T(8,128)} %shard_map.86), slice={[0:6912], [0:256]} | slice | bytes 14155776 | tf_op jit(solution)/shard_map/slice | solution.py:186
  146.6 0.0 copy-done.2
  146.6 3.7 %fusion.23 = f32[1024,256]{1,0:T(8,128)} fusion(pred[2,9,128,1024]{2,3,1,0:T(32,128)(4,1)} %iota_compare_fusion.10, bf16[9,128,256]{2,1,0:T(8,128)(2,1)} %collective-permute-done.1, bf16[27,256,256]{2,1,0:T(8,128)(2,1)S(1)} %copy-done.2), kind=kOutput, calls=%fused_computation.32 | convolution fusion | flops 755269632 | bytes 3997696 | tf_op jit(solution)/shard_map/fbv,fbc->vc/dot_general | solution.py:219
  150.3 3.7 %fusion.22 = f32[1024,256]{1,0:T(8,128)} fusion(pred[2,9,128,1024]{2,3,1,0:T(32,128)(4,1)} %iota_compare_fusion.10, bf16[9,128,256]{2,1,0:T(8,128)(2,1)} %collective-permute-done, bf16[27,256,256]{2,1,0:T(8,128)(2,1)S(1)} %copy-done.2), kind=kOutput, calls=%fused_computation.31 | convolution fusion | flops 755269632 | bytes 3997696 | tf_op jit(solution)/shard_map/fbv,fbc->vc/dot_general | solution.py:219
  153.9 13.1 %fusion.49 = bf16[1,1024,256]{2,1,0:T(8,128)(2,1)} fusion(f32[1024,256]{1,0:T(8,128)} %fusion.23, f32[1024,256]{1,0:T(8,128)} %fusion.22, f32[1024,256]{1,0:T(8,128)} %fusion.66, bf16[13,256,256]{2,1,0:T(8,128)(2,1)} %get-tuple-element.3, bf16[13,256,256]{2,1,0:T(8,128)(2,1)} %get-tuple-element.2, bf16[26,256,256]{2,1,0:T(8,128)(2,1)} %fusion.18, ...), kind=kOutput, calls=%fused_computation.40 | convolution fusion | flops 6995705856 | bytes 10512384 | tf_op jit(solution)/shard_map/vkd,kcd->vc/dot_general | solution.py:245
  (2 shorter events, 0.0 us)
Async XLA Ops:
  1.3 11.1 %copy-start.8 = (s32[1,1,2,9,128]{4,2,3,1,0:T(2,128)S(1)}, s32[1,1,2,9,128]{4,2,3,1,0:T(2,128)}, u32[]{:S(2)}) copy-start(s32[1,1,2,9,128]{4,2,3,1,0:T(2,128)} %param.13) | copy-start | bytes 27652
  1.3 11.1 %copy-start.6 = (s32[1,1,26,256]{3,1,2,0:T(1,128)S(1)}, s32[1,1,26,256]{3,1,2,0:T(1,128)}, u32[]{:S(2)}) copy-start(s32[1,1,26,256]{3,1,2,0:T(1,128)} %param.10) | copy-start | bytes 79876
  1.3 11.7 %copy-start.7 = (s32[1,1,26,256]{3,1,2,0:T(1,128)S(1)}, s32[1,1,26,256]{3,1,2,0:T(1,128)}, u32[]{:S(2)}) copy-start(s32[1,1,26,256]{3,1,2,0:T(1,128)} %param.11) | copy-start | bytes 79876
  1.3 11.7 %copy-start.4 = (bf16[1,1024,256]{2,1,0:T(8,128)(2,1)S(1)}, bf16[1,1024,256]{2,1,0:T(8,128)(2,1)}, u32[]{:S(2)}) copy-start(bf16[1,1024,256]{2,1,0:T(8,128)(2,1)} %param.8) | copy-start | bytes 1572868
  5.6 42.5 %collective-permute-start = (bf16[9,128,256]{2,1,0:T(8,128)(2,1)}, bf16[9,128,256]{2,1,0:T(8,128)(2,1)}, u32[]{:S(2)}, u32[]{:S(2)}) collective-permute-start(bf16[9,128,256]{2,1,0:T(8,128)(2,1)} %get-tuple-element.4), channel_id=1, source_target_pairs={{0,1},{1,2},{2,3},{3,4},{4,5},{5,6},{6,7},{7,8},{8,9},{9,10},{10,1... | collective-permute-start | bytes 1769480 | tf_op jit(solution)/shard_map/ppermute | solution.py:192
  10.5 30.5 %collective-permute-start.1 = (bf16[9,128,256]{2,1,0:T(8,128)(2,1)}, bf16[9,128,256]{2,1,0:T(8,128)(2,1)}, u32[]{:S(2)}, u32[]{:S(2)}) collective-permute-start(bf16[9,128,256]{2,1,0:T(8,128)(2,1)} %get-tuple-element.5), channel_id=1, source_target_pairs={{1,0},{2,1},{3,2},{4,3},{5,4},{6,5},{7,6},{8,7},{9,8},{10,9},{11,1... | collective-permute-start | bytes 1769480 | tf_op jit(solution)/shard_map/ppermute | solution.py:192
  13.1 6.6 %copy-start.1 = (bf16[27,256,256]{2,1,0:T(8,128)(2,1)S(1)}, bf16[27,256,256]{2,1,0:T(8,128)(2,1)}, u32[]{:S(2)}) copy-start(bf16[27,256,256]{2,1,0:T(8,128)(2,1)} %param.9) | copy-start | bytes 10616836
  19.6 2.1 %copy-start.9 = (bf16[1,1024,256]{2,1,0:T(8,128)(2,1)S(1)}, bf16[1,1024,256]{2,1,0:T(8,128)(2,1)}, u32[]{:S(2)}) copy-start(bf16[1,1024,256]{2,1,0:T(8,128)(2,1)} %param.7) | copy-start | bytes 1572868
  35.7 5.3 %copy-start.3 = (bf16[2,9,128,256]{3,2,1,0:T(8,128)(2,1)S(1)}, bf16[2,9,128,256]{3,2,1,0:T(8,128)(2,1)}, u32[]{:S(2)}) copy-start(bf16[2,9,128,256]{3,2,1,0:T(8,128)(2,1)} %convolution_convert_fusion) | copy-start | bytes 3538948
  38.2 6.7 %copy-start = (f32[26,256,256]{2,1,0:T(8,128)S(1)}, f32[26,256,256]{2,1,0:T(8,128)}, u32[]{:S(2)}) copy-start(f32[26,256,256]{2,1,0:T(8,128)} %fusion.16) | copy-start | bytes 20447236
  41.0 5.0 %copy-start.5 = (bf16[1,1024,256]{2,1,0:T(8,128)(2,1)S(1)}, bf16[1,1024,256]{2,1,0:T(8,128)(2,1)}, u32[]{:S(2)}) copy-start(bf16[1,1024,256]{2,1,0:T(8,128)(2,1)} %param.8) | copy-start | bytes 1572868
  41.0 5.0 %copy-start.10 = (bf16[1,1024,256]{2,1,0:T(8,128)(2,1)S(1)}, bf16[1,1024,256]{2,1,0:T(8,128)(2,1)}, u32[]{:S(2)}) copy-start(bf16[1,1024,256]{2,1,0:T(8,128)(2,1)} %param.7) | copy-start | bytes 1572868
  140.0 6.6 %copy-start.2 = (bf16[27,256,256]{2,1,0:T(8,128)(2,1)S(1)}, bf16[27,256,256]{2,1,0:T(8,128)(2,1)}, u32[]{:S(2)}) copy-start(bf16[27,256,256]{2,1,0:T(8,128)(2,1)} %param.9) | copy-start | bytes 10616836

commit v4 on v3

--- a/solution.py
+++ b/solution.py
@@ -209,10 +209,10 @@
     return (lists[..., None] == numbers).astype(jnp.bfloat16)
 
 
-def pick_rows(table, source):
-    return jnp.einsum("...v,vc->...c", table, source, preferred_element_type=jnp.float32).astype(
-        jnp.bfloat16
-    )
+def take_rows(source, lists):
+    padded = jnp.concatenate([source, jnp.zeros((1,) + source.shape[1:], source.dtype)], 0)
+    picked = jnp.take(padded, lists.reshape(-1), axis=0, mode="clip")
+    return picked.reshape(lists.shape + source.shape[1:])
 
 
 def place_rows(table, rows):
@@ -235,9 +235,8 @@
     center = contract_rows(own_feat, own_grad)
     accumulated = through_kernel(own_grad, weight[13])
     table_in = one_hot_rows(loc_in[0, 0], rows_here)
-    table_out = one_hot_rows(loc_out[0, 0], rows_here)
-    gathered_x = pick_rows(table_in, own_feat)
-    gathered_g = pick_rows(table_out, own_grad)
+    gathered_x = take_rows(own_feat, loc_in[0, 0])
+    gathered_g = take_rows(own_grad, loc_out[0, 0])
     placed = jnp.einsum(
         "kpv,kpc->vkc", table_in, gathered_g, preferred_element_type=jnp.float32
     ).astype(jnp.bfloat16)
@@ -250,10 +249,9 @@
     )
     low_kernels = weight[0:9]
     high_kernels = weight[18:27]
-    face_out_table = one_hot_rows(bnd_out[0, 0], rows_here)
     face_in_table = one_hot_rows(bnd_in[0, 0], rows_here)
-    own_grads = pick_rows(face_out_table, own_grad)
-    asked = pick_rows(face_in_table, own_feat)
+    own_grads = take_rows(own_grad, bnd_out[0, 0])
+    asked = take_rows(own_feat, bnd_in[0, 0])
     from_below = passed_along(own_grads[1], "region", 1)
     from_above = passed_along(own_grads[0], "region", -1)
     high_grad, below_rows = face_products(asked[0], from_below, high_kernels)

time: 167 us -> 204 us (1.22)
  local copies, waits for them, and re-layouts: 14.9 us -> 69.1 us
  matrix products: 54.6 us -> 34.6 us
    gather x0 -> x4, local copies, waits for them, and re-layouts: none -> 52.3 us  [take_rows(): picked = jnp.take(padded, lists.reshape(-1), axis=0, mode='clip')]
    dot_general x3 -> x0, matrix products: 13.3 us -> none  [pick_rows(): jnp.einsum('...v,vc->...c', table, source, preferred_element_type=jnp.flo...]
    dot_general x1, matrix products: 10.3 us -> 4.1 us  [per_device(): jnp.einsum('kpc,kpd->kcd', gathered_x, gathered_g, preferred_element_type...]
    unnamed x26 -> x27, local copies, waits for them, and re-layouts: 2.76 us -> 4.2 us
  transfers between devices with their start and end apart: 2 -> 2, of which waited for: 0 -> 0; matrix products, arithmetic and copies ran while one was open for 21% -> 32% of each run, Pallas kernels for 0% -> 0%
where the time goes in v4:
time: 204 us; the launch traced here: 202 us
  Pallas kernels  87.6 us (43%)
  local copies, waits for them, and re-layouts  69.1 us (34%)
  matrix products  34.6 us (17%)
  starting transfers between devices  6.97 us (3%)
  other arithmetic  2.97 us (1%)
    pallas_call x1, Pallas kernels, summed_everywhere(): pl.pallas_call(functools.partial(allreduce_kernel, scale), out_shape=jax....  87.6 us
    gather x4, local copies, waits for them, and re-layouts, take_rows(): picked = jnp.take(padded, lists.reshape(-1), axis=0, mode='clip')  52.3 us
    dot_general x1, matrix products, per_device(): jnp.einsum('vkd,kcd->vc', placed, side_kernels, preferred_element_type=jn...  12.8 us
    dot_general x2, matrix products, place_rows(): jnp.einsum('fbv,fbc->vc', table, rows, preferred_element_type=jnp.float32)  8.3 us
    ppermute x2, starting transfers between devices, passed_along(): return lax.ppermute(array, axis, pairs)  6.97 us
    slice x1, local copies, waits for them, and re-layouts, summed_everywhere(): return total[:stacked.shape[0] * stacked.shape[1]].reshape(stacked.shape)  6.58 us
    dot_general x2, matrix products, face_products(): jnp.einsum('fbc,fbd->fcd', features, grads, preferred_element_type=jnp.fl...  6.12 us
    unnamed x27, local copies, waits for them, and re-layouts  4.2 us
  transfers between devices with their start and end apart: 2, of which 0 were waited for; matrix products, arithmetic and copies ran while one was open for 32% of the time, Pallas kernels for 0%

profile of v4, /device:TPU:1, one launch (start us, length us, event | category | flops | bytes accessed | tf_op | source)
XLA Modules:
  0.0 202.1 jit_solution(11083406672391462456)
XLA Ops:
  0.6 0.7 copy.12
  1.3 0.7 copy.14
  2.1 1.1 concatenate.14
  3.1 0.0 copy-start.3
  3.2 6.9 %gather_fusion.1 = bf16[2304,256]{1,0:T(8,128)(2,1)S(1)} fusion(bf16[1025,256]{1,0:T(8,128)(2,1)S(1)} %concatenate.14, s32[3072]{0:T(1024)S(1)} %get-tuple-element.9), kind=kCustom, calls=%fused_computation.1 | custom fusion | bytes 2368512 | tf_op jit(solution)/shard_map/jit(_take)/gather | solution.py:214
  10.0 0.0 copy-start.1
  10.0 1.1 fusion.58
  11.1 3.4 %collective-permute-start.1 = (bf16[9,128,256]{2,1,0:T(8,128)(2,1)}, bf16[9,128,256]{2,1,0:T(8,128)(2,1)}, u32[]{:S(2)}, u32[]{:S(2)}) collective-permute-start(bf16[9,128,256]{2,1,0:T(8,128)(2,1)} %bitcast.10), channel_id=1, source_target_pairs={{1,0},{2,1},{3,2},{4,3},{5,4},{6,5},{7,6},{8,7},{9,8},{10,9},{11,1... | collective-permute-start | bytes 1769480 | tf_op jit(solution)/shard_map/ppermute | solution.py:192
  14.6 3.6 %collective-permute-start = (bf16[9,128,256]{2,1,0:T(8,128)(2,1)}, bf16[9,128,256]{2,1,0:T(8,128)(2,1)}, u32[]{:S(2)}, u32[]{:S(2)}) collective-permute-start(bf16[9,128,256]{2,1,0:T(8,128)(2,1)} %bitcast.7), channel_id=1, source_target_pairs={{0,1},{1,2},{2,3},{3,4},{4,5},{5,6},{6,7},{7,8},{8,9},{9,10},{10,1... | collective-permute-start | bytes 1769480 | tf_op jit(solution)/shard_map/ppermute | solution.py:192
  18.1 0.0 copy-done.3
  18.1 2.2 %fusion.49 = f32[1024,256]{1,0:T(8,128)} fusion(bf16[27,256,256]{2,1,0:T(8,128)(2,1)} %param.9, bf16[1,1024,256]{2,1,0:T(8,128)(2,1)S(1)} %copy-done.3), kind=kOutput, calls=%fused_computation.39 | convolution fusion | flops 134217728 | bytes 1703936 | tf_op jit(solution)/shard_map/dot_general | solution.py:202
  20.3 0.0 copy-done.1
  20.3 0.0 copy-start.5
  20.4 2.1 %fusion.56 = (bf16[13,256,256]{2,1,0:T(8,128)(2,1)}, bf16[13,256,256]{2,1,0:T(8,128)(2,1)}) fusion(bf16[27,256,256]{2,1,0:T(8,128)(2,1)S(1)} %copy-done.1), kind=kLoop, calls=%fused_computation.51 | loop fusion | bytes 6815744 | tf_op jit(solution)/shard_map/slice | solution.py:243
  22.4 0.0 copy-done.8
  22.4 0.0 copy-done.10
  22.4 0.1 reduce
  22.5 0.0 copy-done.7
  22.6 0.1 reduce.1
  22.6 0.0 copy-done.5
  22.7 6.9 %gather_fusion.3 = bf16[2304,256]{1,0:T(8,128)(2,1)S(1)} fusion(bf16[1025,256]{1,0:T(8,128)(2,1)S(1)} %concatenate.16, s32[3072]{0:T(1024)S(1)} %get-tuple-element.8), kind=kCustom, calls=%fused_computation.3 | custom fusion | bytes 2368512 | tf_op jit(solution)/shard_map/jit(_take)/gather | solution.py:214
  29.6 0.1 fusion.57
  29.7 2.8 %iota_compare_fusion.6 = pred[2,9,128,1024]{2,3,1,0:T(32,128)(4,1)} fusion(s32[2,9,128]{2,1,0:T(8,128)S(1)} %copy.11), kind=kLoop, calls=%fused_computation.10 | loop fusion | flops 2359296 | bytes 2368512 | tf_op jit(solution)/shard_map/eq | solution.py:209
  32.5 0.6 copy.22
  33.1 19.3 %gather_fusion = bf16[6656,256]{1,0:T(8,128)(2,1)} fusion(bf16[1025,256]{1,0:T(8,128)(2,1)S(1)} %concatenate.14, s32[7168]{0:T(1024)S(1)} %pad_clamp_fusion.1), kind=kCustom, calls=%fused_computation | custom fusion | bytes 6842368 | tf_op jit(solution)/shard_map/jit(_take)/gather | solution.py:214
  52.4 19.3 %gather_fusion.2 = bf16[6656,256]{1,0:T(8,128)(2,1)} fusion(bf16[1025,256]{1,0:T(8,128)(2,1)S(1)} %concatenate.16, s32[7168]{0:T(1024)S(1)} %pad_clamp_fusion), kind=kCustom, calls=%fused_computation.2 | custom fusion | bytes 6842368 | tf_op jit(solution)/shard_map/jit(_take)/gather | solution.py:214
  71.6 4.1 %fusion.59 = f32[26,256,256]{2,1,0:T(8,128)S(1)} fusion(bf16[26,256,256]{2,1,0:T(8,128)(2,1)} %bitcast.81, bf16[26,256,256]{2,1,0:T(8,128)(2,1)} %bitcast.79), kind=kOutput, calls=%fused_computation.54 | convolution fusion | flops 872415232 | bytes 13631488 | tf_op jit(solution)/shard_map/kpc,kpd->kcd/dot_general | solution.py:247
  75.7 0.0 collective-permute-done.1
  75.8 0.0 copy-start.4
  75.8 0.0 copy-start.6
  75.8 3.1 %fusion.11 = f32[36,256,256]{2,1,0:T(8,128)} fusion(f32[26,256,256]{2,1,0:T(8,128)S(1)} %fusion.59, bf16[9,128,256]{2,1,0:T(8,128)(2,1)S(1)} %bitcast.84, bf16[9,128,256]{2,1,0:T(8,128)(2,1)} %collective-permute-done.1), kind=kOutput, calls=%fused_computation.21 | convolution fusion | flops 151584768 | bytes 5898240 | tf_op jit(solution)/shard_map/fbc,fbd->fcd/dot_general | solution.py:223
  78.9 1.1 slice_dynamic-update-slice_fusion.1
  79.9 0.0 copy-done.4
  79.9 0.0 copy-done.6
  79.9 1.1 fusion.48
  81.0 1.1 slice_dynamic-update-slice_fusion
  82.1 0.0 collective-permute-done
  82.1 3.0 %fusion.10 = f32[36,256,256]{2,1,0:T(8,128)} fusion(f32[36,256,256]{2,1,0:T(8,128)} %slice_dynamic-update-slice_fusion, f32[26,256,256]{2,1,0:T(8,128)S(1)} %fusion.59, bf16[9,128,256]{2,1,0:T(8,128)(2,1)S(1)} %bitcast.83, bf16[9,128,256]{2,1,0:T(8,128)(2,1)} %collective-permute-done), kind=kOutput, calls=%fused_computation.19 | convolution fusion | flops 151584768 | bytes 5898240 | tf_op jit(solution)/shard_map/fbc,fbd->fcd/dot_general | solution.py:223
  85.1 1.7 broadcast_dynamic-update-slice_fusion
  86.8 87.6 %shard_map.86 = f32[9216,256]{1,0:T(8,128)} custom-call(f32[9216,256]{1,0:T(8,128)} %bitcast.18.x_ref), custom_call_target="tpu_custom_call" | custom-call | tf_op jit(solution)/shard_map/pallas_call | solution.py:158
  174.3 0.0 copy-start.2
  174.4 6.6 %slice.67 = f32[6912,256]{1,0:T(8,128)} slice(f32[9216,256]{1,0:T(8,128)} %shard_map.86), slice={[0:6912], [0:256]} | slice | bytes 14155776 | tf_op jit(solution)/shard_map/slice | solution.py:186
  180.9 0.0 copy-done.2
  180.9 4.1 %fusion.13 = f32[1024,256]{1,0:T(8,128)} fusion(pred[2,9,128,1024]{2,3,1,0:T(32,128)(4,1)S(1)} %copy-done.2, bf16[9,128,256]{2,1,0:T(8,128)(2,1)} %collective-permute-done.1, bf16[27,256,256]{2,1,0:T(8,128)(2,1)} %param.9), kind=kOutput, calls=%fused_computation.23 | convolution fusion | flops 755269632 | bytes 3997696 | tf_op jit(solution)/shard_map/fbv,fbc->vc/dot_general | solution.py:219
  185.0 4.2 %fusion.12 = f32[1024,256]{1,0:T(8,128)} fusion(pred[2,9,128,1024]{2,3,1,0:T(32,128)(4,1)} %iota_compare_fusion.6, bf16[9,128,256]{2,1,0:T(8,128)(2,1)} %collective-permute-done, bf16[27,256,256]{2,1,0:T(8,128)(2,1)} %param.9), kind=kOutput, calls=%fused_computation.22 | convolution fusion | flops 755269632 | bytes 3997696 | tf_op jit(solution)/shard_map/fbv,fbc->vc/dot_general | solution.py:219
  189.2 0.0 copy-done
  189.2 0.0 copy-done.9
  189.2 12.8 %fusion.39 = bf16[1,1024,256]{2,1,0:T(8,128)(2,1)} fusion(f32[1024,256]{1,0:T(8,128)} %fusion.13, f32[1024,256]{1,0:T(8,128)} %fusion.12, f32[1024,256]{1,0:T(8,128)} %fusion.49, bf16[13,256,256]{2,1,0:T(8,128)(2,1)} %get-tuple-element.3, bf16[13,256,256]{2,1,0:T(8,128)(2,1)} %get-tuple-element.2, bf16[26,256,256]{2,1,0:T(8,128)(2,1)S(1)} %bitcast.80, ...), kind=kOutput, calls=%fused_computation.31 | convolution fusion | flops 6995705856 | bytes 10512384 | tf_op jit(solution)/shard_map/vkd,kcd->vc/dot_general | solution.py:244
  (14 shorter events, 0.1 us)
Async XLA Ops:
  3.1 15.0 %copy-start.3 = (bf16[1,1024,256]{2,1,0:T(8,128)(2,1)S(1)}, bf16[1,1024,256]{2,1,0:T(8,128)(2,1)}, u32[]{:S(2)}) copy-start(bf16[1,1024,256]{2,1,0:T(8,128)(2,1)} %param.8) | copy-start | bytes 1572868
  10.0 10.3 %copy-start.1 = (bf16[27,256,256]{2,1,0:T(8,128)(2,1)S(1)}, bf16[27,256,256]{2,1,0:T(8,128)(2,1)}, u32[]{:S(2)}) copy-start(bf16[27,256,256]{2,1,0:T(8,128)(2,1)} %param.9) | copy-start | bytes 10616836
  11.1 64.6 %collective-permute-start.1 = (bf16[9,128,256]{2,1,0:T(8,128)(2,1)}, bf16[9,128,256]{2,1,0:T(8,128)(2,1)}, u32[]{:S(2)}, u32[]{:S(2)}) collective-permute-start(bf16[9,128,256]{2,1,0:T(8,128)(2,1)} %bitcast.10), channel_id=1, source_target_pairs={{1,0},{2,1},{3,2},{4,3},{5,4},{6,5},{7,6},{8,7},{9,8},{10,9},{11,1... | collective-permute-start | bytes 1769480 | tf_op jit(solution)/shard_map/ppermute | solution.py:192
  14.6 67.5 %collective-permute-start = (bf16[9,128,256]{2,1,0:T(8,128)(2,1)}, bf16[9,128,256]{2,1,0:T(8,128)(2,1)}, u32[]{:S(2)}, u32[]{:S(2)}) collective-permute-start(bf16[9,128,256]{2,1,0:T(8,128)(2,1)} %bitcast.7), channel_id=1, source_target_pairs={{0,1},{1,2},{2,3},{3,4},{4,5},{5,6},{6,7},{7,8},{8,9},{9,10},{10,1... | collective-permute-start | bytes 1769480 | tf_op jit(solution)/shard_map/ppermute | solution.py:192
  20.3 2.1 %copy-start.8 = (s32[1,1,2,9,128]{4,2,3,1,0:T(2,128)S(1)}, s32[1,1,2,9,128]{4,2,3,1,0:T(2,128)}, u32[]{:S(2)}) copy-start(s32[1,1,2,9,128]{4,2,3,1,0:T(2,128)} %param.13) | copy-start | bytes 27652
  20.3 2.1 %copy-start.10 = (s32[1,1,26,256]{3,1,2,0:T(1,128)S(1)}, s32[1,1,26,256]{3,1,2,0:T(1,128)}, u32[]{:S(2)}) copy-start(s32[1,1,26,256]{3,1,2,0:T(1,128)} %param.11) | copy-start | bytes 79876
  20.3 2.2 %copy-start.7 = (s32[1,1,26,256]{3,1,2,0:T(1,128)S(1)}, s32[1,1,26,256]{3,1,2,0:T(1,128)}, u32[]{:S(2)}) copy-start(s32[1,1,26,256]{3,1,2,0:T(1,128)} %param.10) | copy-start | bytes 79876
  20.3 2.3 %copy-start.5 = (bf16[1,1024,256]{2,1,0:T(8,128)(2,1)S(1)}, bf16[1,1024,256]{2,1,0:T(8,128)(2,1)}, u32[]{:S(2)}) copy-start(bf16[1,1024,256]{2,1,0:T(8,128)(2,1)} %param.7) | copy-start | bytes 1572868
  75.8 4.2 %copy-start.4 = (bf16[1,1024,256]{2,1,0:T(8,128)(2,1)S(1)}, bf16[1,1024,256]{2,1,0:T(8,128)(2,1)}, u32[]{:S(2)}) copy-start(bf16[1,1024,256]{2,1,0:T(8,128)(2,1)} %param.8) | copy-start | bytes 1572868
  75.8 4.2 %copy-start.6 = (bf16[1,1024,256]{2,1,0:T(8,128)(2,1)S(1)}, bf16[1,1024,256]{2,1,0:T(8,128)(2,1)}, u32[]{:S(2)}) copy-start(bf16[1,1024,256]{2,1,0:T(8,128)(2,1)} %param.7) | copy-start | bytes 1572868
  174.3 6.6 %copy-start.2 = (pred[2,9,128,1024]{2,3,1,0:T(32,128)(4,1)S(1)}, pred[2,9,128,1024]{2,3,1,0:T(32,128)(4,1)}, u32[]{:S(2)}) copy-start(pred[2,9,128,1024]{2,3,1,0:T(32,128)(4,1)} %iota_compare_fusion.6) | copy-start | bytes 7077892
  185.0 4.2 %copy-start = (bf16[6656,256]{1,0:T(8,128)(2,1)S(1)}, bf16[6656,256]{1,0:T(8,128)(2,1)}, u32[]{:S(2)}) copy-start(bf16[6656,256]{1,0:T(8,128)(2,1)} %gather_fusion) | copy-start | bytes 10223620
  185.0 4.2 %copy-start.9 = (s32[1,1,26,256]{3,2,1,0:T(8,128)S(1)}, s32[1,1,26,256]{3,2,1,0:T(8,128)}, u32[]{:S(2)}) copy-start(s32[1,1,26,256]{3,2,1,0:T(8,128)} %copy.22) | copy-start | bytes 79876

commit v5 on v3

--- a/solution.py
+++ b/solution.py
@@ -14,6 +14,13 @@
 CHUNK_ROWS = 24
 COLOR_ROWS = 128 * CHUNK_ROWS
 PAD_OFFSETS = 36
+
+
+REAL_ROWS = 27 * 256
+
+
+def real_chunk(color, lead):
+    return color * COLOR_ROWS + lead * CHUNK_ROWS < REAL_ROWS
 
 
 def coords_here():
@@ -109,9 +116,14 @@
                 a, b, e = ranks[k]
                 pos = pl.multiple_of(k * COLOR_ROWS + (c * 64 + a * 16 + b * 4 + e) * CHUNK_ROWS, 8)
                 red[k] = total * scale
-                put = pltpu.make_async_copy(red.at[k], out_ref.at[pl.ds(pos, blk)], out_sem.at[k])
-                put.start()
-                put.wait()
+                lead = c * 64 + a * 16 + b * 4 + e
+                put = pltpu.make_async_copy(
+                    red.at[k], out_ref.at[pl.ds(jnp.minimum(pos, out_ref.shape[0] - blk), blk)], out_sem.at[k])
+
+                @pl.when(real_chunk(k, lead))
+                def _():
+                    put.start()
+                    put.wait()
 
     sizes = (COLOR_ROWS // 128, COLOR_ROWS // 32, COLOR_ROWS // 8)
     for step, stage in enumerate((2, 1, 0)):
@@ -120,31 +132,46 @@
         for k, order in enumerate(COLOR_ORDERS):
             dim = order[stage]
             a, b, e = ranks[k]
-            lead = (c * 64 + a * 16 + b * 4 + e, c * 64 + a * 16 + b * 4, c * 64 + a * 16)[step]
+
+            def lead_of(a, b, e):
+                return (c * 64 + a * 16 + b * 4 + e, c * 64 + a * 16 + b * 4, c * 64 + a * 16)[step]
+
+            lead = lead_of(a, b, e)
             pos = pl.multiple_of(k * COLOR_ROWS + lead * CHUNK_ROWS, 8)
+            pos = jnp.minimum(pos, out_ref.shape[0] - blk)
             row = []
             for s in (1, 2, 3):
+                moved = [a, b, e]
+                moved[stage] = (moved[stage] + 4 - s) % 4
                 cp = pltpu.make_async_remote_copy(
                     src_ref=out_ref.at[pl.ds(pos, blk)], dst_ref=out_ref.at[pl.ds(pos, blk)],
                     send_sem=ag_send.at[stage, k, s - 1], recv_sem=ag_recv.at[stage, k, s - 1],
                     device_id=peer_of(at, dim, s), device_id_type=MESH_IDS)
-                cp.start()
-                row.append(cp)
+                mine, theirs = real_chunk(k, lead), real_chunk(k, lead_of(*moved))
+                pl.when(mine)(cp.start)
+                row.append((cp, mine, theirs))
             staged.append(row)
         for row in staged:
-            for cp in row:
-                cp.wait()
+            for cp, mine, theirs in row:
+                pl.when(mine)(cp.wait_send)
+                pl.when(theirs)(cp.wait_recv)
     last = []
     for k in range(3):
-        pos = pl.multiple_of(k * COLOR_ROWS + c * half, 8)
+        if k < 2:
+            pos = pl.multiple_of(k * COLOR_ROWS + c * half, 8)
+            size, mine, theirs = half, c >= 0, c >= 0
+        else:
+            pos = k * COLOR_ROWS
+            size, mine, theirs = out_ref.shape[0] - pos, c == 0, c == 1
         cp = pltpu.make_async_remote_copy(
-            src_ref=out_ref.at[pl.ds(pos, half)], dst_ref=out_ref.at[pl.ds(pos, half)],
+            src_ref=out_ref.at[pl.ds(pos, size)], dst_ref=out_ref.at[pl.ds(pos, size)],
             send_sem=agc_send.at[k], recv_sem=agc_recv.at[k],
             device_id=peer_of(at, "core", 1), device_id_type=MESH_IDS)
-        cp.start()
-        last.append(cp)
-    for cp in last:
-        cp.wait()
+        pl.when(mine)(cp.start)
+        last.append((cp, mine, theirs))
+    for cp, mine, theirs in last:
+        pl.when(mine)(cp.wait_send)
+        pl.when(theirs)(cp.wait_recv)
 
 
 def summed_everywhere(stacked, scale):
@@ -157,7 +184,7 @@
     blocks = (COLOR_ROWS // 8, COLOR_ROWS // 32, COLOR_ROWS // 128)
     total = pl.pallas_call(
         functools.partial(allreduce_kernel, scale),
-        out_shape=jax.ShapeDtypeStruct((rows, width), f32),
+        out_shape=jax.ShapeDtypeStruct((REAL_ROWS, width), f32),
         in_specs=[pl.BlockSpec(memory_space=pltpu.VMEM)],
         out_specs=pl.BlockSpec(memory_space=pl.ANY),
         scratch_shapes=[
@@ -183,7 +210,7 @@
             collective_id=0, has_side_effects=True, vmem_limit_bytes=64 * 1024 * 1024
         ),
     )(data)
-    return total[: stacked.shape[0] * stacked.shape[1]].reshape(stacked.shape)
+    return total.reshape(stacked.shape)
 
 
 def passed_along(array, axis, by):

time: 167 us -> 168 us (level)
    unnamed x26 -> x31, local copies, waits for them, and re-layouts: 2.76 us -> 9.5 us
    slice x1 -> x0, local copies, waits for them, and re-layouts: 6.59 us -> none  [summed_everywhere(): return total[:stacked.shape[0] * stacked.shape[1]].reshape(stacked.shape)]
where the time goes in v5:
time: 168 us; the launch traced here: 167 us
  Pallas kernels  86.6 us (52%)
  matrix products  55.2 us (33%)
  local copies, waits for them, and re-layouts  15 us (9%)
  starting transfers between devices  6.83 us (4%)
  other arithmetic  2.89 us (2%)
    pallas_call x1, Pallas kernels, summed_everywhere(): pl.pallas_call(functools.partial(allreduce_kernel, scale), out_shape=jax....  86.6 us
    dot_general x3, matrix products, pick_rows(): jnp.einsum('...v,vc->...c', table, source, preferred_element_type=jnp.flo...  13.4 us
    dot_general x1, matrix products, per_device(): jnp.einsum('vkd,kcd->vc', placed, side_kernels, preferred_element_type=jn...  12.8 us
    dot_general x1, matrix products, per_device(): jnp.einsum('kpc,kpd->kcd', gathered_x, gathered_g, preferred_element_type...  10.3 us
    unnamed x31, local copies, waits for them, and re-layouts  9.5 us
    dot_general x2, matrix products, place_rows(): jnp.einsum('fbv,fbc->vc', table, rows, preferred_element_type=jnp.float32)  8.31 us
    dot_general x2, matrix products, face_products(): jnp.einsum('fbc,fbd->fcd', features, grads, preferred_element_type=jnp.fl...  6.94 us
    ppermute x2, starting transfers between devices, passed_along(): return lax.ppermute(array, axis, pairs)  6.83 us
  transfers between devices with their start and end apart: 2, of which 0 were waited for; matrix products, arithmetic and copies ran while one was open for 21% of the time, Pallas kernels for 0%

profile of v5, /device:TPU:1, one launch (start us, length us, event | category | flops | bytes accessed | tf_op | source)
XLA Modules:
  0.0 167.3 jit_solution(2961527635666131771)
XLA Ops:
  0.6 0.7 copy.10
  1.3 0.0 copy-start.10
  1.3 0.0 copy-start.8
  1.3 0.0 copy-start.9
  1.3 0.0 copy-start.5
  1.3 3.1 %fusion.21 = bf16[2,9,128,256]{3,2,1,0:T(8,128)(2,1)S(1)} fusion(s32[2,9,128]{2,1,0:T(8,128)S(1)} %copy.10, bf16[1,1024,256]{2,1,0:T(8,128)(2,1)} %param.8), kind=kOutput, calls=%fused_computation.30 | convolution fusion | flops 1210908672 | bytes 1713152 | tf_op jit(solution)/shard_map/...v,vc->...c/dot_general | solution.py:240
  4.5 1.1 slice_bitcast_fusion.13
  5.6 4.9 %collective-permute-start = (bf16[9,128,256]{2,1,0:T(8,128)(2,1)}, bf16[9,128,256]{2,1,0:T(8,128)(2,1)}, u32[]{:S(2)}, u32[]{:S(2)}) collective-permute-start(bf16[9,128,256]{2,1,0:T(8,128)(2,1)} %get-tuple-element.4), channel_id=1, source_target_pairs={{0,1},{1,2},{2,3},{3,4},{4,5},{5,6},{6,7},{7,8},{8,9},{9,10},{10,1... | collective-permute-start | bytes 1769480 | tf_op jit(solution)/shard_map/ppermute | solution.py:219
  10.5 1.9 %collective-permute-start.1 = (bf16[9,128,256]{2,1,0:T(8,128)(2,1)}, bf16[9,128,256]{2,1,0:T(8,128)(2,1)}, u32[]{:S(2)}, u32[]{:S(2)}) collective-permute-start(bf16[9,128,256]{2,1,0:T(8,128)(2,1)} %get-tuple-element.5), channel_id=1, source_target_pairs={{1,0},{2,1},{3,2},{4,3},{5,4},{6,5},{7,6},{8,7},{9,8},{10,9},{11,1... | collective-permute-start | bytes 1769480 | tf_op jit(solution)/shard_map/ppermute | solution.py:219
  12.4 0.0 copy-done.10
  12.5 0.0 copy-done.8
  12.5 0.6 copy.23
  13.1 0.0 copy-done.9
  13.1 0.0 copy-done.5
  13.1 0.0 copy-start.1
  13.1 6.6 %fusion.18 = bf16[26,256,256]{2,1,0:T(8,128)(2,1)} fusion(s32[26,256]{1,0:T(8,128)S(1)} %bitcast.106, bf16[1,1024,256]{2,1,0:T(8,128)(2,1)S(1)} %copy-done.5), kind=kOutput, calls=%fused_computation.24 | convolution fusion | flops 3498180608 | bytes 3958784 | tf_op jit(solution)/shard_map/...v,vc->...c/dot_general | solution.py:240
  19.7 0.0 copy-done.1
  19.7 0.0 copy-start.11
  19.7 2.0 %fusion.71 = (bf16[13,256,256]{2,1,0:T(8,128)(2,1)}, bf16[13,256,256]{2,1,0:T(8,128)(2,1)}) fusion(bf16[27,256,256]{2,1,0:T(8,128)(2,1)S(1)} %copy-done.1), kind=kLoop, calls=%fused_computation.65 | loop fusion | bytes 6815744 | tf_op jit(solution)/shard_map/slice | solution.py:271
  21.7 0.0 copy-done.11
  21.7 3.7 %convolution_convert_fusion = bf16[2,9,128,256]{3,2,1,0:T(8,128)(2,1)} fusion(bf16[1,1024,256]{2,1,0:T(8,128)(2,1)S(1)} %copy-done.11, s32[2,9,128]{2,1,0:T(8,128)S(1)} %copy.9), kind=kOutput, calls=%fused_computation.29 | convolution fusion | flops 1210908672 | bytes 1713152 | tf_op jit(solution)/shard_map/...v,vc->...c/dot_general | solution.py:240
  25.4 10.3 %fusion.16 = f32[26,256,256]{2,1,0:T(8,128)} fusion(bf16[26,256,256]{2,1,0:T(8,128)(2,1)} %fusion.18, s32[26,256]{1,0:T(8,128)} %bitcast.104, bf16[1,1024,256]{2,1,0:T(8,128)(2,1)} %param.7), kind=kOutput, calls=%fused_computation.22 | convolution fusion | flops 4370595840 | bytes 10774528 | tf_op jit(solution)/shard_map/kpc,kpd->kcd/dot_general | solution.py:275
  35.7 0.0 copy-start.3
  35.7 2.4 %fusion.66 = f32[1024,256]{1,0:T(8,128)} fusion(bf16[1,1024,256]{2,1,0:T(8,128)(2,1)} %param.8, bf16[27,256,256]{2,1,0:T(8,128)(2,1)S(1)} %copy-done.1), kind=kOutput, calls=%fused_computation.58 | convolution fusion | flops 134217728 | bytes 1703936 | tf_op jit(solution)/shard_map/dot_general | solution.py:229
  38.2 0.0 copy-start
  38.2 2.9 %iota_compare_fusion.10 = pred[2,9,128,1024]{2,3,1,0:T(32,128)(4,1)} fusion(s32[2,9,128]{2,1,0:T(8,128)S(1)} %copy.9), kind=kLoop, calls=%fused_computation.12 | loop fusion | flops 2359296 | bytes 2368512 | tf_op jit(solution)/shard_map/eq | solution.py:236
  41.1 0.0 copy-start.6
  41.1 0.0 collective-permute-done.1
  41.1 0.0 copy-done.3
  41.1 3.9 %fusion.20 = f32[36,256,256]{2,1,0:T(8,128)} fusion(f32[26,256,256]{2,1,0:T(8,128)} %fusion.16, bf16[9,128,256]{2,1,0:T(8,128)(2,1)} %collective-permute-done.1, bf16[2,9,128,256]{3,2,1,0:T(8,128)(2,1)S(1)} %copy-done.3), kind=kOutput, calls=%fused_computation.28 | convolution fusion | flops 151584768 | bytes 5898240 | tf_op jit(solution)/shard_map/fbc,fbd->fcd/dot_general | solution.py:250
  45.0 0.0 copy-done
  45.0 1.1 slice_dynamic-update-slice_fusion.1
  46.0 0.0 copy-done.6
  46.0 0.0 copy-done.12
  46.0 1.0 fusion.58
  47.1 1.0 slice_dynamic-update-slice_fusion
  48.1 0.0 collective-permute-done
  48.1 3.0 %fusion.19 = f32[36,256,256]{2,1,0:T(8,128)} fusion(f32[36,256,256]{2,1,0:T(8,128)} %slice_dynamic-update-slice_fusion, f32[26,256,256]{2,1,0:T(8,128)S(1)} %copy-done, bf16[9,128,256]{2,1,0:T(8,128)(2,1)} %collective-permute-done, bf16[2,9,128,256]{3,2,1,0:T(8,128)(2,1)S(1)} %copy-done.3), kind=kOutput, calls=%fused_computation.26 | convolution fusion | flops 151584768 | bytes 5898240 | tf_op jit(solution)/shard_map/fbc,fbd->fcd/dot_general | solution.py:250
  51.1 1.7 %broadcast_dynamic-update-slice_fusion = f32[36,256,256]{2,1,0:T(8,128)} fusion(f32[36,256,256]{2,1,0:T(8,128)} %fusion.19), kind=kLoop, calls=%fused_computation.41 | loop fusion | bytes 2359296 | tf_op jit(solution)/shard_map/concatenate | solution.py:180
  52.8 86.6 %shard_map.86 = f32[6912,256]{1,0:T(8,128)} custom-call(f32[9216,256]{1,0:T(8,128)} %bitcast.23.x_ref), custom_call_target="tpu_custom_call" | custom-call | tf_op jit(solution)/shard_map/pallas_call | solution.py:185
  139.4 0.0 copy-start.2
  139.4 4.2 %fusion.23 = f32[1024,256]{1,0:T(8,128)} fusion(pred[2,9,128,1024]{2,3,1,0:T(32,128)(4,1)} %iota_compare_fusion.10, bf16[9,128,256]{2,1,0:T(8,128)(2,1)} %collective-permute-done.1, bf16[27,256,256]{2,1,0:T(8,128)(2,1)} %param.9), kind=kOutput, calls=%fused_computation.32 | convolution fusion | flops 755269632 | bytes 3997696 | tf_op jit(solution)/shard_map/fbv,fbc->vc/dot_general | solution.py:246
  143.6 0.0 copy-done.2
  143.6 4.1 %fusion.22 = f32[1024,256]{1,0:T(8,128)} fusion(pred[2,9,128,1024]{2,3,1,0:T(32,128)(4,1)S(1)} %copy-done.2, bf16[9,128,256]{2,1,0:T(8,128)(2,1)} %collective-permute-done, bf16[27,256,256]{2,1,0:T(8,128)(2,1)} %param.9), kind=kOutput, calls=%fused_computation.31 | convolution fusion | flops 755269632 | bytes 3997696 | tf_op jit(solution)/shard_map/fbv,fbc->vc/dot_general | solution.py:246
  147.8 0.0 copy-done.4
  147.8 0.0 copy-done.7
  147.8 12.8 %fusion.49 = bf16[1,1024,256]{2,1,0:T(8,128)(2,1)} fusion(f32[1024,256]{1,0:T(8,128)} %fusion.23, f32[1024,256]{1,0:T(8,128)} %fusion.22, f32[1024,256]{1,0:T(8,128)S(1)} %copy-done.4, bf16[13,256,256]{2,1,0:T(8,128)(2,1)} %get-tuple-element.3, bf16[13,256,256]{2,1,0:T(8,128)(2,1)} %get-tuple-element.2, bf16[26,256,256]{2,1,0:T(8,128)(2,1)} %fusion.18, ...), kind=kOutput, calls=%fused_computation.40 | convolution fusion | flops 6995705856 | bytes 10512384 | tf_op jit(solution)/shard_map/vkd,kcd->vc/dot_general | solution.py:272
  160.6 6.7 %copy.32 = f32[27,256,256]{2,1,0:T(8,128)} copy(f32[27,256,256]{2,1,0:T(8,128)} %bitcast.103) | data formatting | bytes 14155776
  (5 shorter events, 0.0 us)
Async XLA Ops:
  1.3 11.1 %copy-start.10 = (s32[1,1,2,9,128]{4,2,3,1,0:T(2,128)S(1)}, s32[1,1,2,9,128]{4,2,3,1,0:T(2,128)}, u32[]{:S(2)}) copy-start(s32[1,1,2,9,128]{4,2,3,1,0:T(2,128)} %param.13) | copy-start | bytes 27652
  1.3 11.1 %copy-start.8 = (s32[1,1,26,256]{3,1,2,0:T(1,128)S(1)}, s32[1,1,26,256]{3,1,2,0:T(1,128)}, u32[]{:S(2)}) copy-start(s32[1,1,26,256]{3,1,2,0:T(1,128)} %param.10) | copy-start | bytes 79876
  1.3 11.8 %copy-start.9 = (s32[1,1,26,256]{3,1,2,0:T(1,128)S(1)}, s32[1,1,26,256]{3,1,2,0:T(1,128)}, u32[]{:S(2)}) copy-start(s32[1,1,26,256]{3,1,2,0:T(1,128)} %param.11) | copy-start | bytes 79876
  1.3 11.8 %copy-start.5 = (bf16[1,1024,256]{2,1,0:T(8,128)(2,1)S(1)}, bf16[1,1024,256]{2,1,0:T(8,128)(2,1)}, u32[]{:S(2)}) copy-start(bf16[1,1024,256]{2,1,0:T(8,128)(2,1)} %param.8) | copy-start | bytes 1572868
  5.6 42.5 %collective-permute-start = (bf16[9,128,256]{2,1,0:T(8,128)(2,1)}, bf16[9,128,256]{2,1,0:T(8,128)(2,1)}, u32[]{:S(2)}, u32[]{:S(2)}) collective-permute-start(bf16[9,128,256]{2,1,0:T(8,128)(2,1)} %get-tuple-element.4), channel_id=1, source_target_pairs={{0,1},{1,2},{2,3},{3,4},{4,5},{5,6},{6,7},{7,8},{8,9},{9,10},{10,1... | collective-permute-start | bytes 1769480 | tf_op jit(solution)/shard_map/ppermute | solution.py:219
  10.5 30.6 %collective-permute-start.1 = (bf16[9,128,256]{2,1,0:T(8,128)(2,1)}, bf16[9,128,256]{2,1,0:T(8,128)(2,1)}, u32[]{:S(2)}, u32[]{:S(2)}) collective-permute-start(bf16[9,128,256]{2,1,0:T(8,128)(2,1)} %get-tuple-element.5), channel_id=1, source_target_pairs={{1,0},{2,1},{3,2},{4,3},{5,4},{6,5},{7,6},{8,7},{9,8},{10,9},{11,1... | collective-permute-start | bytes 1769480 | tf_op jit(solution)/shard_map/ppermute | solution.py:219
  13.1 6.6 %copy-start.1 = (bf16[27,256,256]{2,1,0:T(8,128)(2,1)S(1)}, bf16[27,256,256]{2,1,0:T(8,128)(2,1)}, u32[]{:S(2)}) copy-start(bf16[27,256,256]{2,1,0:T(8,128)(2,1)} %param.9) | copy-start | bytes 10616836
  19.7 2.0 %copy-start.11 = (bf16[1,1024,256]{2,1,0:T(8,128)(2,1)S(1)}, bf16[1,1024,256]{2,1,0:T(8,128)(2,1)}, u32[]{:S(2)}) copy-start(bf16[1,1024,256]{2,1,0:T(8,128)(2,1)} %param.7) | copy-start | bytes 1572868
  35.7 5.4 %copy-start.3 = (bf16[2,9,128,256]{3,2,1,0:T(8,128)(2,1)S(1)}, bf16[2,9,128,256]{3,2,1,0:T(8,128)(2,1)}, u32[]{:S(2)}) copy-start(bf16[2,9,128,256]{3,2,1,0:T(8,128)(2,1)} %convolution_convert_fusion) | copy-start | bytes 3538948
  38.2 6.8 %copy-start = (f32[26,256,256]{2,1,0:T(8,128)S(1)}, f32[26,256,256]{2,1,0:T(8,128)}, u32[]{:S(2)}) copy-start(f32[26,256,256]{2,1,0:T(8,128)} %fusion.16) | copy-start | bytes 20447236
  41.1 5.0 %copy-start.6 = (bf16[1,1024,256]{2,1,0:T(8,128)(2,1)S(1)}, bf16[1,1024,256]{2,1,0:T(8,128)(2,1)}, u32[]{:S(2)}) copy-start(bf16[1,1024,256]{2,1,0:T(8,128)(2,1)} %param.8) | copy-start | bytes 1572868
  41.1 5.0 %copy-start.12 = (bf16[1,1024,256]{2,1,0:T(8,128)(2,1)S(1)}, bf16[1,1024,256]{2,1,0:T(8,128)(2,1)}, u32[]{:S(2)}) copy-start(bf16[1,1024,256]{2,1,0:T(8,128)(2,1)} %param.7) | copy-start | bytes 1572868
  139.4 4.2 %copy-start.2 = (pred[2,9,128,1024]{2,3,1,0:T(32,128)(4,1)S(1)}, pred[2,9,128,1024]{2,3,1,0:T(32,128)(4,1)}, u32[]{:S(2)}) copy-start(pred[2,9,128,1024]{2,3,1,0:T(32,128)(4,1)} %iota_compare_fusion.10) | copy-start | bytes 7077892
  143.6 4.1 %copy-start.4 = (f32[1024,256]{1,0:T(8,128)S(1)}, f32[1024,256]{1,0:T(8,128)}, u32[]{:S(2)}) copy-start(f32[1024,256]{1,0:T(8,128)} %fusion.66) | copy-start | bytes 3145732
  143.6 4.1 %copy-start.7 = (s32[1,1,26,256]{3,2,1,0:T(8,128)S(1)}, s32[1,1,26,256]{3,2,1,0:T(8,128)}, u32[]{:S(2)}) copy-start(s32[1,1,26,256]{3,2,1,0:T(8,128)} %copy.23) | copy-start | bytes 79876

commit v6 on v3

--- a/solution.py
+++ b/solution.py
@@ -65,45 +65,74 @@
             device_id=peer_of(at, "core", 1), device_id_type=MESH_IDS)
         cp.start()
         copies.append(cp)
+    sources = (part, p1, p2)
+    recvs = (r1, r2, r3)
+    blocks = (COLOR_ROWS // 8, COLOR_ROWS // 32, COLOR_ROWS // 128)
+    ranks = [[at[d] for d in order] for order in COLOR_ORDERS]
+
+    def scatter_sends(stage, k):
+        blk, src, rbuf = blocks[stage], sources[stage], recvs[stage]
+        dim, me = COLOR_ORDERS[k][stage], ranks[k][stage]
+        row = []
+        for s in (1, 2, 3):
+            cp = pltpu.make_async_remote_copy(
+                src_ref=src.at[k, pl.ds(pl.multiple_of(((me + s) % 4) * blk, 8), blk)],
+                dst_ref=rbuf.at[k, s - 1], send_sem=rs_send.at[stage, k, s - 1],
+                recv_sem=rs_recv.at[stage, k, s - 1],
+                device_id=peer_of(at, dim, s), device_id_type=MESH_IDS)
+            cp.start()
+            row.append(cp)
+        return row
+
+    def gather_sends(step, k):
+        stage = (2, 1, 0)[step]
+        blk = (COLOR_ROWS // 128, COLOR_ROWS // 32, COLOR_ROWS // 8)[step]
+        dim = COLOR_ORDERS[k][stage]
+        a, b, e = ranks[k]
+        lead = (c * 64 + a * 16 + b * 4 + e, c * 64 + a * 16 + b * 4, c * 64 + a * 16)[step]
+        pos = pl.multiple_of(k * COLOR_ROWS + lead * CHUNK_ROWS, 8)
+        row = []
+        for s in (1, 2, 3):
+            cp = pltpu.make_async_remote_copy(
+                src_ref=out_ref.at[pl.ds(pos, blk)], dst_ref=out_ref.at[pl.ds(pos, blk)],
+                send_sem=ag_send.at[stage, k, s - 1], recv_sem=ag_recv.at[stage, k, s - 1],
+                device_id=peer_of(at, dim, s), device_id_type=MESH_IDS)
+            cp.start()
+            row.append(cp)
+        return row
+
+    def pair_send(k):
+        pos = pl.multiple_of(k * COLOR_ROWS + c * half, 8)
+        cp = pltpu.make_async_remote_copy(
+            src_ref=out_ref.at[pl.ds(pos, half)], dst_ref=out_ref.at[pl.ds(pos, half)],
+            send_sem=agc_send.at[k], recv_sem=agc_recv.at[k],
+            device_id=peer_of(at, "core", 1), device_id_type=MESH_IDS)
+        cp.start()
+        return cp
+
+    staged = [None] * 3
     for k in range(3):
         copies[k].wait()
         base = k * COLOR_ROWS + c * half
         add_rows(lambda a, v, k=k: part.__setitem__((k, a), v),
                  lambda a, base=base: x_ref[pl.ds(pl.multiple_of(base, 8) + a.start, a.size)],
                  [lambda a, k=k: rcore[k, a]], half, 128)
-
-    sources = (part, p1, p2)
-    recvs = (r1, r2, r3)
-    blocks = (COLOR_ROWS // 8, COLOR_ROWS // 32, COLOR_ROWS // 128)
-    ranks = [[at[d] for d in order] for order in COLOR_ORDERS]
+        staged[k] = scatter_sends(0, k)
     for stage in range(3):
-        blk = blocks[stage]
-        src, rbuf = sources[stage], recvs[stage]
-        staged = []
-        for k, order in enumerate(COLOR_ORDERS):
-            dim = order[stage]
-            me = ranks[k][stage]
-            row = []
-            for s in (1, 2, 3):
-                cp = pltpu.make_async_remote_copy(
-                    src_ref=src.at[k, pl.ds(pl.multiple_of(((me + s) % 4) * blk, 8), blk)],
-                    dst_ref=rbuf.at[k, s - 1], send_sem=rs_send.at[stage, k, s - 1],
-                    recv_sem=rs_recv.at[stage, k, s - 1],
-                    device_id=peer_of(at, dim, s), device_id_type=MESH_IDS)
-                cp.start()
-                row.append(cp)
-            staged.append(row)
+        blk, src, rbuf = blocks[stage], sources[stage], recvs[stage]
         for k in range(3):
             for cp in staged[k]:
                 cp.wait()
             me = ranks[k][stage]
             own = pl.multiple_of(me * blk, 8)
-            others = [lambda a, k=k, j=j: rbuf[k, j, a] for j in range(3)]
+            others = [lambda a, k=k, j=j, rbuf=rbuf: rbuf[k, j, a] for j in range(3)]
             first = lambda a, k=k, own=own, src=src: src[k, pl.ds(own + a.start, a.size)]
             if stage == 0:
                 add_rows(lambda a, v, k=k: p1.__setitem__((k, a), v), first, others, blk, 128)
+                staged[k] = scatter_sends(1, k)
             elif stage == 1:
                 add_rows(lambda a, v, k=k: p2.__setitem__((k, a), v), first, others, blk, blk)
+                staged[k] = scatter_sends(2, k)
             else:
                 total = first(pl.ds(0, blk)) + others[0](pl.ds(0, blk)) + others[1](pl.ds(0, blk)) + others[2](pl.ds(0, blk))
                 a, b, e = ranks[k]
@@ -112,40 +141,15 @@
                 put = pltpu.make_async_copy(red.at[k], out_ref.at[pl.ds(pos, blk)], out_sem.at[k])
                 put.start()
                 put.wait()
-
-    sizes = (COLOR_ROWS // 128, COLOR_ROWS // 32, COLOR_ROWS // 8)
-    for step, stage in enumerate((2, 1, 0)):
-        blk = sizes[step]
-        staged = []
-        for k, order in enumerate(COLOR_ORDERS):
-            dim = order[stage]
-            a, b, e = ranks[k]
-            lead = (c * 64 + a * 16 + b * 4 + e, c * 64 + a * 16 + b * 4, c * 64 + a * 16)[step]
-            pos = pl.multiple_of(k * COLOR_ROWS + lead * CHUNK_ROWS, 8)
-            row = []
-            for s in (1, 2, 3):
-                cp = pltpu.make_async_remote_copy(
-                    src_ref=out_ref.at[pl.ds(pos, blk)], dst_ref=out_ref.at[pl.ds(pos, blk)],
-                    send_sem=ag_send.at[stage, k, s - 1], recv_sem=ag_recv.at[stage, k, s - 1],
-                    device_id=peer_of(at, dim, s), device_id_type=MESH_IDS)
-                cp.start()
-                row.append(cp)
-            staged.append(row)
-        for row in staged:
-            for cp in row:
+                staged[k] = gather_sends(0, k)
+    for step in range(3):
+        for k in range(3):
+            for cp in staged[k]:
                 cp.wait()
-    last = []
+            staged[k] = gather_sends(step + 1, k) if step < 2 else [pair_send(k)]
     for k in range(3):
-        pos = pl.multiple_of(k * COLOR_ROWS + c * half, 8)
-        cp = pltpu.make_async_remote_copy(
-            src_ref=out_ref.at[pl.ds(pos, half)], dst_ref=out_ref.at[pl.ds(pos, half)],
-            send_sem=agc_send.at[k], recv_sem=agc_recv.at[k],
-            device_id=peer_of(at, "core", 1), device_id_type=MESH_IDS)
-        cp.start()
-        last.append(cp)
-    for cp in last:
-        cp.wait()
-
+        for cp in staged[k]:
+            cp.wait()
 
 def summed_everywhere(stacked, scale):
     rows = PAD_OFFSETS * 256

time: 167 us -> 166 us (level)
  Pallas kernels: 87.2 us -> 85.3 us
    pallas_call x1, Pallas kernels: 87.2 us -> 85.3 us  [summed_everywhere(): pl.pallas_call(functools.partial(allreduce_kernel, scale), out_shape=jax....]
  transfers between devices with their start and end apart: 2 -> 2, of which waited for: 0 -> 0; matrix products, arithmetic and copies ran while one was open for 21% -> 22% of each run, Pallas kernels for 0% -> 0%
where the time goes in v6:
time: 166 us; the launch traced here: 165 us
  Pallas kernels  85.3 us (51%)
  matrix products  54.6 us (33%)
  local copies, waits for them, and re-layouts  14.9 us (9%)
  starting transfers between devices  6.83 us (4%)
  other arithmetic  2.81 us (2%)
    pallas_call x1, Pallas kernels, summed_everywhere(): pl.pallas_call(functools.partial(allreduce_kernel, scale), out_shape=jax....  85.3 us
    dot_general x3, matrix products, pick_rows(): jnp.einsum('...v,vc->...c', table, source, preferred_element_type=jnp.flo...  13.3 us
    dot_general x1, matrix products, per_device(): jnp.einsum('vkd,kcd->vc', placed, side_kernels, preferred_element_type=jn...  13.1 us
    dot_general x1, matrix products, per_device(): jnp.einsum('kpc,kpd->kcd', gathered_x, gathered_g, preferred_element_type...  10.3 us
    dot_general x2, matrix products, place_rows(): jnp.einsum('fbv,fbc->vc', table, rows, preferred_element_type=jnp.float32)  7.34 us
    dot_general x2, matrix products, face_products(): jnp.einsum('fbc,fbd->fcd', features, grads, preferred_element_type=jnp.fl...  6.93 us
    ppermute x2, starting transfers between devices, passed_along(): return lax.ppermute(array, axis, pairs)  6.83 us
    slice x1, local copies, waits for them, and re-layouts, summed_everywhere(): return total[:stacked.shape[0] * stacked.shape[1]].reshape(stacked.shape)  6.59 us
  transfers between devices with their start and end apart: 2, of which 0 were waited for; matrix products, arithmetic and copies ran while one was open for 22% of the time, Pallas kernels for 0%

profile of v6, /device:TPU:1, one launch (start us, length us, event | category | flops | bytes accessed | tf_op | source)
XLA Modules:
  0.0 165.1 jit_solution(12415282064487562585)
XLA Ops:
  0.6 0.7 copy.10
  1.3 0.0 copy-start.8
  1.3 0.0 copy-start.6
  1.3 0.0 copy-start.7
  1.3 0.0 copy-start.4
  1.3 3.1 %fusion.21 = bf16[2,9,128,256]{3,2,1,0:T(8,128)(2,1)S(1)} fusion(s32[2,9,128]{2,1,0:T(8,128)S(1)} %copy.10, bf16[1,1024,256]{2,1,0:T(8,128)(2,1)} %param.8), kind=kOutput, calls=%fused_computation.30 | convolution fusion | flops 1210908672 | bytes 1713152 | tf_op jit(solution)/shard_map/...v,vc->...c/dot_general | solution.py:217
  4.5 1.1 slice_bitcast_fusion.13
  5.6 4.9 %collective-permute-start = (bf16[9,128,256]{2,1,0:T(8,128)(2,1)}, bf16[9,128,256]{2,1,0:T(8,128)(2,1)}, u32[]{:S(2)}, u32[]{:S(2)}) collective-permute-start(bf16[9,128,256]{2,1,0:T(8,128)(2,1)} %get-tuple-element.4), channel_id=1, source_target_pairs={{0,1},{1,2},{2,3},{3,4},{4,5},{5,6},{6,7},{7,8},{8,9},{9,10},{10,1... | collective-permute-start | bytes 1769480 | tf_op jit(solution)/shard_map/ppermute | solution.py:196
  10.5 1.9 %collective-permute-start.1 = (bf16[9,128,256]{2,1,0:T(8,128)(2,1)}, bf16[9,128,256]{2,1,0:T(8,128)(2,1)}, u32[]{:S(2)}, u32[]{:S(2)}) collective-permute-start(bf16[9,128,256]{2,1,0:T(8,128)(2,1)} %get-tuple-element.5), channel_id=1, source_target_pairs={{1,0},{2,1},{3,2},{4,3},{5,4},{6,5},{7,6},{8,7},{9,8},{10,9},{11,1... | collective-permute-start | bytes 1769480 | tf_op jit(solution)/shard_map/ppermute | solution.py:196
  12.4 0.0 copy-done.8
  12.4 0.0 copy-done.6
  12.5 0.6 copy.23
  13.1 0.0 copy-done.7
  13.1 0.0 copy-done.4
  13.1 0.0 copy-start.1
  13.1 6.5 %fusion.18 = bf16[26,256,256]{2,1,0:T(8,128)(2,1)} fusion(s32[26,256]{1,0:T(8,128)S(1)} %bitcast.106, bf16[1,1024,256]{2,1,0:T(8,128)(2,1)S(1)} %copy-done.4), kind=kOutput, calls=%fused_computation.24 | convolution fusion | flops 3498180608 | bytes 3958784 | tf_op jit(solution)/shard_map/...v,vc->...c/dot_general | solution.py:217
  19.6 0.0 copy-done.1
  19.6 0.0 copy-start.9
  19.6 2.1 %fusion.71 = (bf16[13,256,256]{2,1,0:T(8,128)(2,1)}, bf16[13,256,256]{2,1,0:T(8,128)(2,1)}) fusion(bf16[27,256,256]{2,1,0:T(8,128)(2,1)S(1)} %copy-done.1), kind=kLoop, calls=%fused_computation.65 | loop fusion | bytes 6815744 | tf_op jit(solution)/shard_map/slice | solution.py:248
  21.7 0.0 copy-done.9
  21.7 3.7 %convolution_convert_fusion = bf16[2,9,128,256]{3,2,1,0:T(8,128)(2,1)} fusion(bf16[1,1024,256]{2,1,0:T(8,128)(2,1)S(1)} %copy-done.9, s32[2,9,128]{2,1,0:T(8,128)S(1)} %copy.9), kind=kOutput, calls=%fused_computation.29 | convolution fusion | flops 1210908672 | bytes 1713152 | tf_op jit(solution)/shard_map/...v,vc->...c/dot_general | solution.py:217
  25.4 10.3 %fusion.16 = f32[26,256,256]{2,1,0:T(8,128)} fusion(bf16[26,256,256]{2,1,0:T(8,128)(2,1)} %fusion.18, s32[26,256]{1,0:T(8,128)} %bitcast.104, bf16[1,1024,256]{2,1,0:T(8,128)(2,1)} %param.7), kind=kOutput, calls=%fused_computation.22 | convolution fusion | flops 4370595840 | bytes 10774528 | tf_op jit(solution)/shard_map/kpc,kpd->kcd/dot_general | solution.py:252
  35.7 0.0 copy-start.3
  35.7 2.4 %fusion.66 = f32[1024,256]{1,0:T(8,128)} fusion(bf16[1,1024,256]{2,1,0:T(8,128)(2,1)} %param.8, bf16[27,256,256]{2,1,0:T(8,128)(2,1)S(1)} %copy-done.1), kind=kOutput, calls=%fused_computation.58 | convolution fusion | flops 134217728 | bytes 1703936 | tf_op jit(solution)/shard_map/dot_general | solution.py:206
  38.2 0.0 copy-start
  38.2 2.8 %iota_compare_fusion.10 = pred[2,9,128,1024]{2,3,1,0:T(32,128)(4,1)} fusion(s32[2,9,128]{2,1,0:T(8,128)S(1)} %copy.9), kind=kLoop, calls=%fused_computation.12 | loop fusion | flops 2359296 | bytes 2368512 | tf_op jit(solution)/shard_map/eq | solution.py:213
  41.0 0.0 copy-start.5
  41.0 0.0 copy-start.10
  41.0 0.0 collective-permute-done.1
  41.0 0.0 copy-done.3
  41.0 3.9 %fusion.20 = f32[36,256,256]{2,1,0:T(8,128)} fusion(f32[26,256,256]{2,1,0:T(8,128)} %fusion.16, bf16[9,128,256]{2,1,0:T(8,128)(2,1)} %collective-permute-done.1, bf16[2,9,128,256]{3,2,1,0:T(8,128)(2,1)S(1)} %copy-done.3), kind=kOutput, calls=%fused_computation.28 | convolution fusion | flops 151584768 | bytes 5898240 | tf_op jit(solution)/shard_map/fbc,fbd->fcd/dot_general | solution.py:227
  44.9 0.0 copy-done
  44.9 1.0 slice_dynamic-update-slice_fusion.1
  45.9 0.0 copy-done.5
  45.9 0.0 copy-done.10
  45.9 1.0 fusion.58
  47.0 1.1 slice_dynamic-update-slice_fusion
  48.0 0.0 collective-permute-done
  48.0 3.0 %fusion.19 = f32[36,256,256]{2,1,0:T(8,128)} fusion(f32[36,256,256]{2,1,0:T(8,128)} %slice_dynamic-update-slice_fusion, f32[26,256,256]{2,1,0:T(8,128)S(1)} %copy-done, bf16[9,128,256]{2,1,0:T(8,128)(2,1)} %collective-permute-done, bf16[2,9,128,256]{3,2,1,0:T(8,128)(2,1)S(1)} %copy-done.3), kind=kOutput, calls=%fused_computation.26 | convolution fusion | flops 151584768 | bytes 5898240 | tf_op jit(solution)/shard_map/fbc,fbd->fcd/dot_general | solution.py:227
  51.1 1.7 %broadcast_dynamic-update-slice_fusion = f32[36,256,256]{2,1,0:T(8,128)} fusion(f32[36,256,256]{2,1,0:T(8,128)} %fusion.19), kind=kLoop, calls=%fused_computation.41 | loop fusion | bytes 2359296 | tf_op jit(solution)/shard_map/concatenate | solution.py:157
  52.8 85.3 %shard_map.86 = f32[9216,256]{1,0:T(8,128)} custom-call(f32[9216,256]{1,0:T(8,128)} %bitcast.23.x_ref), custom_call_target="tpu_custom_call" | custom-call | tf_op jit(solution)/shard_map/pallas_call | solution.py:162
  138.1 0.0 copy-start.2
  138.1 6.6 %slice.63 = f32[6912,256]{1,0:T(8,128)} slice(f32[9216,256]{1,0:T(8,128)} %shard_map.86), slice={[0:6912], [0:256]} | slice | bytes 14155776 | tf_op jit(solution)/shard_map/slice | solution.py:190
  144.7 0.0 copy-done.2
  144.7 3.7 %fusion.23 = f32[1024,256]{1,0:T(8,128)} fusion(pred[2,9,128,1024]{2,3,1,0:T(32,128)(4,1)} %iota_compare_fusion.10, bf16[9,128,256]{2,1,0:T(8,128)(2,1)} %collective-permute-done.1, bf16[27,256,256]{2,1,0:T(8,128)(2,1)S(1)} %copy-done.2), kind=kOutput, calls=%fused_computation.32 | convolution fusion | flops 755269632 | bytes 3997696 | tf_op jit(solution)/shard_map/fbv,fbc->vc/dot_general | solution.py:223
  148.3 3.7 %fusion.22 = f32[1024,256]{1,0:T(8,128)} fusion(pred[2,9,128,1024]{2,3,1,0:T(32,128)(4,1)} %iota_compare_fusion.10, bf16[9,128,256]{2,1,0:T(8,128)(2,1)} %collective-permute-done, bf16[27,256,256]{2,1,0:T(8,128)(2,1)S(1)} %copy-done.2), kind=kOutput, calls=%fused_computation.31 | convolution fusion | flops 755269632 | bytes 3997696 | tf_op jit(solution)/shard_map/fbv,fbc->vc/dot_general | solution.py:223
  152.0 13.1 %fusion.49 = bf16[1,1024,256]{2,1,0:T(8,128)(2,1)} fusion(f32[1024,256]{1,0:T(8,128)} %fusion.23, f32[1024,256]{1,0:T(8,128)} %fusion.22, f32[1024,256]{1,0:T(8,128)} %fusion.66, bf16[13,256,256]{2,1,0:T(8,128)(2,1)} %get-tuple-element.3, bf16[13,256,256]{2,1,0:T(8,128)(2,1)} %get-tuple-element.2, bf16[26,256,256]{2,1,0:T(8,128)(2,1)} %fusion.18, ...), kind=kOutput, calls=%fused_computation.40 | convolution fusion | flops 6995705856 | bytes 10512384 | tf_op jit(solution)/shard_map/vkd,kcd->vc/dot_general | solution.py:249
  (2 shorter events, 0.0 us)
Async XLA Ops:
  1.3 11.1 %copy-start.8 = (s32[1,1,2,9,128]{4,2,3,1,0:T(2,128)S(1)}, s32[1,1,2,9,128]{4,2,3,1,0:T(2,128)}, u32[]{:S(2)}) copy-start(s32[1,1,2,9,128]{4,2,3,1,0:T(2,128)} %param.13) | copy-start | bytes 27652
  1.3 11.1 %copy-start.6 = (s32[1,1,26,256]{3,1,2,0:T(1,128)S(1)}, s32[1,1,26,256]{3,1,2,0:T(1,128)}, u32[]{:S(2)}) copy-start(s32[1,1,26,256]{3,1,2,0:T(1,128)} %param.10) | copy-start | bytes 79876
  1.3 11.7 %copy-start.7 = (s32[1,1,26,256]{3,1,2,0:T(1,128)S(1)}, s32[1,1,26,256]{3,1,2,0:T(1,128)}, u32[]{:S(2)}) copy-start(s32[1,1,26,256]{3,1,2,0:T(1,128)} %param.11) | copy-start | bytes 79876
  1.3 11.7 %copy-start.4 = (bf16[1,1024,256]{2,1,0:T(8,128)(2,1)S(1)}, bf16[1,1024,256]{2,1,0:T(8,128)(2,1)}, u32[]{:S(2)}) copy-start(bf16[1,1024,256]{2,1,0:T(8,128)(2,1)} %param.8) | copy-start | bytes 1572868
  5.6 42.5 %collective-permute-start = (bf16[9,128,256]{2,1,0:T(8,128)(2,1)}, bf16[9,128,256]{2,1,0:T(8,128)(2,1)}, u32[]{:S(2)}, u32[]{:S(2)}) collective-permute-start(bf16[9,128,256]{2,1,0:T(8,128)(2,1)} %get-tuple-element.4), channel_id=1, source_target_pairs={{0,1},{1,2},{2,3},{3,4},{4,5},{5,6},{6,7},{7,8},{8,9},{9,10},{10,1... | collective-permute-start | bytes 1769480 | tf_op jit(solution)/shard_map/ppermute | solution.py:196
  10.5 30.5 %collective-permute-start.1 = (bf16[9,128,256]{2,1,0:T(8,128)(2,1)}, bf16[9,128,256]{2,1,0:T(8,128)(2,1)}, u32[]{:S(2)}, u32[]{:S(2)}) collective-permute-start(bf16[9,128,256]{2,1,0:T(8,128)(2,1)} %get-tuple-element.5), channel_id=1, source_target_pairs={{1,0},{2,1},{3,2},{4,3},{5,4},{6,5},{7,6},{8,7},{9,8},{10,9},{11,1... | collective-permute-start | bytes 1769480 | tf_op jit(solution)/shard_map/ppermute | solution.py:196
  13.1 6.6 %copy-start.1 = (bf16[27,256,256]{2,1,0:T(8,128)(2,1)S(1)}, bf16[27,256,256]{2,1,0:T(8,128)(2,1)}, u32[]{:S(2)}) copy-start(bf16[27,256,256]{2,1,0:T(8,128)(2,1)} %param.9) | copy-start | bytes 10616836
  19.6 2.1 %copy-start.9 = (bf16[1,1024,256]{2,1,0:T(8,128)(2,1)S(1)}, bf16[1,1024,256]{2,1,0:T(8,128)(2,1)}, u32[]{:S(2)}) copy-start(bf16[1,1024,256]{2,1,0:T(8,128)(2,1)} %param.7) | copy-start | bytes 1572868
  35.7 5.3 %copy-start.3 = (bf16[2,9,128,256]{3,2,1,0:T(8,128)(2,1)S(1)}, bf16[2,9,128,256]{3,2,1,0:T(8,128)(2,1)}, u32[]{:S(2)}) copy-start(bf16[2,9,128,256]{3,2,1,0:T(8,128)(2,1)} %convolution_convert_fusion) | copy-start | bytes 3538948
  38.2 6.7 %copy-start = (f32[26,256,256]{2,1,0:T(8,128)S(1)}, f32[26,256,256]{2,1,0:T(8,128)}, u32[]{:S(2)}) copy-start(f32[26,256,256]{2,1,0:T(8,128)} %fusion.16) | copy-start | bytes 20447236
  41.0 5.0 %copy-start.5 = (bf16[1,1024,256]{2,1,0:T(8,128)(2,1)S(1)}, bf16[1,1024,256]{2,1,0:T(8,128)(2,1)}, u32[]{:S(2)}) copy-start(bf16[1,1024,256]{2,1,0:T(8,128)(2,1)} %param.8) | copy-start | bytes 1572868
  41.0 5.0 %copy-start.10 = (bf16[1,1024,256]{2,1,0:T(8,128)(2,1)S(1)}, bf16[1,1024,256]{2,1,0:T(8,128)(2,1)}, u32[]{:S(2)}) copy-start(bf16[1,1024,256]{2,1,0:T(8,128)(2,1)} %param.7) | copy-start | bytes 1572868
  138.1 6.6 %copy-start.2 = (bf16[27,256,256]{2,1,0:T(8,128)(2,1)S(1)}, bf16[27,256,256]{2,1,0:T(8,128)(2,1)}, u32[]{:S(2)}) copy-start(bf16[27,256,256]{2,1,0:T(8,128)(2,1)} %param.9) | copy-start | bytes 10616836

commit v7 on v6

--- a/solution.py
+++ b/solution.py
@@ -46,8 +46,9 @@
     lax.fori_loop(0, rows // slab, body, 0)
 
 
-def allreduce_kernel(scale, x_ref, out_ref, rcore, part, r1, p1, r2, p2, r3, red,
-                     core_send, core_recv, rs_send, rs_recv, ag_send, ag_recv, agc_send, agc_recv, out_sem):
+def allreduce_kernel(scale, x_ref, out_ref, rcore, part, rr0, sb0, p1, rr1, sb1, p2, r3, red,
+                     core_send, core_recv, rs_send, rs_recv, ag_send, ag_recv, agc_send, agc_recv, out_sem,
+                     ring_send, ring_recv, ring_ag_send, ring_ag_recv):
     at = coords_here()
     half = COLOR_ROWS // 2
     barrier = pltpu.get_barrier_semaphore()
@@ -66,7 +67,7 @@
         cp.start()
         copies.append(cp)
     sources = (part, p1, p2)
-    recvs = (r1, r2, r3)
+    recvs = (None, None, r3)
     blocks = (COLOR_ROWS // 8, COLOR_ROWS // 32, COLOR_ROWS // 128)
     ranks = [[at[d] for d in order] for order in COLOR_ORDERS]
 
@@ -110,43 +111,102 @@
         cp.start()
         return cp
 
-    staged = [None] * 3
+    rings = ((rr0, sb0), (rr1, sb1))
+    nexts = (p1, p2)
+
+    def own_half(stage, k, chunk, d):
+        blk = blocks[stage]
+        return sources[stage].at[k, pl.ds(pl.multiple_of(chunk * blk + d * (blk // 2), 8), blk // 2)]
+
+    def ring_peer(stage, k, d):
+        return peer_of(at, COLOR_ORDERS[k][stage], 1 if d == 0 else 3)
+
+    def scatter_ring(stage):
+        rr, sb = rings[stage]
+        live = {}
+        for k in range(3):
+            me = ranks[k][stage]
+            for d in range(2):
+                chunk = (me + 3) % 4 if d == 0 else (me + 1) % 4
+                cp = pltpu.make_async_remote_copy(
+                    src_ref=own_half(stage, k, chunk, d), dst_ref=rr.at[k, d, 0],
+                    send_sem=ring_send.at[stage, k, d, 0], recv_sem=ring_recv.at[stage, k, d, 0],
+                    device_id=ring_peer(stage, k, d), device_id_type=MESH_IDS)
+                cp.start()
+                live[k, d] = cp
+        for t in (1, 2):
+            for k in range(3):
+                me = ranks[k][stage]
+                for d in range(2):
+                    live[k, d].wait()
+                    chunk = (me + 3 - t) % 4 if d == 0 else (me + t + 1) % 4
+                    sb[k, d, t] = rr[k, d, t - 1] + own_half(stage, k, chunk, d)[...]
+                    cp = pltpu.make_async_remote_copy(
+                        src_ref=sb.at[k, d, t], dst_ref=rr.at[k, d, t],
+                        send_sem=ring_send.at[stage, k, d, t], recv_sem=ring_recv.at[stage, k, d, t],
+                        device_id=ring_peer(stage, k, d), device_id_type=MESH_IDS)
+                    cp.start()
+                    live[k, d] = cp
+        for k in range(3):
+            me = ranks[k][stage]
+            h = blocks[stage] // 2
+            for d in range(2):
+                live[k, d].wait()
+                nexts[stage][k, pl.ds(d * h, h)] = rr[k, d, 2] + own_half(stage, k, me, d)[...]
+
+    def gather_ring(stage):
+        blk = blocks[stage]
+        h = blk // 2
+        live = {}
+        for t in range(3):
+            for k in range(3):
+                a, b, e = ranks[k]
+                me = ranks[k][stage]
+                parent = (c * 64, c * 64 + a * 16)[stage]
+                for d in range(2):
+                    if t > 0:
+                        live[k, d].wait()
+                    chunk = (me + 4 - t) % 4 if d == 0 else (me + t) % 4
+                    pos = pl.multiple_of(k * COLOR_ROWS + parent * CHUNK_ROWS + chunk * blk + d * h, 8)
+                    cp = pltpu.make_async_remote_copy(
+                        src_ref=out_ref.at[pl.ds(pos, h)], dst_ref=out_ref.at[pl.ds(pos, h)],
+                        send_sem=ring_ag_send.at[stage, k, d, t], recv_sem=ring_ag_recv.at[stage, k, d, t],
+                        device_id=ring_peer(stage, k, d), device_id_type=MESH_IDS)
+                    cp.start()
+                    live[k, d] = cp
+        for k in range(3):
+            for d in range(2):
+                live[k, d].wait()
+
     for k in range(3):
         copies[k].wait()
         base = k * COLOR_ROWS + c * half
         add_rows(lambda a, v, k=k: part.__setitem__((k, a), v),
                  lambda a, base=base: x_ref[pl.ds(pl.multiple_of(base, 8) + a.start, a.size)],
                  [lambda a, k=k: rcore[k, a]], half, 128)
-        staged[k] = scatter_sends(0, k)
-    for stage in range(3):
-        blk, src, rbuf = blocks[stage], sources[stage], recvs[stage]
-        for k in range(3):
-            for cp in staged[k]:
-                cp.wait()
-            me = ranks[k][stage]
-            own = pl.multiple_of(me * blk, 8)
-            others = [lambda a, k=k, j=j, rbuf=rbuf: rbuf[k, j, a] for j in range(3)]
-            first = lambda a, k=k, own=own, src=src: src[k, pl.ds(own + a.start, a.size)]
-            if stage == 0:
-                add_rows(lambda a, v, k=k: p1.__setitem__((k, a), v), first, others, blk, 128)
-                staged[k] = scatter_sends(1, k)
-            elif stage == 1:
-                add_rows(lambda a, v, k=k: p2.__setitem__((k, a), v), first, others, blk, blk)
-                staged[k] = scatter_sends(2, k)
-            else:
-                total = first(pl.ds(0, blk)) + others[0](pl.ds(0, blk)) + others[1](pl.ds(0, blk)) + others[2](pl.ds(0, blk))
-                a, b, e = ranks[k]
-                pos = pl.multiple_of(k * COLOR_ROWS + (c * 64 + a * 16 + b * 4 + e) * CHUNK_ROWS, 8)
-                red[k] = total * scale
-                put = pltpu.make_async_copy(red.at[k], out_ref.at[pl.ds(pos, blk)], out_sem.at[k])
-                put.start()
-                put.wait()
-                staged[k] = gather_sends(0, k)
-    for step in range(3):
-        for k in range(3):
-            for cp in staged[k]:
-                cp.wait()
-            staged[k] = gather_sends(step + 1, k) if step < 2 else [pair_send(k)]
+    scatter_ring(0)
+    scatter_ring(1)
+    staged = [scatter_sends(2, k) for k in range(3)]
+    blk = blocks[2]
+    for k in range(3):
+        for cp in staged[k]:
+            cp.wait()
+        me = ranks[k][2]
+        own = pl.multiple_of(me * blk, 8)
+        total = p2[k, pl.ds(own, blk)] + r3[k, 0] + r3[k, 1] + r3[k, 2]
+        a, b, e = ranks[k]
+        pos = pl.multiple_of(k * COLOR_ROWS + (c * 64 + a * 16 + b * 4 + e) * CHUNK_ROWS, 8)
+        red[k] = total * scale
+        put = pltpu.make_async_copy(red.at[k], out_ref.at[pl.ds(pos, blk)], out_sem.at[k])
+        put.start()
+        put.wait()
+        staged[k] = gather_sends(0, k)
+    for k in range(3):
+        for cp in staged[k]:
+            cp.wait()
+    gather_ring(1)
+    gather_ring(0)
+    staged = [[pair_send(k)] for k in range(3)]
     for k in range(3):
         for cp in staged[k]:
             cp.wait()
@@ -167,9 +227,11 @@
         scratch_shapes=[
             pltpu.VMEM((3, COLOR_ROWS // 2, width), f32),
             pltpu.VMEM((3, COLOR_ROWS // 2, width), f32),
-            pltpu.VMEM((3, 3, blocks[0], width), f32),
+            pltpu.VMEM((3, 2, 3, blocks[0] // 2, width), f32),
+            pltpu.VMEM((3, 2, 3, blocks[0] // 2, width), f32),
             pltpu.VMEM((3, blocks[0], width), f32),
-            pltpu.VMEM((3, 3, blocks[1], width), f32),
+            pltpu.VMEM((3, 2, 3, blocks[1] // 2, width), f32),
+            pltpu.VMEM((3, 2, 3, blocks[1] // 2, width), f32),
             pltpu.VMEM((3, blocks[1], width), f32),
             pltpu.VMEM((3, 3, blocks[2], width), f32),
             pltpu.VMEM((3, blocks[2], width), f32),
@@ -182,6 +244,10 @@
             pltpu.SemaphoreType.DMA((3,)),
             pltpu.SemaphoreType.DMA((3,)),
             pltpu.SemaphoreType.DMA((3,)),
+            pltpu.SemaphoreType.DMA((2, 3, 2, 3)),
+            pltpu.SemaphoreType.DMA((2, 3, 2, 3)),
+            pltpu.SemaphoreType.DMA((2, 3, 2, 3)),
+            pltpu.SemaphoreType.DMA((2, 3, 2, 3)),
         ],
         compiler_params=pltpu.CompilerParams(
             collective_id=0, has_side_effects=True, vmem_limit_bytes=64 * 1024 * 1024

time: 166 us -> 181 us (1.090)
  Pallas kernels: 85.3 us -> 101 us
    pallas_call x1, Pallas kernels: 85.3 us -> 101 us  [summed_everywhere(): pl.pallas_call(functools.partial(allreduce_kernel, scale), out_shape=jax....]
  transfers between devices with their start and end apart: 2 -> 2, of which waited for: 0 -> 0; matrix products, arithmetic and copies ran while one was open for 22% -> 20% of each run, Pallas kernels for 0% -> 0%
where the time goes in v7:
time: 181 us
  Pallas kernels  101 us (56%)
  matrix products  54.6 us (30%)
  local copies, waits for them, and re-layouts  14.9 us (8%)
  starting transfers between devices  6.83 us (4%)
  other arithmetic  2.81 us (2%)
    pallas_call x1, Pallas kernels, summed_everywhere(): pl.pallas_call(functools.partial(allreduce_kernel, scale), out_shape=jax....  101 us
    dot_general x3, matrix products, pick_rows(): jnp.einsum('...v,vc->...c', table, source, preferred_element_type=jnp.flo...  13.3 us
    dot_general x1, matrix products, per_device(): jnp.einsum('vkd,kcd->vc', placed, side_kernels, preferred_element_type=jn...  13.1 us
    dot_general x1, matrix products, per_device(): jnp.einsum('kpc,kpd->kcd', gathered_x, gathered_g, preferred_element_type...  10.3 us
    dot_general x2, matrix products, place_rows(): jnp.einsum('fbv,fbc->vc', table, rows, preferred_element_type=jnp.float32)  7.34 us
    dot_general x2, matrix products, face_products(): jnp.einsum('fbc,fbd->fcd', features, grads, preferred_element_type=jnp.fl...  6.93 us
    ppermute x2, starting transfers between devices, passed_along(): return lax.ppermute(array, axis, pairs)  6.83 us
    slice x1, local copies, waits for them, and re-layouts, summed_everywhere(): return total[:stacked.shape[0] * stacked.shape[1]].reshape(stacked.shape)  6.59 us
  transfers between devices with their start and end apart: 2, of which 0 were waited for; matrix products, arithmetic and copies ran while one was open for 20% of the time, Pallas kernels for 0%

profile of v7, /device:TPU:1, one launch (start us, length us, event | category | flops | bytes accessed | tf_op | source)
XLA Modules:
  0.0 181.0 jit_solution(16526544743140451668)
XLA Ops:
  0.6 0.7 copy.10
  1.3 0.0 copy-start.8
  1.3 0.0 copy-start.6
  1.3 0.0 copy-start.7
  1.3 0.0 copy-start.4
  1.3 3.1 %fusion.21 = bf16[2,9,128,256]{3,2,1,0:T(8,128)(2,1)S(1)} fusion(s32[2,9,128]{2,1,0:T(8,128)S(1)} %copy.10, bf16[1,1024,256]{2,1,0:T(8,128)(2,1)} %param.8), kind=kOutput, calls=%fused_computation.30 | convolution fusion | flops 1210908672 | bytes 1713152 | tf_op jit(solution)/shard_map/...v,vc->...c/dot_general | solution.py:283
  4.5 1.1 slice_bitcast_fusion.13
  5.6 4.9 %collective-permute-start = (bf16[9,128,256]{2,1,0:T(8,128)(2,1)}, bf16[9,128,256]{2,1,0:T(8,128)(2,1)}, u32[]{:S(2)}, u32[]{:S(2)}) collective-permute-start(bf16[9,128,256]{2,1,0:T(8,128)(2,1)} %get-tuple-element.4), channel_id=1, source_target_pairs={{0,1},{1,2},{2,3},{3,4},{4,5},{5,6},{6,7},{7,8},{8,9},{9,10},{10,1... | collective-permute-start | bytes 1769480 | tf_op jit(solution)/shard_map/ppermute | solution.py:262
  10.5 1.9 %collective-permute-start.1 = (bf16[9,128,256]{2,1,0:T(8,128)(2,1)}, bf16[9,128,256]{2,1,0:T(8,128)(2,1)}, u32[]{:S(2)}, u32[]{:S(2)}) collective-permute-start(bf16[9,128,256]{2,1,0:T(8,128)(2,1)} %get-tuple-element.5), channel_id=1, source_target_pairs={{1,0},{2,1},{3,2},{4,3},{5,4},{6,5},{7,6},{8,7},{9,8},{10,9},{11,1... | collective-permute-start | bytes 1769480 | tf_op jit(solution)/shard_map/ppermute | solution.py:262
  12.4 0.0 copy-done.8
  12.4 0.0 copy-done.6
  12.5 0.6 copy.23
  13.1 0.0 copy-done.7
  13.1 0.0 copy-done.4
  13.1 0.0 copy-start.1
  13.1 6.5 %fusion.18 = bf16[26,256,256]{2,1,0:T(8,128)(2,1)} fusion(s32[26,256]{1,0:T(8,128)S(1)} %bitcast.106, bf16[1,1024,256]{2,1,0:T(8,128)(2,1)S(1)} %copy-done.4), kind=kOutput, calls=%fused_computation.24 | convolution fusion | flops 3498180608 | bytes 3958784 | tf_op jit(solution)/shard_map/...v,vc->...c/dot_general | solution.py:283
  19.6 0.0 copy-done.1
  19.6 0.0 copy-start.9
  19.6 2.1 %fusion.71 = (bf16[13,256,256]{2,1,0:T(8,128)(2,1)}, bf16[13,256,256]{2,1,0:T(8,128)(2,1)}) fusion(bf16[27,256,256]{2,1,0:T(8,128)(2,1)S(1)} %copy-done.1), kind=kLoop, calls=%fused_computation.65 | loop fusion | bytes 6815744 | tf_op jit(solution)/shard_map/slice | solution.py:314
  21.7 0.0 copy-done.9
  21.7 3.7 %convolution_convert_fusion = bf16[2,9,128,256]{3,2,1,0:T(8,128)(2,1)} fusion(bf16[1,1024,256]{2,1,0:T(8,128)(2,1)S(1)} %copy-done.9, s32[2,9,128]{2,1,0:T(8,128)S(1)} %copy.9), kind=kOutput, calls=%fused_computation.29 | convolution fusion | flops 1210908672 | bytes 1713152 | tf_op jit(solution)/shard_map/...v,vc->...c/dot_general | solution.py:283
  25.4 10.3 %fusion.16 = f32[26,256,256]{2,1,0:T(8,128)} fusion(bf16[26,256,256]{2,1,0:T(8,128)(2,1)} %fusion.18, s32[26,256]{1,0:T(8,128)} %bitcast.104, bf16[1,1024,256]{2,1,0:T(8,128)(2,1)} %param.7), kind=kOutput, calls=%fused_computation.22 | convolution fusion | flops 4370595840 | bytes 10774528 | tf_op jit(solution)/shard_map/kpc,kpd->kcd/dot_general | solution.py:318
  35.7 0.0 copy-start.3
  35.7 2.4 %fusion.66 = f32[1024,256]{1,0:T(8,128)} fusion(bf16[1,1024,256]{2,1,0:T(8,128)(2,1)} %param.8, bf16[27,256,256]{2,1,0:T(8,128)(2,1)S(1)} %copy-done.1), kind=kOutput, calls=%fused_computation.58 | convolution fusion | flops 134217728 | bytes 1703936 | tf_op jit(solution)/shard_map/dot_general | solution.py:272
  38.2 0.0 copy-start
  38.2 2.8 %iota_compare_fusion.10 = pred[2,9,128,1024]{2,3,1,0:T(32,128)(4,1)} fusion(s32[2,9,128]{2,1,0:T(8,128)S(1)} %copy.9), kind=kLoop, calls=%fused_computation.12 | loop fusion | flops 2359296 | bytes 2368512 | tf_op jit(solution)/shard_map/eq | solution.py:279
  41.0 0.0 copy-start.5
  41.0 0.0 copy-start.10
  41.0 0.0 collective-permute-done.1
  41.0 0.0 copy-done.3
  41.0 3.9 %fusion.20 = f32[36,256,256]{2,1,0:T(8,128)} fusion(f32[26,256,256]{2,1,0:T(8,128)} %fusion.16, bf16[9,128,256]{2,1,0:T(8,128)(2,1)} %collective-permute-done.1, bf16[2,9,128,256]{3,2,1,0:T(8,128)(2,1)S(1)} %copy-done.3), kind=kOutput, calls=%fused_computation.28 | convolution fusion | flops 151584768 | bytes 5898240 | tf_op jit(solution)/shard_map/fbc,fbd->fcd/dot_general | solution.py:293
  44.9 0.0 copy-done
  44.9 1.0 slice_dynamic-update-slice_fusion.1
  45.9 0.0 copy-done.5
  45.9 0.0 copy-done.10
  45.9 1.0 fusion.58
  47.0 1.1 slice_dynamic-update-slice_fusion
  48.0 0.0 collective-permute-done
  48.0 3.0 %fusion.19 = f32[36,256,256]{2,1,0:T(8,128)} fusion(f32[36,256,256]{2,1,0:T(8,128)} %slice_dynamic-update-slice_fusion, f32[26,256,256]{2,1,0:T(8,128)S(1)} %copy-done, bf16[9,128,256]{2,1,0:T(8,128)(2,1)} %collective-permute-done, bf16[2,9,128,256]{3,2,1,0:T(8,128)(2,1)S(1)} %copy-done.3), kind=kOutput, calls=%fused_computation.26 | convolution fusion | flops 151584768 | bytes 5898240 | tf_op jit(solution)/shard_map/fbc,fbd->fcd/dot_general | solution.py:293
  51.1 1.7 broadcast_dynamic-update-slice_fusion
  52.8 101.1 %shard_map.86 = f32[9216,256]{1,0:T(8,128)} custom-call(f32[9216,256]{1,0:T(8,128)} %bitcast.23.x_ref), custom_call_target="tpu_custom_call" | custom-call | tf_op jit(solution)/shard_map/pallas_call | solution.py:222
  153.9 0.0 copy-start.2
  153.9 6.6 %slice.63 = f32[6912,256]{1,0:T(8,128)} slice(f32[9216,256]{1,0:T(8,128)} %shard_map.86), slice={[0:6912], [0:256]} | slice | bytes 14155776 | tf_op jit(solution)/shard_map/slice | solution.py:256
  160.5 0.0 copy-done.2
  160.5 3.7 %fusion.23 = f32[1024,256]{1,0:T(8,128)} fusion(pred[2,9,128,1024]{2,3,1,0:T(32,128)(4,1)} %iota_compare_fusion.10, bf16[9,128,256]{2,1,0:T(8,128)(2,1)} %collective-permute-done.1, bf16[27,256,256]{2,1,0:T(8,128)(2,1)S(1)} %copy-done.2), kind=kOutput, calls=%fused_computation.32 | convolution fusion | flops 755269632 | bytes 3997696 | tf_op jit(solution)/shard_map/fbv,fbc->vc/dot_general | solution.py:289
  164.2 3.7 %fusion.22 = f32[1024,256]{1,0:T(8,128)} fusion(pred[2,9,128,1024]{2,3,1,0:T(32,128)(4,1)} %iota_compare_fusion.10, bf16[9,128,256]{2,1,0:T(8,128)(2,1)} %collective-permute-done, bf16[27,256,256]{2,1,0:T(8,128)(2,1)S(1)} %copy-done.2), kind=kOutput, calls=%fused_computation.31 | convolution fusion | flops 755269632 | bytes 3997696 | tf_op jit(solution)/shard_map/fbv,fbc->vc/dot_general | solution.py:289
  167.8 13.1 %fusion.49 = bf16[1,1024,256]{2,1,0:T(8,128)(2,1)} fusion(f32[1024,256]{1,0:T(8,128)} %fusion.23, f32[1024,256]{1,0:T(8,128)} %fusion.22, f32[1024,256]{1,0:T(8,128)} %fusion.66, bf16[13,256,256]{2,1,0:T(8,128)(2,1)} %get-tuple-element.3, bf16[13,256,256]{2,1,0:T(8,128)(2,1)} %get-tuple-element.2, bf16[26,256,256]{2,1,0:T(8,128)(2,1)} %fusion.18, ...), kind=kOutput, calls=%fused_computation.40 | convolution fusion | flops 6995705856 | bytes 10512384 | tf_op jit(solution)/shard_map/vkd,kcd->vc/dot_general | solution.py:315
  (2 shorter events, 0.0 us)
Async XLA Ops:
  1.3 11.1 %copy-start.8 = (s32[1,1,2,9,128]{4,2,3,1,0:T(2,128)S(1)}, s32[1,1,2,9,128]{4,2,3,1,0:T(2,128)}, u32[]{:S(2)}) copy-start(s32[1,1,2,9,128]{4,2,3,1,0:T(2,128)} %param.13) | copy-start | bytes 27652
  1.3 11.1 %copy-start.6 = (s32[1,1,26,256]{3,1,2,0:T(1,128)S(1)}, s32[1,1,26,256]{3,1,2,0:T(1,128)}, u32[]{:S(2)}) copy-start(s32[1,1,26,256]{3,1,2,0:T(1,128)} %param.10) | copy-start | bytes 79876
  1.3 11.7 %copy-start.7 = (s32[1,1,26,256]{3,1,2,0:T(1,128)S(1)}, s32[1,1,26,256]{3,1,2,0:T(1,128)}, u32[]{:S(2)}) copy-start(s32[1,1,26,256]{3,1,2,0:T(1,128)} %param.11) | copy-start | bytes 79876
  1.3 11.7 %copy-start.4 = (bf16[1,1024,256]{2,1,0:T(8,128)(2,1)S(1)}, bf16[1,1024,256]{2,1,0:T(8,128)(2,1)}, u32[]{:S(2)}) copy-start(bf16[1,1024,256]{2,1,0:T(8,128)(2,1)} %param.8) | copy-start | bytes 1572868
  5.6 42.5 %collective-permute-start = (bf16[9,128,256]{2,1,0:T(8,128)(2,1)}, bf16[9,128,256]{2,1,0:T(8,128)(2,1)}, u32[]{:S(2)}, u32[]{:S(2)}) collective-permute-start(bf16[9,128,256]{2,1,0:T(8,128)(2,1)} %get-tuple-element.4), channel_id=1, source_target_pairs={{0,1},{1,2},{2,3},{3,4},{4,5},{5,6},{6,7},{7,8},{8,9},{9,10},{10,1... | collective-permute-start | bytes 1769480 | tf_op jit(solution)/shard_map/ppermute | solution.py:262
  10.5 30.5 %collective-permute-start.1 = (bf16[9,128,256]{2,1,0:T(8,128)(2,1)}, bf16[9,128,256]{2,1,0:T(8,128)(2,1)}, u32[]{:S(2)}, u32[]{:S(2)}) collective-permute-start(bf16[9,128,256]{2,1,0:T(8,128)(2,1)} %get-tuple-element.5), channel_id=1, source_target_pairs={{1,0},{2,1},{3,2},{4,3},{5,4},{6,5},{7,6},{8,7},{9,8},{10,9},{11,1... | collective-permute-start | bytes 1769480 | tf_op jit(solution)/shard_map/ppermute | solution.py:262
  13.1 6.6 %copy-start.1 = (bf16[27,256,256]{2,1,0:T(8,128)(2,1)S(1)}, bf16[27,256,256]{2,1,0:T(8,128)(2,1)}, u32[]{:S(2)}) copy-start(bf16[27,256,256]{2,1,0:T(8,128)(2,1)} %param.9) | copy-start | bytes 10616836
  19.6 2.1 %copy-start.9 = (bf16[1,1024,256]{2,1,0:T(8,128)(2,1)S(1)}, bf16[1,1024,256]{2,1,0:T(8,128)(2,1)}, u32[]{:S(2)}) copy-start(bf16[1,1024,256]{2,1,0:T(8,128)(2,1)} %param.7) | copy-start | bytes 1572868
  35.7 5.3 %copy-start.3 = (bf16[2,9,128,256]{3,2,1,0:T(8,128)(2,1)S(1)}, bf16[2,9,128,256]{3,2,1,0:T(8,128)(2,1)}, u32[]{:S(2)}) copy-start(bf16[2,9,128,256]{3,2,1,0:T(8,128)(2,1)} %convolution_convert_fusion) | copy-start | bytes 3538948
  38.2 6.7 %copy-start = (f32[26,256,256]{2,1,0:T(8,128)S(1)}, f32[26,256,256]{2,1,0:T(8,128)}, u32[]{:S(2)}) copy-start(f32[26,256,256]{2,1,0:T(8,128)} %fusion.16) | copy-start | bytes 20447236
  41.0 5.0 %copy-start.5 = (bf16[1,1024,256]{2,1,0:T(8,128)(2,1)S(1)}, bf16[1,1024,256]{2,1,0:T(8,128)(2,1)}, u32[]{:S(2)}) copy-start(bf16[1,1024,256]{2,1,0:T(8,128)(2,1)} %param.8) | copy-start | bytes 1572868
  41.0 5.0 %copy-start.10 = (bf16[1,1024,256]{2,1,0:T(8,128)(2,1)S(1)}, bf16[1,1024,256]{2,1,0:T(8,128)(2,1)}, u32[]{:S(2)}) copy-start(bf16[1,1024,256]{2,1,0:T(8,128)(2,1)} %param.7) | copy-start | bytes 1572868
  153.9 6.6 %copy-start.2 = (bf16[27,256,256]{2,1,0:T(8,128)(2,1)S(1)}, bf16[27,256,256]{2,1,0:T(8,128)(2,1)}, u32[]{:S(2)}) copy-start(bf16[27,256,256]{2,1,0:T(8,128)(2,1)} %param.9) | copy-start | bytes 10616836

commit v8 on v6

--- a/solution.py
+++ b/solution.py
@@ -46,10 +46,19 @@
     lax.fori_loop(0, rows // slab, body, 0)
 
 
-def allreduce_kernel(scale, x_ref, out_ref, rcore, part, r1, p1, r2, p2, r3, red,
+def allreduce_kernel(scale, x_ref, placed_ref, kmat_ref, out_ref, side_ref, rcore, part, r1, p1, r2, p2, r3, red,
                      core_send, core_recv, rs_send, rs_recv, ag_send, ag_recv, agc_send, agc_recv, out_sem):
     at = coords_here()
     half = COLOR_ROWS // 2
+
+    def side_part(j0, j1):
+        for j in range(j0, j1):
+            term = jnp.dot(placed_ref[:, j * 256:(j + 1) * 256], kmat_ref[j * 256:(j + 1) * 256, :],
+                           preferred_element_type=jnp.float32)
+            if j == 0:
+                side_ref[...] = term
+            else:
+                side_ref[...] += term
     barrier = pltpu.get_barrier_semaphore()
     peers = [peer_of(at, "core", 1)] + [peer_of(at, d, s) for d in ("z", "y", "x") for s in (1, 2, 3)]
     for p in peers:
@@ -65,6 +74,7 @@
             device_id=peer_of(at, "core", 1), device_id_type=MESH_IDS)
         cp.start()
         copies.append(cp)
+    side_part(0, 4)
     sources = (part, p1, p2)
     recvs = (r1, r2, r3)
     blocks = (COLOR_ROWS // 8, COLOR_ROWS // 32, COLOR_ROWS // 128)
@@ -120,6 +130,7 @@
         staged[k] = scatter_sends(0, k)
     for stage in range(3):
         blk, src, rbuf = blocks[stage], sources[stage], recvs[stage]
+        side_part(4 + 4 * stage, 8 + 4 * stage)
         for k in range(3):
             for cp in staged[k]:
                 cp.wait()
@@ -143,15 +154,17 @@
                 put.wait()
                 staged[k] = gather_sends(0, k)
     for step in range(3):
+        side_part(16 + 3 * step, 19 + 3 * step)
         for k in range(3):
             for cp in staged[k]:
                 cp.wait()
             staged[k] = gather_sends(step + 1, k) if step < 2 else [pair_send(k)]
+    side_part(25, 26)
     for k in range(3):
         for cp in staged[k]:
             cp.wait()
 
-def summed_everywhere(stacked, scale):
+def summed_everywhere(stacked, scale, placed, kmat):
     rows = PAD_OFFSETS * 256
     width = stacked.shape[2]
     data = jnp.concatenate(
@@ -159,11 +172,12 @@
     ).reshape(rows, width)
     f32 = jnp.float32
     blocks = (COLOR_ROWS // 8, COLOR_ROWS // 32, COLOR_ROWS // 128)
-    total = pl.pallas_call(
+    total, side = pl.pallas_call(
         functools.partial(allreduce_kernel, scale),
-        out_shape=jax.ShapeDtypeStruct((rows, width), f32),
-        in_specs=[pl.BlockSpec(memory_space=pltpu.VMEM)],
-        out_specs=pl.BlockSpec(memory_space=pl.ANY),
+        out_shape=(jax.ShapeDtypeStruct((rows, width), f32),
+                   jax.ShapeDtypeStruct((placed.shape[0], kmat.shape[1]), f32)),
+        in_specs=[pl.BlockSpec(memory_space=pltpu.VMEM)] * 3,
+        out_specs=(pl.BlockSpec(memory_space=pl.ANY), pl.BlockSpec(memory_space=pltpu.VMEM)),
         scratch_shapes=[
             pltpu.VMEM((3, COLOR_ROWS // 2, width), f32),
             pltpu.VMEM((3, COLOR_ROWS // 2, width), f32),
@@ -186,8 +200,8 @@
         compiler_params=pltpu.CompilerParams(
             collective_id=0, has_side_effects=True, vmem_limit_bytes=64 * 1024 * 1024
         ),
-    )(data)
-    return total[: stacked.shape[0] * stacked.shape[1]].reshape(stacked.shape)
+    )(data, placed, kmat)
+    return total[: stacked.shape[0] * stacked.shape[1]].reshape(stacked.shape), side
 
 
 def passed_along(array, axis, by):
@@ -246,9 +260,8 @@
         "kpv,kpc->vkc", table_in, gathered_g, preferred_element_type=jnp.float32
     ).astype(jnp.bfloat16)
     side_kernels = jnp.concatenate([weight[0:13], weight[14:27]], 0)
-    accumulated = accumulated + jnp.einsum(
-        "vkd,kcd->vc", placed, side_kernels, preferred_element_type=jnp.float32
-    )
+    kmat = jnp.swapaxes(side_kernels, 1, 2).reshape(-1, side_kernels.shape[1])
+    placed = placed.reshape(placed.shape[0], -1)
     offset_grads = jnp.einsum(
         "kpc,kpd->kcd", gathered_x, gathered_g, preferred_element_type=jnp.float32
     )
@@ -275,7 +288,8 @@
         0,
     )
     loss_scale = 1.0 / math.sqrt(pairs * lax.axis_size("dp") * lax.axis_size("region"))
-    grad_weight = summed_everywhere(stacked, loss_scale)
+    grad_weight, side = summed_everywhere(stacked, loss_scale, placed, kmat)
+    accumulated = accumulated + side
     grad_input = accumulated.astype(jnp.bfloat16)[None]
     return (grad_input, grad_weight)
 

time: 166 us -> 193 us (1.16)
  local copies, waits for them, and re-layouts: 14.9 us -> 36.1 us
  Pallas kernels: 85.3 us -> 91.7 us
    reshape x0 -> x1, local copies, waits for them, and re-layouts: none -> 17.6 us  [per_device(): placed = placed.reshape(placed.shape[0], -1)]
    pallas_call x1, Pallas kernels: 85.3 us -> 91.7 us  [summed_everywhere(): pl.pallas_call(functools.partial(allreduce_kernel, scale), out_shape=(jax...]
    transpose x0 -> x1, local copies, waits for them, and re-layouts: none -> 3.56 us  [per_device(): kmat = jnp.swapaxes(side_kernels, 1, 2).reshape(-1, side_kernels.shape[1])]
    unnamed x26, local copies, waits for them, and re-layouts: 2.76 us -> 4.77 us
    dot_general x1, matrix products: 13.1 us -> 11.2 us  [per_device(): jnp.einsum('kpv,kpc->vkc', table_in, gathered_g, preferred_element_type=j...]
  transfers between devices with their start and end apart: 2 -> 2, of which waited for: 0 -> 0; matrix products, arithmetic and copies ran while one was open for 22% -> 34% of each run, Pallas kernels for 0% -> 0%
where the time goes in v8:
time: 193 us
  Pallas kernels  91.7 us (48%)
  matrix products  53.2 us (28%)
  local copies, waits for them, and re-layouts  36.1 us (19%)
  starting transfers between devices  6.83 us (4%)
  other arithmetic  4.05 us (2%)
    pallas_call x1, Pallas kernels, summed_everywhere(): pl.pallas_call(functools.partial(allreduce_kernel, scale), out_shape=(jax...  91.7 us
    reshape x1, local copies, waits for them, and re-layouts, per_device(): placed = placed.reshape(placed.shape[0], -1)  17.6 us
    dot_general x3, matrix products, pick_rows(): jnp.einsum('...v,vc->...c', table, source, preferred_element_type=jnp.flo...  13.3 us
    dot_general x1, matrix products, per_device(): jnp.einsum('kpv,kpc->vkc', table_in, gathered_g, preferred_element_type=j...  11.2 us
    dot_general x1, matrix products, per_device(): jnp.einsum('kpc,kpd->kcd', gathered_x, gathered_g, preferred_element_type...  10.2 us
    dot_general x2, matrix products, face_products(): jnp.einsum('fbc,fbd->fcd', features, grads, preferred_element_type=jnp.fl...  8 us
    dot_general x2, matrix products, place_rows(): jnp.einsum('fbv,fbc->vc', table, rows, preferred_element_type=jnp.float32)  7.33 us
    ppermute x2, starting transfers between devices, passed_along(): return lax.ppermute(array, axis, pairs)  6.83 us
  transfers between devices with their start and end apart: 2, of which 0 were waited for; matrix products, arithmetic and copies ran while one was open for 34% of the time, Pallas kernels for 0%

profile of v8, /device:TPU:1, one launch (start us, length us, event | category | flops | bytes accessed | tf_op | source)
XLA Modules:
  0.0 192.6 jit_solution(6661634728313684699)
XLA Ops:
  0.6 0.7 copy.18
  1.3 0.0 copy-start.8
  1.3 0.0 copy-start.6
  1.3 0.0 copy-start.4
  1.3 3.1 %fusion.16 = bf16[2,9,128,256]{3,2,1,0:T(8,128)(2,1)S(1)} fusion(s32[2,9,128]{2,1,0:T(8,128)S(1)} %copy.18, bf16[1,1024,256]{2,1,0:T(8,128)(2,1)} %param.8), kind=kOutput, calls=%fused_computation.26 | convolution fusion | flops 1210908672 | bytes 1713152 | tf_op jit(solution)/shard_map/...v,vc->...c/dot_general | solution.py:231
  4.5 1.1 slice_bitcast_fusion.13
  5.6 3.3 %collective-permute-start.1 = (bf16[9,128,256]{2,1,0:T(8,128)(2,1)}, bf16[9,128,256]{2,1,0:T(8,128)(2,1)}, u32[]{:S(2)}, u32[]{:S(2)}) collective-permute-start(bf16[9,128,256]{2,1,0:T(8,128)(2,1)} %get-tuple-element.9), channel_id=1, source_target_pairs={{1,0},{2,1},{3,2},{4,3},{5,4},{6,5},{7,6},{8,7},{9,8},{10,9},{11,1... | collective-permute-start | bytes 1769480 | tf_op jit(solution)/shard_map/ppermute | solution.py:210
  8.8 3.6 %collective-permute-start = (bf16[9,128,256]{2,1,0:T(8,128)(2,1)}, bf16[9,128,256]{2,1,0:T(8,128)(2,1)}, u32[]{:S(2)}, u32[]{:S(2)}) collective-permute-start(bf16[9,128,256]{2,1,0:T(8,128)(2,1)} %get-tuple-element.8), channel_id=1, source_target_pairs={{0,1},{1,2},{2,3},{3,4},{4,5},{5,6},{6,7},{7,8},{8,9},{9,10},{10,1... | collective-permute-start | bytes 1769480 | tf_op jit(solution)/shard_map/ppermute | solution.py:210
  12.4 0.0 copy-done.8
  12.4 0.0 copy-done.6
  12.4 0.0 copy-done.4
  12.5 0.0 copy-start.7
  12.5 6.5 %fusion.13 = bf16[26,256,256]{2,1,0:T(8,128)(2,1)} fusion(s32[26,256]{1,0:T(8,128)S(1)} %bitcast.87, bf16[1,1024,256]{2,1,0:T(8,128)(2,1)S(1)} %copy-done.4), kind=kOutput, calls=%fused_computation.20 | convolution fusion | flops 3498180608 | bytes 3958784 | tf_op jit(solution)/shard_map/...v,vc->...c/dot_general | solution.py:231
  19.0 0.0 copy-done.7
  19.0 0.0 copy-start.9
  19.0 11.2 %fusion.6 = bf16[26,256,1024]{2,1,0:T(8,128)(2,1)} fusion(bf16[26,256,256]{2,1,0:T(8,128)(2,1)} %fusion.13, s32[26,256]{1,0:T(8,128)S(1)} %bitcast.85), kind=kOutput, calls=%fused_computation.8 | convolution fusion | flops 3503292416 | bytes 17065984 | tf_op jit(solution)/shard_map/kpv,kpc->vkc/dot_general | solution.py:259
  30.2 0.0 copy-done.9
  30.2 10.2 %fusion.11 = f32[26,256,256]{2,1,0:T(8,128)} fusion(bf16[26,256,256]{2,1,0:T(8,128)(2,1)} %fusion.13, s32[26,256]{1,0:T(8,128)S(1)} %bitcast.86, bf16[1,1024,256]{2,1,0:T(8,128)(2,1)S(1)} %copy-done.9), kind=kOutput, calls=%fused_computation.18 | convolution fusion | flops 4370595840 | bytes 10774528 | tf_op jit(solution)/shard_map/kpc,kpd->kcd/dot_general | solution.py:265
  40.3 0.0 copy-start
  40.4 3.7 %convolution_convert_fusion = bf16[2,9,128,256]{3,2,1,0:T(8,128)(2,1)} fusion(bf16[1,1024,256]{2,1,0:T(8,128)(2,1)S(1)} %copy-done.9, s32[2,9,128]{2,1,0:T(8,128)S(1)} %copy.17), kind=kOutput, calls=%fused_computation.25 | convolution fusion | flops 1210908672 | bytes 1713152 | tf_op jit(solution)/shard_map/...v,vc->...c/dot_general | solution.py:231
  44.0 0.0 copy-done
  44.0 0.2 fusion.36
  44.3 0.3 maximum_bitcast_fusion
  44.6 17.6 %copy.24.placed_ref = bf16[1024,6656]{1,0:T(8,128)(2,1)} copy(bf16[1024,6656]{0,1:T(8,128)(2,1)} %bitcast.83) | data formatting | bytes 27262976 | tf_op jit(solution)/shard_map/reshape | solution.py:264
  62.1 3.6 %copy.23 = bf16[26,256,256]{2,1,0:T(8,128)(2,1)} copy(bf16[26,256,256]{1,2,0:T(8,128)(2,1)S(1)} %maximum_bitcast_fusion) | data formatting | bytes 6815744 | tf_op jit(solution)/shard_map/transpose | solution.py:263
  65.7 2.9 %iota_compare_fusion.8 = pred[2,9,128,1024]{2,3,1,0:T(32,128)(4,1)} fusion(s32[2,9,128]{2,1,0:T(8,128)S(1)} %copy.17), kind=kLoop, calls=%fused_computation.10 | loop fusion | flops 2359296 | bytes 2368512 | tf_op jit(solution)/shard_map/eq | solution.py:227
  68.5 0.0 copy-start.10
  68.5 0.0 collective-permute-done.1
  68.6 4.1 %fusion.15 = f32[36,256,256]{2,1,0:T(8,128)} fusion(f32[26,256,256]{2,1,0:T(8,128)} %fusion.11, bf16[9,128,256]{2,1,0:T(8,128)(2,1)} %collective-permute-done.1, bf16[2,9,128,256]{3,2,1,0:T(8,128)(2,1)} %convolution_convert_fusion), kind=kOutput, calls=%fused_computation.24 | convolution fusion | flops 151584768 | bytes 5898240 | tf_op jit(solution)/shard_map/fbc,fbd->fcd/dot_general | solution.py:241
  72.7 0.0 copy-start.2
  72.7 2.4 %slice_dynamic-update-slice_fusion.1 = f32[36,256,256]{2,1,0:T(8,128)} fusion(f32[36,256,256]{2,1,0:T(8,128)} %fusion.15, f32[26,256,256]{2,1,0:T(8,128)} %fusion.11), kind=kLoop, calls=%fused_computation.39 | loop fusion | bytes 2097152
  75.1 0.0 copy-done.5
  75.1 0.0 copy-done.10
  75.1 1.1 fusion.24
  76.2 2.3 %slice_dynamic-update-slice_fusion = f32[36,256,256]{2,1,0:T(8,128)} fusion(f32[36,256,256]{2,1,0:T(8,128)} %fusion.24, f32[26,256,256]{2,1,0:T(8,128)} %fusion.11), kind=kLoop, calls=%fused_computation.38 | loop fusion | bytes 2097152
  78.4 0.0 collective-permute-done
  78.4 0.0 copy-done.2
  78.4 3.9 %fusion.14 = f32[36,256,256]{2,1,0:T(8,128)} fusion(f32[36,256,256]{2,1,0:T(8,128)} %slice_dynamic-update-slice_fusion, f32[26,256,256]{2,1,0:T(8,128)} %fusion.11, bf16[9,128,256]{2,1,0:T(8,128)(2,1)} %collective-permute-done, bf16[2,9,128,256]{3,2,1,0:T(8,128)(2,1)S(1)} %copy-done.2), kind=kOutput, calls=%fused_computation.22 | convolution fusion | flops 151584768 | bytes 5898240 | tf_op jit(solution)/shard_map/fbc,fbd->fcd/dot_general | solution.py:241
  82.3 1.6 broadcast_dynamic-update-slice_fusion
  83.9 91.7 %shard_map.86 = (f32[9216,256]{1,0:T(8,128)}, f32[1024,256]{1,0:T(8,128)}) custom-call(f32[9216,256]{1,0:T(8,128)} %bitcast.20.x_ref, bf16[1024,6656]{1,0:T(8,128)(2,1)} %copy.24.placed_ref, bf16[6656,256]{1,0:T(8,128)(2,1)} %bitcast.82), custom_call_target="tpu_custom_call" | custom-call | tf_op jit(solution)/shard_map/pallas_call | solution.py:175
  175.6 0.0 copy-start.1
  175.6 6.6 %slice.63 = f32[6912,256]{1,0:T(8,128)} slice(f32[9216,256]{1,0:T(8,128)} %get-tuple-element.5), slice={[0:6912], [0:256]} | slice | bytes 14155776 | tf_op jit(solution)/shard_map/slice | solution.py:204
  182.2 0.0 copy-done.1
  182.2 3.7 %fusion.18 = f32[1024,256]{1,0:T(8,128)} fusion(pred[2,9,128,1024]{2,3,1,0:T(32,128)(4,1)} %iota_compare_fusion.8, bf16[9,128,256]{2,1,0:T(8,128)(2,1)} %collective-permute-done.1, bf16[27,256,256]{2,1,0:T(8,128)(2,1)S(1)} %copy-done.1), kind=kOutput, calls=%fused_computation.28 | convolution fusion | flops 755269632 | bytes 3997696 | tf_op jit(solution)/shard_map/fbv,fbc->vc/dot_general | solution.py:237
  185.9 3.7 %fusion.17 = f32[1024,256]{1,0:T(8,128)} fusion(pred[2,9,128,1024]{2,3,1,0:T(32,128)(4,1)} %iota_compare_fusion.8, bf16[9,128,256]{2,1,0:T(8,128)(2,1)} %collective-permute-done, bf16[27,256,256]{2,1,0:T(8,128)(2,1)S(1)} %copy-done.1), kind=kOutput, calls=%fused_computation.27 | convolution fusion | flops 755269632 | bytes 3997696 | tf_op jit(solution)/shard_map/fbv,fbc->vc/dot_general | solution.py:237
  189.6 2.1 %fusion.19 = f32[1024,256]{1,0:T(8,128)S(1)} fusion(f32[1024,256]{1,0:T(8,128)} %fusion.18, f32[1024,256]{1,0:T(8,128)} %fusion.17, bf16[1,1024,256]{2,1,0:T(8,128)(2,1)} %param.8, bf16[27,256,256]{2,1,0:T(8,128)(2,1)S(1)} %copy-done.1), kind=kOutput, calls=%fused_computation.30 | convolution fusion | flops 134742016 | bytes 3801088 | tf_op jit(solution)/shard_map/dot_general | solution.py:220
  191.7 0.0 copy-done.3
  191.7 0.9 fusion.25
  (5 shorter events, 0.0 us)
Async XLA Ops:
  1.3 11.1 %copy-start.8 = (s32[1,1,2,9,128]{4,2,3,1,0:T(2,128)S(1)}, s32[1,1,2,9,128]{4,2,3,1,0:T(2,128)}, u32[]{:S(2)}) copy-start(s32[1,1,2,9,128]{4,2,3,1,0:T(2,128)} %param.13) | copy-start | bytes 27652
  1.3 11.1 %copy-start.6 = (s32[1,1,26,256]{3,1,2,0:T(1,128)S(1)}, s32[1,1,26,256]{3,1,2,0:T(1,128)}, u32[]{:S(2)}) copy-start(s32[1,1,26,256]{3,1,2,0:T(1,128)} %param.11) | copy-start | bytes 79876
  1.3 11.1 %copy-start.4 = (bf16[1,1024,256]{2,1,0:T(8,128)(2,1)S(1)}, bf16[1,1024,256]{2,1,0:T(8,128)(2,1)}, u32[]{:S(2)}) copy-start(bf16[1,1024,256]{2,1,0:T(8,128)(2,1)} %param.8) | copy-start | bytes 1572868
  5.6 63.0 %collective-permute-start.1 = (bf16[9,128,256]{2,1,0:T(8,128)(2,1)}, bf16[9,128,256]{2,1,0:T(8,128)(2,1)}, u32[]{:S(2)}, u32[]{:S(2)}) collective-permute-start(bf16[9,128,256]{2,1,0:T(8,128)(2,1)} %get-tuple-element.9), channel_id=1, source_target_pairs={{1,0},{2,1},{3,2},{4,3},{5,4},{6,5},{7,6},{8,7},{9,8},{10,9},{11,1... | collective-permute-start | bytes 1769480 | tf_op jit(solution)/shard_map/ppermute | solution.py:210
  8.8 69.6 %collective-permute-start = (bf16[9,128,256]{2,1,0:T(8,128)(2,1)}, bf16[9,128,256]{2,1,0:T(8,128)(2,1)}, u32[]{:S(2)}, u32[]{:S(2)}) collective-permute-start(bf16[9,128,256]{2,1,0:T(8,128)(2,1)} %get-tuple-element.8), channel_id=1, source_target_pairs={{0,1},{1,2},{2,3},{3,4},{4,5},{5,6},{6,7},{7,8},{8,9},{9,10},{10,1... | collective-permute-start | bytes 1769480 | tf_op jit(solution)/shard_map/ppermute | solution.py:210
  12.5 6.5 %copy-start.7 = (s32[1,1,26,256]{3,1,2,0:T(1,128)S(1)}, s32[1,1,26,256]{3,1,2,0:T(1,128)}, u32[]{:S(2)}) copy-start(s32[1,1,26,256]{3,1,2,0:T(1,128)} %param.10) | copy-start | bytes 79876
  19.0 11.2 %copy-start.9 = (bf16[1,1024,256]{2,1,0:T(8,128)(2,1)S(1)}, bf16[1,1024,256]{2,1,0:T(8,128)(2,1)}, u32[]{:S(2)}) copy-start(bf16[1,1024,256]{2,1,0:T(8,128)(2,1)} %param.7) | copy-start | bytes 1572868
  40.3 3.7 %copy-start = (bf16[27,256,256]{2,1,0:T(8,128)(2,1)S(1)}, bf16[27,256,256]{2,1,0:T(8,128)(2,1)}, u32[]{:S(2)}) copy-start(bf16[27,256,256]{2,1,0:T(8,128)(2,1)} %param.9) | copy-start | bytes 10616836
  68.5 6.6 %copy-start.5 = (bf16[1,1024,256]{2,1,0:T(8,128)(2,1)S(1)}, bf16[1,1024,256]{2,1,0:T(8,128)(2,1)}, u32[]{:S(2)}) copy-start(bf16[1,1024,256]{2,1,0:T(8,128)(2,1)} %param.8) | copy-start | bytes 1572868
  68.5 6.6 %copy-start.10 = (bf16[1,1024,256]{2,1,0:T(8,128)(2,1)S(1)}, bf16[1,1024,256]{2,1,0:T(8,128)(2,1)}, u32[]{:S(2)}) copy-start(bf16[1,1024,256]{2,1,0:T(8,128)(2,1)} %param.7) | copy-start | bytes 1572868
  72.7 5.8 %copy-start.2 = (bf16[2,9,128,256]{3,2,1,0:T(8,128)(2,1)S(1)}, bf16[2,9,128,256]{3,2,1,0:T(8,128)(2,1)}, u32[]{:S(2)}) copy-start(bf16[2,9,128,256]{3,2,1,0:T(8,128)(2,1)} %convolution_convert_fusion) | copy-start | bytes 3538948
  175.6 6.6 %copy-start.1 = (bf16[27,256,256]{2,1,0:T(8,128)(2,1)S(1)}, bf16[27,256,256]{2,1,0:T(8,128)(2,1)}, u32[]{:S(2)}) copy-start(bf16[27,256,256]{2,1,0:T(8,128)(2,1)} %param.9) | copy-start | bytes 10616836
  189.6 2.1 %copy-start.3 = (f32[1024,256]{1,0:T(8,128)S(1)}, f32[1024,256]{1,0:T(8,128)}, u32[]{:S(2)}) copy-start(f32[1024,256]{1,0:T(8,128)} %get-tuple-element.4) | copy-start | bytes 3145732

commit v9 on v6

--- a/solution.py
+++ b/solution.py
@@ -34,6 +34,17 @@
     return (x, (y * 4 + z) * 2 + c)
 
 
+def peer_multi(at, shifts):
+    x, y, z, c = at["x"], at["y"], at["z"], at["core"]
+    x = (x + shifts.get("x", 0)) % 4
+    y = (y + shifts.get("y", 0)) % 4
+    z = (z + shifts.get("z", 0)) % 4
+    return (x, (y * 4 + z) * 2 + c)
+
+
+PLANE_SHIFTS = [(sb, se) for sb in range(4) for se in range(4) if (sb, se) != (0, 0)]
+
+
 def add_rows(dst, first, others, rows, slab):
     def body(i, carry):
         at = pl.ds(pl.multiple_of(i * slab, slab), slab)
@@ -46,12 +57,20 @@
     lax.fori_loop(0, rows // slab, body, 0)
 
 
-def allreduce_kernel(scale, x_ref, out_ref, rcore, part, r1, p1, r2, p2, r3, red,
-                     core_send, core_recv, rs_send, rs_recv, ag_send, ag_recv, agc_send, agc_recv, out_sem):
+def allreduce_kernel(scale, x_ref, out_ref, rcore, part, r1, p1, r2, p2, r3, red, r23,
+                     core_send, core_recv, rs_send, rs_recv, ag_send, ag_recv, agc_send, agc_recv, out_sem,
+                     pl_send, pl_recv, pg_send, pg_recv):
     at = coords_here()
     half = COLOR_ROWS // 2
     barrier = pltpu.get_barrier_semaphore()
-    peers = [peer_of(at, "core", 1)] + [peer_of(at, d, s) for d in ("z", "y", "x") for s in (1, 2, 3)]
+    shift_sets = {(("x", 0), ("y", 0), ("z", 0))}
+    for order in COLOR_ORDERS:
+        for s in (1, 2, 3):
+            shift_sets.add(tuple(sorted({"x": 0, "y": 0, "z": 0, order[0]: s}.items())))
+        for sb, se in PLANE_SHIFTS:
+            shift_sets.add(tuple(sorted({"x": 0, "y": 0, "z": 0, order[1]: sb, order[2]: se}.items())))
+    shift_sets.discard((("x", 0), ("y", 0), ("z", 0)))
+    peers = [peer_of(at, "core", 1)] + [peer_multi(at, dict(s)) for s in sorted(shift_sets)]
     for p in peers:
         pl.semaphore_signal(barrier, inc=1, device_id=p, device_id_type=MESH_IDS)
     pl.semaphore_wait(barrier, len(peers))
@@ -110,6 +129,34 @@
         cp.start()
         return cp
 
+    def plane_sends(k):
+        a, b, e = ranks[k]
+        order = COLOR_ORDERS[k]
+        row = []
+        for slot, (sb, se) in enumerate(PLANE_SHIFTS):
+            chunk = ((b + sb) % 4) * 4 + (e + se) % 4
+            cp = pltpu.make_async_remote_copy(
+                src_ref=p1.at[k, pl.ds(pl.multiple_of(chunk * CHUNK_ROWS, 8), CHUNK_ROWS)],
+                dst_ref=r23.at[k, slot], send_sem=pl_send.at[k, slot], recv_sem=pl_recv.at[k, slot],
+                device_id=peer_multi(at, {order[1]: sb, order[2]: se}), device_id_type=MESH_IDS)
+            cp.start()
+            row.append(cp)
+        return row
+
+    def plane_gather(k):
+        a, b, e = ranks[k]
+        order = COLOR_ORDERS[k]
+        pos = pl.multiple_of(k * COLOR_ROWS + (c * 64 + a * 16 + b * 4 + e) * CHUNK_ROWS, 8)
+        row = []
+        for slot, (sb, se) in enumerate(PLANE_SHIFTS):
+            cp = pltpu.make_async_remote_copy(
+                src_ref=out_ref.at[pl.ds(pos, CHUNK_ROWS)], dst_ref=out_ref.at[pl.ds(pos, CHUNK_ROWS)],
+                send_sem=pg_send.at[k, slot], recv_sem=pg_recv.at[k, slot],
+                device_id=peer_multi(at, {order[1]: sb, order[2]: se}), device_id_type=MESH_IDS)
+            cp.start()
+            row.append(cp)
+        return row
+
     staged = [None] * 3
     for k in range(3):
         copies[k].wait()
@@ -118,35 +165,38 @@
                  lambda a, base=base: x_ref[pl.ds(pl.multiple_of(base, 8) + a.start, a.size)],
                  [lambda a, k=k: rcore[k, a]], half, 128)
         staged[k] = scatter_sends(0, k)
-    for stage in range(3):
-        blk, src, rbuf = blocks[stage], sources[stage], recvs[stage]
-        for k in range(3):
-            for cp in staged[k]:
-                cp.wait()
-            me = ranks[k][stage]
-            own = pl.multiple_of(me * blk, 8)
-            others = [lambda a, k=k, j=j, rbuf=rbuf: rbuf[k, j, a] for j in range(3)]
-            first = lambda a, k=k, own=own, src=src: src[k, pl.ds(own + a.start, a.size)]
-            if stage == 0:
-                add_rows(lambda a, v, k=k: p1.__setitem__((k, a), v), first, others, blk, 128)
-                staged[k] = scatter_sends(1, k)
-            elif stage == 1:
-                add_rows(lambda a, v, k=k: p2.__setitem__((k, a), v), first, others, blk, blk)
-                staged[k] = scatter_sends(2, k)
-            else:
-                total = first(pl.ds(0, blk)) + others[0](pl.ds(0, blk)) + others[1](pl.ds(0, blk)) + others[2](pl.ds(0, blk))
-                a, b, e = ranks[k]
-                pos = pl.multiple_of(k * COLOR_ROWS + (c * 64 + a * 16 + b * 4 + e) * CHUNK_ROWS, 8)
-                red[k] = total * scale
-                put = pltpu.make_async_copy(red.at[k], out_ref.at[pl.ds(pos, blk)], out_sem.at[k])
-                put.start()
-                put.wait()
-                staged[k] = gather_sends(0, k)
-    for step in range(3):
-        for k in range(3):
-            for cp in staged[k]:
-                cp.wait()
-            staged[k] = gather_sends(step + 1, k) if step < 2 else [pair_send(k)]
+    blk = blocks[0]
+    for k in range(3):
+        for cp in staged[k]:
+            cp.wait()
+        me = ranks[k][0]
+        own = pl.multiple_of(me * blk, 8)
+        others = [lambda a, k=k, j=j: r1[k, j, a] for j in range(3)]
+        first = lambda a, k=k, own=own: part[k, pl.ds(own + a.start, a.size)]
+        add_rows(lambda a, v, k=k: p1.__setitem__((k, a), v), first, others, blk, 128)
+        staged[k] = plane_sends(k)
+    for k in range(3):
+        for cp in staged[k]:
+            cp.wait()
+        a, b, e = ranks[k]
+        mine = pl.multiple_of((b * 4 + e) * CHUNK_ROWS, 8)
+        total = p1[k, pl.ds(mine, CHUNK_ROWS)]
+        for slot in range(len(PLANE_SHIFTS)):
+            total = total + r23[k, slot]
+        pos = pl.multiple_of(k * COLOR_ROWS + (c * 64 + a * 16 + b * 4 + e) * CHUNK_ROWS, 8)
+        red[k] = total * scale
+        put = pltpu.make_async_copy(red.at[k], out_ref.at[pl.ds(pos, CHUNK_ROWS)], out_sem.at[k])
+        put.start()
+        put.wait()
+        staged[k] = plane_gather(k)
+    for k in range(3):
+        for cp in staged[k]:
+            cp.wait()
+        staged[k] = gather_sends(2, k)
+    for k in range(3):
+        for cp in staged[k]:
+            cp.wait()
+        staged[k] = [pair_send(k)]
     for k in range(3):
         for cp in staged[k]:
             cp.wait()
@@ -173,6 +223,7 @@
             pltpu.VMEM((3, blocks[1], width), f32),
             pltpu.VMEM((3, 3, blocks[2], width), f32),
             pltpu.VMEM((3, blocks[2], width), f32),
+            pltpu.VMEM((3, 15, CHUNK_ROWS, width), f32),
             pltpu.SemaphoreType.DMA((3,)),
             pltpu.SemaphoreType.DMA((3,)),
             pltpu.SemaphoreType.DMA((3, 3, 3)),
@@ -182,6 +233,10 @@
             pltpu.SemaphoreType.DMA((3,)),
             pltpu.SemaphoreType.DMA((3,)),
             pltpu.SemaphoreType.DMA((3,)),
+            pltpu.SemaphoreType.DMA((3, 15)),
+            pltpu.SemaphoreType.DMA((3, 15)),
+            pltpu.SemaphoreType.DMA((3, 15)),
+            pltpu.SemaphoreType.DMA((3, 15)),
         ],
         compiler_params=pltpu.CompilerParams(
             collective_id=0, has_side_effects=True, vmem_limit_bytes=64 * 1024 * 1024

time: 166 us -> 170 us (1.024)
  Pallas kernels: 85.3 us -> 90.2 us
    pallas_call x1, Pallas kernels: 85.3 us -> 90.2 us  [summed_everywhere(): pl.pallas_call(functools.partial(allreduce_kernel, scale), out_shape=jax....]
  transfers between devices with their start and end apart: 2 -> 2, of which waited for: 0 -> 0; matrix products, arithmetic and copies ran while one was open for 22% -> 21% of each run, Pallas kernels for 0% -> 0%
where the time goes in v9:
time: 170 us
  Pallas kernels  90.2 us (53%)
  matrix products  54.6 us (32%)
  local copies, waits for them, and re-layouts  14.9 us (9%)
  starting transfers between devices  6.83 us (4%)
  other arithmetic  2.81 us (2%)
    pallas_call x1, Pallas kernels, summed_everywhere(): pl.pallas_call(functools.partial(allreduce_kernel, scale), out_shape=jax....  90.2 us
    dot_general x3, matrix products, pick_rows(): jnp.einsum('...v,vc->...c', table, source, preferred_element_type=jnp.flo...  13.3 us
    dot_general x1, matrix products, per_device(): jnp.einsum('vkd,kcd->vc', placed, side_kernels, preferred_element_type=jn...  13.1 us
    dot_general x1, matrix products, per_device(): jnp.einsum('kpc,kpd->kcd', gathered_x, gathered_g, preferred_element_type...  10.3 us
    dot_general x2, matrix products, place_rows(): jnp.einsum('fbv,fbc->vc', table, rows, preferred_element_type=jnp.float32)  7.34 us
    dot_general x2, matrix products, face_products(): jnp.einsum('fbc,fbd->fcd', features, grads, preferred_element_type=jnp.fl...  6.93 us
    ppermute x2, starting transfers between devices, passed_along(): return lax.ppermute(array, axis, pairs)  6.83 us
    slice x1, local copies, waits for them, and re-layouts, summed_everywhere(): return total[:stacked.shape[0] * stacked.shape[1]].reshape(stacked.shape)  6.59 us
  transfers between devices with their start and end apart: 2, of which 0 were waited for; matrix products, arithmetic and copies ran while one was open for 21% of the time, Pallas kernels for 0%

profile of v9, /device:TPU:1, one launch (start us, length us, event | category | flops | bytes accessed | tf_op | source)
XLA Modules:
  0.0 170.0 jit_solution(11123195596333392368)
XLA Ops:
  0.6 0.7 copy.10
  1.3 0.0 copy-start.8
  1.3 0.0 copy-start.6
  1.3 0.0 copy-start.7
  1.3 0.0 copy-start.4
  1.3 3.1 %fusion.21 = bf16[2,9,128,256]{3,2,1,0:T(8,128)(2,1)S(1)} fusion(s32[2,9,128]{2,1,0:T(8,128)S(1)} %copy.10, bf16[1,1024,256]{2,1,0:T(8,128)(2,1)} %param.8), kind=kOutput, calls=%fused_computation.30 | convolution fusion | flops 1210908672 | bytes 1713152 | tf_op jit(solution)/shard_map/...v,vc->...c/dot_general | solution.py:272
  4.5 1.1 slice_bitcast_fusion.13
  5.6 4.9 %collective-permute-start = (bf16[9,128,256]{2,1,0:T(8,128)(2,1)}, bf16[9,128,256]{2,1,0:T(8,128)(2,1)}, u32[]{:S(2)}, u32[]{:S(2)}) collective-permute-start(bf16[9,128,256]{2,1,0:T(8,128)(2,1)} %get-tuple-element.4), channel_id=1, source_target_pairs={{0,1},{1,2},{2,3},{3,4},{4,5},{5,6},{6,7},{7,8},{8,9},{9,10},{10,1... | collective-permute-start | bytes 1769480 | tf_op jit(solution)/shard_map/ppermute | solution.py:251
  10.5 1.9 %collective-permute-start.1 = (bf16[9,128,256]{2,1,0:T(8,128)(2,1)}, bf16[9,128,256]{2,1,0:T(8,128)(2,1)}, u32[]{:S(2)}, u32[]{:S(2)}) collective-permute-start(bf16[9,128,256]{2,1,0:T(8,128)(2,1)} %get-tuple-element.5), channel_id=1, source_target_pairs={{1,0},{2,1},{3,2},{4,3},{5,4},{6,5},{7,6},{8,7},{9,8},{10,9},{11,1... | collective-permute-start | bytes 1769480 | tf_op jit(solution)/shard_map/ppermute | solution.py:251
  12.4 0.0 copy-done.8
  12.4 0.0 copy-done.6
  12.5 0.6 copy.23
  13.1 0.0 copy-done.7
  13.1 0.0 copy-done.4
  13.1 0.0 copy-start.1
  13.1 6.5 %fusion.18 = bf16[26,256,256]{2,1,0:T(8,128)(2,1)} fusion(s32[26,256]{1,0:T(8,128)S(1)} %bitcast.106, bf16[1,1024,256]{2,1,0:T(8,128)(2,1)S(1)} %copy-done.4), kind=kOutput, calls=%fused_computation.24 | convolution fusion | flops 3498180608 | bytes 3958784 | tf_op jit(solution)/shard_map/...v,vc->...c/dot_general | solution.py:272
  19.6 0.0 copy-done.1
  19.6 0.0 copy-start.9
  19.6 2.1 %fusion.71 = (bf16[13,256,256]{2,1,0:T(8,128)(2,1)}, bf16[13,256,256]{2,1,0:T(8,128)(2,1)}) fusion(bf16[27,256,256]{2,1,0:T(8,128)(2,1)S(1)} %copy-done.1), kind=kLoop, calls=%fused_computation.65 | loop fusion | bytes 6815744 | tf_op jit(solution)/shard_map/slice | solution.py:303
  21.7 0.0 copy-done.9
  21.7 3.7 %convolution_convert_fusion = bf16[2,9,128,256]{3,2,1,0:T(8,128)(2,1)} fusion(bf16[1,1024,256]{2,1,0:T(8,128)(2,1)S(1)} %copy-done.9, s32[2,9,128]{2,1,0:T(8,128)S(1)} %copy.9), kind=kOutput, calls=%fused_computation.29 | convolution fusion | flops 1210908672 | bytes 1713152 | tf_op jit(solution)/shard_map/...v,vc->...c/dot_general | solution.py:272
  25.4 10.3 %fusion.16 = f32[26,256,256]{2,1,0:T(8,128)} fusion(bf16[26,256,256]{2,1,0:T(8,128)(2,1)} %fusion.18, s32[26,256]{1,0:T(8,128)} %bitcast.104, bf16[1,1024,256]{2,1,0:T(8,128)(2,1)} %param.7), kind=kOutput, calls=%fused_computation.22 | convolution fusion | flops 4370595840 | bytes 10774528 | tf_op jit(solution)/shard_map/kpc,kpd->kcd/dot_general | solution.py:307
  35.7 0.0 copy-start.3
  35.7 2.4 %fusion.66 = f32[1024,256]{1,0:T(8,128)} fusion(bf16[1,1024,256]{2,1,0:T(8,128)(2,1)} %param.8, bf16[27,256,256]{2,1,0:T(8,128)(2,1)S(1)} %copy-done.1), kind=kOutput, calls=%fused_computation.58 | convolution fusion | flops 134217728 | bytes 1703936 | tf_op jit(solution)/shard_map/dot_general | solution.py:261
  38.2 0.0 copy-start
  38.2 2.8 %iota_compare_fusion.10 = pred[2,9,128,1024]{2,3,1,0:T(32,128)(4,1)} fusion(s32[2,9,128]{2,1,0:T(8,128)S(1)} %copy.9), kind=kLoop, calls=%fused_computation.12 | loop fusion | flops 2359296 | bytes 2368512 | tf_op jit(solution)/shard_map/eq | solution.py:268
  41.0 0.0 copy-start.5
  41.0 0.0 copy-start.10
  41.0 0.0 collective-permute-done.1
  41.0 0.0 copy-done.3
  41.0 3.9 %fusion.20 = f32[36,256,256]{2,1,0:T(8,128)} fusion(f32[26,256,256]{2,1,0:T(8,128)} %fusion.16, bf16[9,128,256]{2,1,0:T(8,128)(2,1)} %collective-permute-done.1, bf16[2,9,128,256]{3,2,1,0:T(8,128)(2,1)S(1)} %copy-done.3), kind=kOutput, calls=%fused_computation.28 | convolution fusion | flops 151584768 | bytes 5898240 | tf_op jit(solution)/shard_map/fbc,fbd->fcd/dot_general | solution.py:282
  44.9 0.0 copy-done
  44.9 1.0 slice_dynamic-update-slice_fusion.1
  45.9 0.0 copy-done.5
  45.9 0.0 copy-done.10
  45.9 1.0 fusion.58
  47.0 1.1 slice_dynamic-update-slice_fusion
  48.0 0.0 collective-permute-done
  48.0 3.0 %fusion.19 = f32[36,256,256]{2,1,0:T(8,128)} fusion(f32[36,256,256]{2,1,0:T(8,128)} %slice_dynamic-update-slice_fusion, f32[26,256,256]{2,1,0:T(8,128)S(1)} %copy-done, bf16[9,128,256]{2,1,0:T(8,128)(2,1)} %collective-permute-done, bf16[2,9,128,256]{3,2,1,0:T(8,128)(2,1)S(1)} %copy-done.3), kind=kOutput, calls=%fused_computation.26 | convolution fusion | flops 151584768 | bytes 5898240 | tf_op jit(solution)/shard_map/fbc,fbd->fcd/dot_general | solution.py:282
  51.1 1.7 broadcast_dynamic-update-slice_fusion
  52.8 90.2 %shard_map.86 = f32[9216,256]{1,0:T(8,128)} custom-call(f32[9216,256]{1,0:T(8,128)} %bitcast.23.x_ref), custom_call_target="tpu_custom_call" | custom-call | tf_op jit(solution)/shard_map/pallas_call | solution.py:212
  142.9 0.0 copy-start.2
  143.0 6.6 %slice.63 = f32[6912,256]{1,0:T(8,128)} slice(f32[9216,256]{1,0:T(8,128)} %shard_map.86), slice={[0:6912], [0:256]} | slice | bytes 14155776 | tf_op jit(solution)/shard_map/slice | solution.py:245
  149.5 0.0 copy-done.2
  149.6 3.7 %fusion.23 = f32[1024,256]{1,0:T(8,128)} fusion(pred[2,9,128,1024]{2,3,1,0:T(32,128)(4,1)} %iota_compare_fusion.10, bf16[9,128,256]{2,1,0:T(8,128)(2,1)} %collective-permute-done.1, bf16[27,256,256]{2,1,0:T(8,128)(2,1)S(1)} %copy-done.2), kind=kOutput, calls=%fused_computation.32 | convolution fusion | flops 755269632 | bytes 3997696 | tf_op jit(solution)/shard_map/fbv,fbc->vc/dot_general | solution.py:278
  153.2 3.7 %fusion.22 = f32[1024,256]{1,0:T(8,128)} fusion(pred[2,9,128,1024]{2,3,1,0:T(32,128)(4,1)} %iota_compare_fusion.10, bf16[9,128,256]{2,1,0:T(8,128)(2,1)} %collective-permute-done, bf16[27,256,256]{2,1,0:T(8,128)(2,1)S(1)} %copy-done.2), kind=kOutput, calls=%fused_computation.31 | convolution fusion | flops 755269632 | bytes 3997696 | tf_op jit(solution)/shard_map/fbv,fbc->vc/dot_general | solution.py:278
  156.9 13.1 %fusion.49 = bf16[1,1024,256]{2,1,0:T(8,128)(2,1)} fusion(f32[1024,256]{1,0:T(8,128)} %fusion.23, f32[1024,256]{1,0:T(8,128)} %fusion.22, f32[1024,256]{1,0:T(8,128)} %fusion.66, bf16[13,256,256]{2,1,0:T(8,128)(2,1)} %get-tuple-element.3, bf16[13,256,256]{2,1,0:T(8,128)(2,1)} %get-tuple-element.2, bf16[26,256,256]{2,1,0:T(8,128)(2,1)} %fusion.18, ...), kind=kOutput, calls=%fused_computation.40 | convolution fusion | flops 6995705856 | bytes 10512384 | tf_op jit(solution)/shard_map/vkd,kcd->vc/dot_general | solution.py:304
  (2 shorter events, 0.0 us)
Async XLA Ops:
  1.3 11.1 %copy-start.8 = (s32[1,1,2,9,128]{4,2,3,1,0:T(2,128)S(1)}, s32[1,1,2,9,128]{4,2,3,1,0:T(2,128)}, u32[]{:S(2)}) copy-start(s32[1,1,2,9,128]{4,2,3,1,0:T(2,128)} %param.13) | copy-start | bytes 27652
  1.3 11.1 %copy-start.6 = (s32[1,1,26,256]{3,1,2,0:T(1,128)S(1)}, s32[1,1,26,256]{3,1,2,0:T(1,128)}, u32[]{:S(2)}) copy-start(s32[1,1,26,256]{3,1,2,0:T(1,128)} %param.10) | copy-start | bytes 79876
  1.3 11.7 %copy-start.7 = (s32[1,1,26,256]{3,1,2,0:T(1,128)S(1)}, s32[1,1,26,256]{3,1,2,0:T(1,128)}, u32[]{:S(2)}) copy-start(s32[1,1,26,256]{3,1,2,0:T(1,128)} %param.11) | copy-start | bytes 79876
  1.3 11.7 %copy-start.4 = (bf16[1,1024,256]{2,1,0:T(8,128)(2,1)S(1)}, bf16[1,1024,256]{2,1,0:T(8,128)(2,1)}, u32[]{:S(2)}) copy-start(bf16[1,1024,256]{2,1,0:T(8,128)(2,1)} %param.8) | copy-start | bytes 1572868
  5.6 42.5 %collective-permute-start = (bf16[9,128,256]{2,1,0:T(8,128)(2,1)}, bf16[9,128,256]{2,1,0:T(8,128)(2,1)}, u32[]{:S(2)}, u32[]{:S(2)}) collective-permute-start(bf16[9,128,256]{2,1,0:T(8,128)(2,1)} %get-tuple-element.4), channel_id=1, source_target_pairs={{0,1},{1,2},{2,3},{3,4},{4,5},{5,6},{6,7},{7,8},{8,9},{9,10},{10,1... | collective-permute-start | bytes 1769480 | tf_op jit(solution)/shard_map/ppermute | solution.py:251
  10.5 30.5 %collective-permute-start.1 = (bf16[9,128,256]{2,1,0:T(8,128)(2,1)}, bf16[9,128,256]{2,1,0:T(8,128)(2,1)}, u32[]{:S(2)}, u32[]{:S(2)}) collective-permute-start(bf16[9,128,256]{2,1,0:T(8,128)(2,1)} %get-tuple-element.5), channel_id=1, source_target_pairs={{1,0},{2,1},{3,2},{4,3},{5,4},{6,5},{7,6},{8,7},{9,8},{10,9},{11,1... | collective-permute-start | bytes 1769480 | tf_op jit(solution)/shard_map/ppermute | solution.py:251
  13.1 6.6 %copy-start.1 = (bf16[27,256,256]{2,1,0:T(8,128)(2,1)S(1)}, bf16[27,256,256]{2,1,0:T(8,128)(2,1)}, u32[]{:S(2)}) copy-start(bf16[27,256,256]{2,1,0:T(8,128)(2,1)} %param.9) | copy-start | bytes 10616836
  19.6 2.1 %copy-start.9 = (bf16[1,1024,256]{2,1,0:T(8,128)(2,1)S(1)}, bf16[1,1024,256]{2,1,0:T(8,128)(2,1)}, u32[]{:S(2)}) copy-start(bf16[1,1024,256]{2,1,0:T(8,128)(2,1)} %param.7) | copy-start | bytes 1572868
  35.7 5.3 %copy-start.3 = (bf16[2,9,128,256]{3,2,1,0:T(8,128)(2,1)S(1)}, bf16[2,9,128,256]{3,2,1,0:T(8,128)(2,1)}, u32[]{:S(2)}) copy-start(bf16[2,9,128,256]{3,2,1,0:T(8,128)(2,1)} %convolution_convert_fusion) | copy-start | bytes 3538948
  38.2 6.7 %copy-start = (f32[26,256,256]{2,1,0:T(8,128)S(1)}, f32[26,256,256]{2,1,0:T(8,128)}, u32[]{:S(2)}) copy-start(f32[26,256,256]{2,1,0:T(8,128)} %fusion.16) | copy-start | bytes 20447236
  41.0 5.0 %copy-start.5 = (bf16[1,1024,256]{2,1,0:T(8,128)(2,1)S(1)}, bf16[1,1024,256]{2,1,0:T(8,128)(2,1)}, u32[]{:S(2)}) copy-start(bf16[1,1024,256]{2,1,0:T(8,128)(2,1)} %param.8) | copy-start | bytes 1572868
  41.0 5.0 %copy-start.10 = (bf16[1,1024,256]{2,1,0:T(8,128)(2,1)S(1)}, bf16[1,1024,256]{2,1,0:T(8,128)(2,1)}, u32[]{:S(2)}) copy-start(bf16[1,1024,256]{2,1,0:T(8,128)(2,1)} %param.7) | copy-start | bytes 1572868
  142.9 6.6 %copy-start.2 = (bf16[27,256,256]{2,1,0:T(8,128)(2,1)S(1)}, bf16[27,256,256]{2,1,0:T(8,128)(2,1)}, u32[]{:S(2)}) copy-start(bf16[27,256,256]{2,1,0:T(8,128)(2,1)} %param.9) | copy-start | bytes 10616836

commit v10 on v6

--- a/solution.py
+++ b/solution.py
@@ -190,6 +190,59 @@
     return total[: stacked.shape[0] * stacked.shape[1]].reshape(stacked.shape)
 
 
+def face_kernel(up_ref, down_ref, below_ref, above_ref, got_below, got_above, sems):
+    r = lax.axis_index("region")
+    size = lax.axis_size("region")
+    last = size - 1
+    dp = lax.axis_index("dp")
+    barrier = pltpu.get_barrier_semaphore()
+    for near in (lax.rem(r + size - 1, size), lax.rem(r + 1, size)):
+        pl.semaphore_signal(barrier, inc=1, device_id=(dp, near), device_id_type=MESH_IDS)
+    pl.semaphore_wait(barrier, 2)
+
+    upward = pltpu.make_async_remote_copy(
+        src_ref=up_ref, dst_ref=got_below, send_sem=sems.at[0], recv_sem=sems.at[1],
+        device_id=(dp, jnp.minimum(r + 1, last)), device_id_type=MESH_IDS)
+    downward = pltpu.make_async_remote_copy(
+        src_ref=down_ref, dst_ref=got_above, send_sem=sems.at[2], recv_sem=sems.at[3],
+        device_id=(dp, jnp.maximum(r - 1, 0)), device_id_type=MESH_IDS)
+    pl.when(r < last)(upward.start)
+    pl.when(r > 0)(downward.start)
+    pl.when(r < last)(upward.wait_send)
+    pl.when(r > 0)(downward.wait_send)
+
+    @pl.when(r > 0)
+    def _():
+        upward.wait_recv()
+        below_ref[...] = got_below[...]
+
+    @pl.when(r == 0)
+    def _():
+        below_ref[...] = jnp.zeros_like(below_ref)
+
+    @pl.when(r < last)
+    def _():
+        downward.wait_recv()
+        above_ref[...] = got_above[...]
+
+    @pl.when(r == last)
+    def _():
+        above_ref[...] = jnp.zeros_like(above_ref)
+
+
+def faces_exchanged(up, down):
+    shape = jax.ShapeDtypeStruct(up.shape, up.dtype)
+    return pl.pallas_call(
+        face_kernel,
+        out_shape=(shape, shape),
+        in_specs=[pl.BlockSpec(memory_space=pltpu.VMEM)] * 2,
+        out_specs=(pl.BlockSpec(memory_space=pltpu.VMEM),) * 2,
+        scratch_shapes=[pltpu.VMEM(up.shape, up.dtype), pltpu.VMEM(up.shape, up.dtype),
+                        pltpu.SemaphoreType.DMA((4,))],
+        compiler_params=pltpu.CompilerParams(collective_id=1, has_side_effects=True),
+    )(up, down)
+
+
 def passed_along(array, axis, by):
     peers = lax.axis_size(axis)
     pairs = [(i, i + by) for i in range(peers) if 0 <= i + by < peers]
@@ -258,8 +311,7 @@
     face_in_table = one_hot_rows(bnd_in[0, 0], rows_here)
     own_grads = pick_rows(face_out_table, own_grad)
     asked = pick_rows(face_in_table, own_feat)
-    from_below = passed_along(own_grads[1], "region", 1)
-    from_above = passed_along(own_grads[0], "region", -1)
+    from_below, from_above = faces_exchanged(own_grads[1], own_grads[0])
     high_grad, below_rows = face_products(asked[0], from_below, high_kernels)
     low_grad, above_rows = face_products(asked[1], from_above, low_kernels)
     accumulated = accumulated + place_rows(face_in_table[0], below_rows)

time: 166 us -> 177 us (1.066)
  Pallas kernels: 85.3 us -> 98.4 us
  starting transfers between devices: 6.83 us -> 0 us
  local copies, waits for them, and re-layouts: 14.9 us -> 18.8 us
    pallas_call x0 -> x1, Pallas kernels: none -> 12.9 us  [faces_exchanged(): pl.pallas_call(face_kernel, out_shape=(shape, shape), in_specs=[pl.BlockS...]
    ppermute x2 -> x0, starting transfers between devices: 6.83 us -> none  [passed_along(): return lax.ppermute(array, axis, pairs)]
    unnamed x26 -> x20, local copies, waits for them, and re-layouts: 2.76 us -> 6.17 us
    dot_general x3, matrix products: 13.3 us -> 15.6 us  [pick_rows(): jnp.einsum('...v,vc->...c', table, source, preferred_element_type=jnp.flo...]
  transfers between devices with their start and end apart: 2 -> 0, of which waited for: 0 -> 0; matrix products, arithmetic and copies ran while one was open for 22% -> 0% of each run, Pallas kernels for 0% -> 0%
where the time goes in v10:
time: 177 us; the launch traced here: 176 us
  Pallas kernels  98.4 us (56%)
  matrix products  55.7 us (31%)
  local copies, waits for them, and re-layouts  18.8 us (11%)
  other arithmetic  2.82 us (2%)
    pallas_call x1, Pallas kernels, summed_everywhere(): pl.pallas_call(functools.partial(allreduce_kernel, scale), out_shape=jax....  85.4 us
    dot_general x3, matrix products, pick_rows(): jnp.einsum('...v,vc->...c', table, source, preferred_element_type=jnp.flo...  15.6 us
    dot_general x1, matrix products, per_device(): jnp.einsum('vkd,kcd->vc', placed, side_kernels, preferred_element_type=jn...  13.2 us
    pallas_call x1, Pallas kernels, faces_exchanged(): pl.pallas_call(face_kernel, out_shape=(shape, shape), in_specs=[pl.BlockS...  12.9 us
    dot_general x1, matrix products, per_device(): jnp.einsum('kpc,kpd->kcd', gathered_x, gathered_g, preferred_element_type...  10.3 us
    dot_general x2, matrix products, place_rows(): jnp.einsum('fbv,fbc->vc', table, rows, preferred_element_type=jnp.float32)  7.46 us
    slice x1, local copies, waits for them, and re-layouts, summed_everywhere(): return total[:stacked.shape[0] * stacked.shape[1]].reshape(stacked.shape)  6.43 us
    unnamed x20, local copies, waits for them, and re-layouts  6.17 us

profile of v10, /device:TPU:1, one launch (start us, length us, event | category | flops | bytes accessed | tf_op | source)
XLA Modules:
  0.0 176.3 jit_solution(6597333985789503040)
XLA Ops:
  0.6 0.7 copy.9
  1.3 0.7 copy.10
  2.0 1.4 copy.23
  3.4 1.4 copy.24
  4.7 2.4 %fusion.66 = f32[1024,256]{1,0:T(8,128)} fusion(bf16[1,1024,256]{2,1,0:T(8,128)(2,1)} %param.8, bf16[27,256,256]{2,1,0:T(8,128)(2,1)} %param.9), kind=kOutput, calls=%fused_computation.58 | convolution fusion | flops 134217728 | bytes 1703936 | tf_op jit(solution)/shard_map/dot_general | solution.py:259
  7.1 3.0 %fusion.21 = bf16[2,9,128,256]{3,2,1,0:T(8,128)(2,1)S(1)} fusion(s32[2,9,128]{2,1,0:T(8,128)S(1)} %copy.10, bf16[1,1024,256]{2,1,0:T(8,128)(2,1)} %param.8), kind=kOutput, calls=%fused_computation.30 | convolution fusion | flops 1210908672 | bytes 1713152 | tf_op jit(solution)/shard_map/...v,vc->...c/dot_general | solution.py:270
  10.2 1.1 slice_bitcast_fusion.12
  11.3 12.9 %shard_map.86 = (bf16[9,128,256]{2,1,0:T(8,128)(2,1)}, bf16[9,128,256]{2,1,0:T(8,128)(2,1)}) custom-call(bf16[9,128,256]{2,1,0:T(8,128)(2,1)} %get-tuple-element.9.up_ref, bf16[9,128,256]{2,1,0:T(8,128)(2,1)} %get-tuple-element.8.down_ref), custom_call_target="tpu_custom_call" | custom-call | tf_op jit(solution)/shard_map/pallas_call | solution.py:235
  24.2 0.0 copy-start.1
  24.2 4.9 %convolution_convert_fusion = bf16[2,9,128,256]{3,2,1,0:T(8,128)(2,1)} fusion(bf16[1,1024,256]{2,1,0:T(8,128)(2,1)} %param.7, s32[2,9,128]{2,1,0:T(8,128)S(1)} %copy.9), kind=kOutput, calls=%fused_computation.29 | convolution fusion | flops 1210908672 | bytes 1713152 | tf_op jit(solution)/shard_map/...v,vc->...c/dot_general | solution.py:270
  29.1 2.8 %iota_compare_fusion.10 = pred[2,9,128,1024]{2,3,1,0:T(32,128)(4,1)} fusion(s32[2,9,128]{2,1,0:T(8,128)S(1)} %copy.9), kind=kLoop, calls=%fused_computation.12 | loop fusion | flops 2359296 | bytes 2368512 | tf_op jit(solution)/shard_map/eq | solution.py:266
  31.9 0.0 copy-done.1
  31.9 3.7 %fusion.23 = f32[1024,256]{1,0:T(8,128)} fusion(pred[2,9,128,1024]{2,3,1,0:T(32,128)(4,1)} %iota_compare_fusion.10, bf16[9,128,256]{2,1,0:T(8,128)(2,1)} %get-tuple-element.5, bf16[27,256,256]{2,1,0:T(8,128)(2,1)S(1)} %copy-done.1), kind=kOutput, calls=%fused_computation.32 | convolution fusion | flops 755269632 | bytes 3997696 | tf_op jit(solution)/shard_map/fbv,fbc->vc/dot_general | solution.py:276
  35.6 3.8 %fusion.22 = f32[1024,256]{1,0:T(8,128)} fusion(pred[2,9,128,1024]{2,3,1,0:T(32,128)(4,1)} %iota_compare_fusion.10, bf16[9,128,256]{2,1,0:T(8,128)(2,1)} %get-tuple-element.4, bf16[27,256,256]{2,1,0:T(8,128)(2,1)S(1)} %copy-done.1), kind=kOutput, calls=%fused_computation.31 | convolution fusion | flops 755269632 | bytes 3997696 | tf_op jit(solution)/shard_map/fbv,fbc->vc/dot_general | solution.py:276
  39.4 7.6 %fusion.18 = bf16[26,256,256]{2,1,0:T(8,128)(2,1)} fusion(s32[26,256]{1,0:T(8,128)} %bitcast.106, bf16[1,1024,256]{2,1,0:T(8,128)(2,1)} %param.8), kind=kOutput, calls=%fused_computation.24 | convolution fusion | flops 3498180608 | bytes 3958784 | tf_op jit(solution)/shard_map/...v,vc->...c/dot_general | solution.py:270
  47.0 2.0 %fusion.71 = (bf16[13,256,256]{2,1,0:T(8,128)(2,1)}, bf16[13,256,256]{2,1,0:T(8,128)(2,1)}) fusion(bf16[27,256,256]{2,1,0:T(8,128)(2,1)S(1)} %copy-done.1), kind=kLoop, calls=%fused_computation.65 | loop fusion | bytes 6815744 | tf_op jit(solution)/shard_map/slice | solution.py:301
  49.0 0.0 copy-start.6
  49.0 0.0 copy-start.7
  49.0 13.2 %fusion.49 = bf16[1,1024,256]{2,1,0:T(8,128)(2,1)} fusion(f32[1024,256]{1,0:T(8,128)} %fusion.23, f32[1024,256]{1,0:T(8,128)} %fusion.22, f32[1024,256]{1,0:T(8,128)} %fusion.66, bf16[13,256,256]{2,1,0:T(8,128)(2,1)} %get-tuple-element.7, bf16[13,256,256]{2,1,0:T(8,128)(2,1)} %get-tuple-element.6, bf16[26,256,256]{2,1,0:T(8,128)(2,1)} %fusion.18, ...), kind=kOutput, calls=%fused_computation.40 | convolution fusion | flops 6995705856 | bytes 10512384 | tf_op jit(solution)/shard_map/vkd,kcd->vc/dot_general | solution.py:302
  62.2 0.0 copy-done.6
  62.2 0.0 copy-done.7
  62.3 0.0 copy-start.2
  62.3 0.0 copy-start.4
  62.3 10.3 %fusion.16 = f32[26,256,256]{2,1,0:T(8,128)} fusion(bf16[26,256,256]{2,1,0:T(8,128)(2,1)} %fusion.18, s32[26,256]{1,0:T(8,128)S(1)} %bitcast.105, bf16[1,1024,256]{2,1,0:T(8,128)(2,1)S(1)} %copy-done.7), kind=kOutput, calls=%fused_computation.22 | convolution fusion | flops 4370595840 | bytes 10774528 | tf_op jit(solution)/shard_map/kpc,kpd->kcd/dot_general | solution.py:305
  72.6 0.0 copy-done.2
  72.6 0.0 copy-done.4
  72.6 0.0 copy-start.5
  72.6 0.0 copy-start
  72.6 3.7 %fusion.20 = f32[36,256,256]{2,1,0:T(8,128)} fusion(f32[26,256,256]{2,1,0:T(8,128)} %fusion.16, bf16[9,128,256]{2,1,0:T(8,128)(2,1)S(1)} %copy-done.4, bf16[2,9,128,256]{3,2,1,0:T(8,128)(2,1)S(1)} %copy-done.2), kind=kOutput, calls=%fused_computation.28 | convolution fusion | flops 151584768 | bytes 5898240 | tf_op jit(solution)/shard_map/fbc,fbd->fcd/dot_general | solution.py:280
  76.4 0.0 copy-start.3
  76.4 2.4 %slice_dynamic-update-slice_fusion.1 = f32[36,256,256]{2,1,0:T(8,128)} fusion(f32[36,256,256]{2,1,0:T(8,128)} %fusion.20, f32[26,256,256]{2,1,0:T(8,128)} %fusion.16), kind=kLoop, calls=%fused_computation.47 | loop fusion | bytes 2097152
  78.7 0.0 copy-done.5
  78.7 1.0 fusion.58
  79.8 0.0 copy-done
  79.8 1.1 slice_dynamic-update-slice_fusion
  80.8 0.0 copy-done.3
  80.8 2.0 %fusion.19 = f32[36,256,256]{2,1,0:T(8,128)} fusion(f32[36,256,256]{2,1,0:T(8,128)} %slice_dynamic-update-slice_fusion, f32[26,256,256]{2,1,0:T(8,128)S(1)} %copy-done, bf16[9,128,256]{2,1,0:T(8,128)(2,1)S(1)} %copy-done.3, bf16[2,9,128,256]{3,2,1,0:T(8,128)(2,1)S(1)} %copy-done.2), kind=kOutput, calls=%fused_computation.26 | convolution fusion | flops 151584768 | bytes 5898240 | tf_op jit(solution)/shard_map/fbc,fbd->fcd/dot_general | solution.py:280
  82.8 1.7 broadcast_dynamic-update-slice_fusion
  84.5 85.4 %shard_map.87 = f32[9216,256]{1,0:T(8,128)} custom-call(f32[9216,256]{1,0:T(8,128)} %bitcast.23.x_ref), custom_call_target="tpu_custom_call" | custom-call | tf_op jit(solution)/shard_map/pallas_call | solution.py:162
  169.9 6.4 %slice.63 = f32[6912,256]{1,0:T(8,128)} slice(f32[9216,256]{1,0:T(8,128)} %shard_map.87), slice={[0:6912], [0:256]} | slice | bytes 14155776 | tf_op jit(solution)/shard_map/slice | solution.py:190
Async XLA Ops:
  24.2 7.7 %copy-start.1 = (bf16[27,256,256]{2,1,0:T(8,128)(2,1)S(1)}, bf16[27,256,256]{2,1,0:T(8,128)(2,1)}, u32[]{:S(2)}) copy-start(bf16[27,256,256]{2,1,0:T(8,128)(2,1)} %param.9) | copy-start | bytes 10616836
  49.0 13.2 %copy-start.6 = (s32[1,1,26,256]{3,2,1,0:T(8,128)S(1)}, s32[1,1,26,256]{3,2,1,0:T(8,128)}, u32[]{:S(2)}) copy-start(s32[1,1,26,256]{3,2,1,0:T(8,128)} %copy.23) | copy-start | bytes 79876
  49.0 13.2 %copy-start.7 = (bf16[1,1024,256]{2,1,0:T(8,128)(2,1)S(1)}, bf16[1,1024,256]{2,1,0:T(8,128)(2,1)}, u32[]{:S(2)}) copy-start(bf16[1,1024,256]{2,1,0:T(8,128)(2,1)} %param.7) | copy-start | bytes 1572868
  62.3 10.3 %copy-start.2 = (bf16[2,9,128,256]{3,2,1,0:T(8,128)(2,1)S(1)}, bf16[2,9,128,256]{3,2,1,0:T(8,128)(2,1)}, u32[]{:S(2)}) copy-start(bf16[2,9,128,256]{3,2,1,0:T(8,128)(2,1)} %convolution_convert_fusion) | copy-start | bytes 3538948
  62.3 10.3 %copy-start.4 = (bf16[9,128,256]{2,1,0:T(8,128)(2,1)S(1)}, bf16[9,128,256]{2,1,0:T(8,128)(2,1)}, u32[]{:S(2)}) copy-start(bf16[9,128,256]{2,1,0:T(8,128)(2,1)} %get-tuple-element.5) | copy-start | bytes 1769476
  72.6 6.1 %copy-start.5 = (bf16[1,1024,256]{2,1,0:T(8,128)(2,1)S(1)}, bf16[1,1024,256]{2,1,0:T(8,128)(2,1)}, u32[]{:S(2)}) copy-start(bf16[1,1024,256]{2,1,0:T(8,128)(2,1)} %param.8) | copy-start | bytes 1572868
  72.6 7.2 %copy-start = (f32[26,256,256]{2,1,0:T(8,128)S(1)}, f32[26,256,256]{2,1,0:T(8,128)}, u32[]{:S(2)}) copy-start(f32[26,256,256]{2,1,0:T(8,128)} %fusion.16) | copy-start | bytes 20447236
  76.4 4.5 %copy-start.3 = (bf16[9,128,256]{2,1,0:T(8,128)(2,1)S(1)}, bf16[9,128,256]{2,1,0:T(8,128)(2,1)}, u32[]{:S(2)}) copy-start(bf16[9,128,256]{2,1,0:T(8,128)(2,1)} %get-tuple-element.4) | copy-start | bytes 1769476

commit v11 on v6

--- a/solution.py
+++ b/solution.py
@@ -116,7 +116,7 @@
         base = k * COLOR_ROWS + c * half
         add_rows(lambda a, v, k=k: part.__setitem__((k, a), v),
                  lambda a, base=base: x_ref[pl.ds(pl.multiple_of(base, 8) + a.start, a.size)],
-                 [lambda a, k=k: rcore[k, a]], half, 128)
+                 [lambda a, k=k: rcore[k, a]], half, 256)
         staged[k] = scatter_sends(0, k)
     for stage in range(3):
         blk, src, rbuf = blocks[stage], sources[stage], recvs[stage]
@@ -128,7 +128,7 @@
             others = [lambda a, k=k, j=j, rbuf=rbuf: rbuf[k, j, a] for j in range(3)]
             first = lambda a, k=k, own=own, src=src: src[k, pl.ds(own + a.start, a.size)]
             if stage == 0:
-                add_rows(lambda a, v, k=k: p1.__setitem__((k, a), v), first, others, blk, 128)
+                add_rows(lambda a, v, k=k: p1.__setitem__((k, a), v), first, others, blk, 192)
                 staged[k] = scatter_sends(1, k)
             elif stage == 1:
                 add_rows(lambda a, v, k=k: p2.__setitem__((k, a), v), first, others, blk, blk)

time: 166 us -> 165 us (level)
  no operation moved by 1% of the time
where the time goes in v11:
time: 165 us
  Pallas kernels  85.2 us (52%)
  matrix products  54.6 us (33%)
  local copies, waits for them, and re-layouts  14.9 us (9%)
  starting transfers between devices  6.83 us (4%)
  other arithmetic  2.81 us (2%)
    pallas_call x1, Pallas kernels, summed_everywhere(): pl.pallas_call(functools.partial(allreduce_kernel, scale), out_shape=jax....  85.2 us
    dot_general x3, matrix products, pick_rows(): jnp.einsum('...v,vc->...c', table, source, preferred_element_type=jnp.flo...  13.3 us
    dot_general x1, matrix products, per_device(): jnp.einsum('vkd,kcd->vc', placed, side_kernels, preferred_element_type=jn...  13.1 us
    dot_general x1, matrix products, per_device(): jnp.einsum('kpc,kpd->kcd', gathered_x, gathered_g, preferred_element_type...  10.3 us
    dot_general x2, matrix products, place_rows(): jnp.einsum('fbv,fbc->vc', table, rows, preferred_element_type=jnp.float32)  7.34 us
    dot_general x2, matrix products, face_products(): jnp.einsum('fbc,fbd->fcd', features, grads, preferred_element_type=jnp.fl...  6.93 us
    ppermute x2, starting transfers between devices, passed_along(): return lax.ppermute(array, axis, pairs)  6.83 us
    slice x1, local copies, waits for them, and re-layouts, summed_everywhere(): return total[:stacked.shape[0] * stacked.shape[1]].reshape(stacked.shape)  6.59 us
  transfers between devices with their start and end apart: 2, of which 0 were waited for; matrix products, arithmetic and copies ran while one was open for 22% of the time, Pallas kernels for 0%

profile of v11, /device:TPU:1, one launch (start us, length us, event | category | flops | bytes accessed | tf_op | source)
XLA Modules:
  0.0 165.1 jit_solution(8205389626315432900)
XLA Ops:
  0.6 0.7 copy.10
  1.3 0.0 copy-start.8
  1.3 0.0 copy-start.6
  1.3 0.0 copy-start.7
  1.3 0.0 copy-start.4
  1.3 3.1 %fusion.21 = bf16[2,9,128,256]{3,2,1,0:T(8,128)(2,1)S(1)} fusion(s32[2,9,128]{2,1,0:T(8,128)S(1)} %copy.10, bf16[1,1024,256]{2,1,0:T(8,128)(2,1)} %param.8), kind=kOutput, calls=%fused_computation.30 | convolution fusion | flops 1210908672 | bytes 1713152 | tf_op jit(solution)/shard_map/...v,vc->...c/dot_general | solution.py:217
  4.5 1.1 slice_bitcast_fusion.13
  5.6 4.9 %collective-permute-start = (bf16[9,128,256]{2,1,0:T(8,128)(2,1)}, bf16[9,128,256]{2,1,0:T(8,128)(2,1)}, u32[]{:S(2)}, u32[]{:S(2)}) collective-permute-start(bf16[9,128,256]{2,1,0:T(8,128)(2,1)} %get-tuple-element.4), channel_id=1, source_target_pairs={{0,1},{1,2},{2,3},{3,4},{4,5},{5,6},{6,7},{7,8},{8,9},{9,10},{10,1... | collective-permute-start | bytes 1769480 | tf_op jit(solution)/shard_map/ppermute | solution.py:196
  10.5 1.9 %collective-permute-start.1 = (bf16[9,128,256]{2,1,0:T(8,128)(2,1)}, bf16[9,128,256]{2,1,0:T(8,128)(2,1)}, u32[]{:S(2)}, u32[]{:S(2)}) collective-permute-start(bf16[9,128,256]{2,1,0:T(8,128)(2,1)} %get-tuple-element.5), channel_id=1, source_target_pairs={{1,0},{2,1},{3,2},{4,3},{5,4},{6,5},{7,6},{8,7},{9,8},{10,9},{11,1... | collective-permute-start | bytes 1769480 | tf_op jit(solution)/shard_map/ppermute | solution.py:196
  12.4 0.0 copy-done.8
  12.4 0.0 copy-done.6
  12.5 0.6 copy.23
  13.1 0.0 copy-done.7
  13.1 0.0 copy-done.4
  13.1 0.0 copy-start.1
  13.1 6.5 %fusion.18 = bf16[26,256,256]{2,1,0:T(8,128)(2,1)} fusion(s32[26,256]{1,0:T(8,128)S(1)} %bitcast.106, bf16[1,1024,256]{2,1,0:T(8,128)(2,1)S(1)} %copy-done.4), kind=kOutput, calls=%fused_computation.24 | convolution fusion | flops 3498180608 | bytes 3958784 | tf_op jit(solution)/shard_map/...v,vc->...c/dot_general | solution.py:217
  19.6 0.0 copy-done.1
  19.6 0.0 copy-start.9
  19.6 2.1 %fusion.71 = (bf16[13,256,256]{2,1,0:T(8,128)(2,1)}, bf16[13,256,256]{2,1,0:T(8,128)(2,1)}) fusion(bf16[27,256,256]{2,1,0:T(8,128)(2,1)S(1)} %copy-done.1), kind=kLoop, calls=%fused_computation.65 | loop fusion | bytes 6815744 | tf_op jit(solution)/shard_map/slice | solution.py:248
  21.7 0.0 copy-done.9
  21.7 3.7 %convolution_convert_fusion = bf16[2,9,128,256]{3,2,1,0:T(8,128)(2,1)} fusion(bf16[1,1024,256]{2,1,0:T(8,128)(2,1)S(1)} %copy-done.9, s32[2,9,128]{2,1,0:T(8,128)S(1)} %copy.9), kind=kOutput, calls=%fused_computation.29 | convolution fusion | flops 1210908672 | bytes 1713152 | tf_op jit(solution)/shard_map/...v,vc->...c/dot_general | solution.py:217
  25.4 10.3 %fusion.16 = f32[26,256,256]{2,1,0:T(8,128)} fusion(bf16[26,256,256]{2,1,0:T(8,128)(2,1)} %fusion.18, s32[26,256]{1,0:T(8,128)} %bitcast.104, bf16[1,1024,256]{2,1,0:T(8,128)(2,1)} %param.7), kind=kOutput, calls=%fused_computation.22 | convolution fusion | flops 4370595840 | bytes 10774528 | tf_op jit(solution)/shard_map/kpc,kpd->kcd/dot_general | solution.py:252
  35.7 0.0 copy-start.3
  35.7 2.4 %fusion.66 = f32[1024,256]{1,0:T(8,128)} fusion(bf16[1,1024,256]{2,1,0:T(8,128)(2,1)} %param.8, bf16[27,256,256]{2,1,0:T(8,128)(2,1)S(1)} %copy-done.1), kind=kOutput, calls=%fused_computation.58 | convolution fusion | flops 134217728 | bytes 1703936 | tf_op jit(solution)/shard_map/dot_general | solution.py:206
  38.2 0.0 copy-start
  38.2 2.8 %iota_compare_fusion.10 = pred[2,9,128,1024]{2,3,1,0:T(32,128)(4,1)} fusion(s32[2,9,128]{2,1,0:T(8,128)S(1)} %copy.9), kind=kLoop, calls=%fused_computation.12 | loop fusion | flops 2359296 | bytes 2368512 | tf_op jit(solution)/shard_map/eq | solution.py:213
  41.0 0.0 copy-start.5
  41.0 0.0 copy-start.10
  41.0 0.0 collective-permute-done.1
  41.0 0.0 copy-done.3
  41.0 3.9 %fusion.20 = f32[36,256,256]{2,1,0:T(8,128)} fusion(f32[26,256,256]{2,1,0:T(8,128)} %fusion.16, bf16[9,128,256]{2,1,0:T(8,128)(2,1)} %collective-permute-done.1, bf16[2,9,128,256]{3,2,1,0:T(8,128)(2,1)S(1)} %copy-done.3), kind=kOutput, calls=%fused_computation.28 | convolution fusion | flops 151584768 | bytes 5898240 | tf_op jit(solution)/shard_map/fbc,fbd->fcd/dot_general | solution.py:227
  44.9 0.0 copy-done
  44.9 1.0 slice_dynamic-update-slice_fusion.1
  45.9 0.0 copy-done.5
  45.9 0.0 copy-done.10
  45.9 1.0 fusion.58
  47.0 1.1 slice_dynamic-update-slice_fusion
  48.0 0.0 collective-permute-done
  48.0 3.0 %fusion.19 = f32[36,256,256]{2,1,0:T(8,128)} fusion(f32[36,256,256]{2,1,0:T(8,128)} %slice_dynamic-update-slice_fusion, f32[26,256,256]{2,1,0:T(8,128)S(1)} %copy-done, bf16[9,128,256]{2,1,0:T(8,128)(2,1)} %collective-permute-done, bf16[2,9,128,256]{3,2,1,0:T(8,128)(2,1)S(1)} %copy-done.3), kind=kOutput, calls=%fused_computation.26 | convolution fusion | flops 151584768 | bytes 5898240 | tf_op jit(solution)/shard_map/fbc,fbd->fcd/dot_general | solution.py:227
  51.1 1.7 %broadcast_dynamic-update-slice_fusion = f32[36,256,256]{2,1,0:T(8,128)} fusion(f32[36,256,256]{2,1,0:T(8,128)} %fusion.19), kind=kLoop, calls=%fused_computation.41 | loop fusion | bytes 2359296 | tf_op jit(solution)/shard_map/concatenate | solution.py:157
  52.8 85.2 %shard_map.86 = f32[9216,256]{1,0:T(8,128)} custom-call(f32[9216,256]{1,0:T(8,128)} %bitcast.23.x_ref), custom_call_target="tpu_custom_call" | custom-call | tf_op jit(solution)/shard_map/pallas_call | solution.py:162
  138.0 0.0 copy-start.2
  138.0 6.6 %slice.63 = f32[6912,256]{1,0:T(8,128)} slice(f32[9216,256]{1,0:T(8,128)} %shard_map.86), slice={[0:6912], [0:256]} | slice | bytes 14155776 | tf_op jit(solution)/shard_map/slice | solution.py:190
  144.6 0.0 copy-done.2
  144.6 3.7 %fusion.23 = f32[1024,256]{1,0:T(8,128)} fusion(pred[2,9,128,1024]{2,3,1,0:T(32,128)(4,1)} %iota_compare_fusion.10, bf16[9,128,256]{2,1,0:T(8,128)(2,1)} %collective-permute-done.1, bf16[27,256,256]{2,1,0:T(8,128)(2,1)S(1)} %copy-done.2), kind=kOutput, calls=%fused_computation.32 | convolution fusion | flops 755269632 | bytes 3997696 | tf_op jit(solution)/shard_map/fbv,fbc->vc/dot_general | solution.py:223
  148.3 3.7 %fusion.22 = f32[1024,256]{1,0:T(8,128)} fusion(pred[2,9,128,1024]{2,3,1,0:T(32,128)(4,1)} %iota_compare_fusion.10, bf16[9,128,256]{2,1,0:T(8,128)(2,1)} %collective-permute-done, bf16[27,256,256]{2,1,0:T(8,128)(2,1)S(1)} %copy-done.2), kind=kOutput, calls=%fused_computation.31 | convolution fusion | flops 755269632 | bytes 3997696 | tf_op jit(solution)/shard_map/fbv,fbc->vc/dot_general | solution.py:223
  152.0 13.1 %fusion.49 = bf16[1,1024,256]{2,1,0:T(8,128)(2,1)} fusion(f32[1024,256]{1,0:T(8,128)} %fusion.23, f32[1024,256]{1,0:T(8,128)} %fusion.22, f32[1024,256]{1,0:T(8,128)} %fusion.66, bf16[13,256,256]{2,1,0:T(8,128)(2,1)} %get-tuple-element.3, bf16[13,256,256]{2,1,0:T(8,128)(2,1)} %get-tuple-element.2, bf16[26,256,256]{2,1,0:T(8,128)(2,1)} %fusion.18, ...), kind=kOutput, calls=%fused_computation.40 | convolution fusion | flops 6995705856 | bytes 10512384 | tf_op jit(solution)/shard_map/vkd,kcd->vc/dot_general | solution.py:249
  (2 shorter events, 0.0 us)
Async XLA Ops:
  1.3 11.1 %copy-start.8 = (s32[1,1,2,9,128]{4,2,3,1,0:T(2,128)S(1)}, s32[1,1,2,9,128]{4,2,3,1,0:T(2,128)}, u32[]{:S(2)}) copy-start(s32[1,1,2,9,128]{4,2,3,1,0:T(2,128)} %param.13) | copy-start | bytes 27652
  1.3 11.1 %copy-start.6 = (s32[1,1,26,256]{3,1,2,0:T(1,128)S(1)}, s32[1,1,26,256]{3,1,2,0:T(1,128)}, u32[]{:S(2)}) copy-start(s32[1,1,26,256]{3,1,2,0:T(1,128)} %param.10) | copy-start | bytes 79876
  1.3 11.7 %copy-start.7 = (s32[1,1,26,256]{3,1,2,0:T(1,128)S(1)}, s32[1,1,26,256]{3,1,2,0:T(1,128)}, u32[]{:S(2)}) copy-start(s32[1,1,26,256]{3,1,2,0:T(1,128)} %param.11) | copy-start | bytes 79876
  1.3 11.7 %copy-start.4 = (bf16[1,1024,256]{2,1,0:T(8,128)(2,1)S(1)}, bf16[1,1024,256]{2,1,0:T(8,128)(2,1)}, u32[]{:S(2)}) copy-start(bf16[1,1024,256]{2,1,0:T(8,128)(2,1)} %param.8) | copy-start | bytes 1572868
  5.6 42.5 %collective-permute-start = (bf16[9,128,256]{2,1,0:T(8,128)(2,1)}, bf16[9,128,256]{2,1,0:T(8,128)(2,1)}, u32[]{:S(2)}, u32[]{:S(2)}) collective-permute-start(bf16[9,128,256]{2,1,0:T(8,128)(2,1)} %get-tuple-element.4), channel_id=1, source_target_pairs={{0,1},{1,2},{2,3},{3,4},{4,5},{5,6},{6,7},{7,8},{8,9},{9,10},{10,1... | collective-permute-start | bytes 1769480 | tf_op jit(solution)/shard_map/ppermute | solution.py:196
  10.5 30.5 %collective-permute-start.1 = (bf16[9,128,256]{2,1,0:T(8,128)(2,1)}, bf16[9,128,256]{2,1,0:T(8,128)(2,1)}, u32[]{:S(2)}, u32[]{:S(2)}) collective-permute-start(bf16[9,128,256]{2,1,0:T(8,128)(2,1)} %get-tuple-element.5), channel_id=1, source_target_pairs={{1,0},{2,1},{3,2},{4,3},{5,4},{6,5},{7,6},{8,7},{9,8},{10,9},{11,1... | collective-permute-start | bytes 1769480 | tf_op jit(solution)/shard_map/ppermute | solution.py:196
  13.1 6.6 %copy-start.1 = (bf16[27,256,256]{2,1,0:T(8,128)(2,1)S(1)}, bf16[27,256,256]{2,1,0:T(8,128)(2,1)}, u32[]{:S(2)}) copy-start(bf16[27,256,256]{2,1,0:T(8,128)(2,1)} %param.9) | copy-start | bytes 10616836
  19.6 2.1 %copy-start.9 = (bf16[1,1024,256]{2,1,0:T(8,128)(2,1)S(1)}, bf16[1,1024,256]{2,1,0:T(8,128)(2,1)}, u32[]{:S(2)}) copy-start(bf16[1,1024,256]{2,1,0:T(8,128)(2,1)} %param.7) | copy-start | bytes 1572868
  35.7 5.3 %copy-start.3 = (bf16[2,9,128,256]{3,2,1,0:T(8,128)(2,1)S(1)}, bf16[2,9,128,256]{3,2,1,0:T(8,128)(2,1)}, u32[]{:S(2)}) copy-start(bf16[2,9,128,256]{3,2,1,0:T(8,128)(2,1)} %convolution_convert_fusion) | copy-start | bytes 3538948
  38.2 6.7 %copy-start = (f32[26,256,256]{2,1,0:T(8,128)S(1)}, f32[26,256,256]{2,1,0:T(8,128)}, u32[]{:S(2)}) copy-start(f32[26,256,256]{2,1,0:T(8,128)} %fusion.16) | copy-start | bytes 20447236
  41.0 5.0 %copy-start.5 = (bf16[1,1024,256]{2,1,0:T(8,128)(2,1)S(1)}, bf16[1,1024,256]{2,1,0:T(8,128)(2,1)}, u32[]{:S(2)}) copy-start(bf16[1,1024,256]{2,1,0:T(8,128)(2,1)} %param.8) | copy-start | bytes 1572868
  41.0 5.0 %copy-start.10 = (bf16[1,1024,256]{2,1,0:T(8,128)(2,1)S(1)}, bf16[1,1024,256]{2,1,0:T(8,128)(2,1)}, u32[]{:S(2)}) copy-start(bf16[1,1024,256]{2,1,0:T(8,128)(2,1)} %param.7) | copy-start | bytes 1572868
  138.0 6.6 %copy-start.2 = (bf16[27,256,256]{2,1,0:T(8,128)(2,1)S(1)}, bf16[27,256,256]{2,1,0:T(8,128)(2,1)}, u32[]{:S(2)}) copy-start(bf16[27,256,256]{2,1,0:T(8,128)(2,1)} %param.9) | copy-start | bytes 10616836
